TPU v7x, 32 devices: a whole 2x2x4 slice. The times are simulated.
32 devices in a mesh: row: 4 (over z), col: 8 (over y, x, core).
Axes of the slice: x: 2, y: 2, z: 4, core: 2. Of those that a mesh axis runs over, the one named last changes fastest.
Arguments:
- density_tiles: bfloat16 [1024, 128, 128], P(('row', 'col')), may hold values from -1 to 1
- send_list: int32 [32, 32, 3], P(('row', 'col')), may hold values from 0 to 31
- basis_values: bfloat16 [64, 2048, 768], P(('row', 'col')), may hold values from -0.625 to 0.625
- active_blocks: int32 [64], P(('row', 'col')), may hold values from 1 to 6, as said below
- touch_slots: int32 [64, 6, 6], P(('row', 'col')), may hold values from -1 to 95, as said below
- point_weights: float32 [64, 2048], P(('row', 'col')), may hold values from 0.2 to 2
- harmonics: float32 [64, 49, 2048], P(('row', 'col')), may hold values from -1.2 to 1.2
- shell_index: int32 [64, 2048], P(('row', 'col')), may hold values from 0 to 127
- batch_atom: int32 [64], P(('row', 'col')), may hold values from 0 to 15
- radial_green: float32 [7, 128, 128], replicated, may hold values from -0.25 to 0.25
Outputs:
- ham_tiles: float32 [1024, 128, 128], P(('row', 'col'))
- multipoles: float32 [16, 49, 128], P('col')
Inputs may be any that keep to these rules, and one draw needn't show every extreme that they name: `active_blocks`: every batch has 1 to 6 active blocks; some batch has 6. `touch_slots`: -1 exactly at pairs with a block at or beyond the batch's active count; the other entries are distinct among the batches of one device, and a slot s names source device s // 3 along row+col.
All inputs are finite; a program needn't handle non-finite values.
Results may differ from a plain program's by a relative error of at most 0.0029.
Values may be sent and summed in bfloat16 or wider, within the bound.
No kernel may reach another device: no remote copies, remote signals or barrier semaphores. Data moves between devices by JAX's collectives and lax.ppermute only.
A program may use at most 128 MiB of HBM per device.

v0:
```python
import jax
import jax.numpy as jnp
from jax import lax
from jax.sharding import PartitionSpec as P

LDEG = 7
ATOM_COL = 2


def degrees(harm_count):
    harm_ids = jnp.arange(harm_count)
    bounds = jnp.arange(1, LDEG) ** 2
    return jnp.sum((harm_ids[:, None] >= bounds[None, :]).astype(jnp.int32), axis=1)


def shells_table(shell_row, shells):
    return (shell_row[:, None] == jnp.arange(shells)[None, :]).astype(jnp.float32)


def solve_radial(green_h, atom_mom):
    return jnp.einsum("hst,aht->ahs", green_h, atom_mom, precision=lax.Precision.HIGHEST)


def shards(
    density_tiles,
    send_list,
    basis_values,
    active_blocks,
    touch_slots,
    point_weights,
    harmonics,
    shell_index,
    batch_atom,
    radial_green,
):
    highest = lax.Precision.HIGHEST
    devices = lax.axis_size(("row", "col"))
    cols_axis = lax.axis_size("col")
    capacity = send_list.shape[2]
    tiles_dev = density_tiles.shape[0]
    block_size = density_tiles.shape[1]
    batches, points, span_width = basis_values.shape
    block_count = span_width // block_size
    harm_count = harmonics.shape[1]
    shells = radial_green.shape[1]
    outgoing = density_tiles[send_list[0]]
    arrived = lax.all_to_all(outgoing, ("row", "col"), split_axis=0, concat_axis=0, tiled=True)
    received = arrived.reshape(devices * capacity, block_size, block_size)
    places = jnp.arange(block_count)

    def masked(batch):
        active = active_blocks[batch]
        pair_mask = (places[:, None] < active) & (places[None, :] < active)
        slot_ids = jnp.clip(touch_slots[batch], 0, devices * capacity - 1)
        column = jnp.arange(span_width) // block_size < active
        values = jnp.where(
            column[None, :], basis_values[batch], jnp.zeros_like(basis_values[batch])
        )
        return (values, pair_mask, slot_ids)

    def first_pass(batch):
        values, pair_mask, slot_ids = masked(batch)
        tile_set = received[slot_ids]
        tile_set = jnp.where(pair_mask[:, :, None, None], tile_set, jnp.zeros_like(tile_set))
        matrix = jnp.transpose(tile_set, (0, 2, 1, 3)).reshape(span_width, span_width)
        product = jnp.dot(values, matrix, preferred_element_type=jnp.float32)
        density = jnp.sum(product * values, axis=1)
        onehot = shells_table(shell_index[batch], shells)
        weighted = harmonics[batch] * (point_weights[batch] * density)[None, :]
        moment = jnp.dot(weighted, onehot, precision=highest)
        return (density, moment)

    density_all, moment_all = lax.map(first_pass, jnp.arange(batches))
    natoms = ATOM_COL * cols_axis
    atom_hot = (batch_atom[:, None] == jnp.arange(natoms)[None, :]).astype(jnp.float32)
    local_atoms = jnp.einsum("ba,bhs->ahs", atom_hot, moment_all, precision=highest)
    green_h = radial_green[degrees(harm_count)]
    shared = lax.psum_scatter(local_atoms, "col", scatter_dimension=0, tiled=True)
    owned_sums = lax.psum(shared, "row")
    multipoles = solve_radial(green_h, owned_sums)
    everyone = lax.all_gather(multipoles, "col", axis=0, tiled=True)

    def second_pass(return_sums, batch):
        values, pair_mask, slot_ids = masked(batch)
        density = density_all[batch]
        onehot = shells_table(shell_index[batch], shells)
        atom_pot = everyone[batch_atom[batch]]
        pot_points = jnp.dot(atom_pot, onehot.T, precision=highest)
        hartree = jnp.sum(harmonics[batch] * pot_points, axis=0)
        potential = hartree - density * jnp.power(1.0 + density * density, -1.0 / 3.0)
        scaled = (values * (point_weights[batch] * potential)[:, None]).astype(jnp.bfloat16)
        ham_batch = jnp.dot(values.T, scaled, preferred_element_type=jnp.float32)
        pieces = jnp.transpose(
            ham_batch.reshape(block_count, block_size, block_count, block_size), (0, 2, 1, 3)
        )
        pieces = jnp.where(pair_mask[:, :, None, None], pieces, jnp.zeros_like(pieces))
        flat_pieces = pieces.reshape(block_count * block_count, block_size, block_size)
        return (return_sums.at[slot_ids.reshape(-1)].add(flat_pieces), None)

    start = jnp.zeros((devices * capacity, block_size, block_size), jnp.float32)
    return_sums, _ = lax.scan(second_pass, start, jnp.arange(batches))
    returned = lax.all_to_all(
        return_sums.reshape(devices, capacity, block_size, block_size),
        ("row", "col"),
        split_axis=0,
        concat_axis=0,
        tiled=True,
    )
    flat_back = returned.reshape(devices * capacity, block_size, block_size)
    ham_tiles = (
        jnp.zeros((tiles_dev, block_size, block_size), jnp.float32)
        .at[send_list[0].reshape(-1)]
        .add(flat_back)
    )
    return (ham_tiles, multipoles)


def solution(mesh):
    in_specs = (
        P(("row", "col"), None, None),
        P(("row", "col"), None, None),
        P(("row", "col"), None, None),
        P(("row", "col")),
        P(("row", "col"), None, None),
        P(("row", "col"), None),
        P(("row", "col"), None, None),
        P(("row", "col"), None),
        P(("row", "col")),
        P(),
    )
    out_specs = (P(("row", "col"), None, None), P("col", None, None))
    return jax.shard_map(shards, mesh=mesh, in_specs=in_specs, out_specs=out_specs, check_vma=False)
```

profile of v0, /device:TPU:0, one launch (start us, length us, event | category | flops | bytes accessed | tf_op | source)
XLA Modules:
  0.0 432.0 jit_solution(14020361378474756144)
XLA Ops:
  8.4 2.7 gather_fusion.1
  11.1 7.4 %all-to-all-start = ((bf16[32,3,128,128]{3,2,1,0:T(8,128)(2,1)}), bf16[32,3,128,128]{3,2,1,0:T(8,128)(2,1)}, u32[]{:S(2)}, u32[]{:S(2)}) async-start(bf16[32,3,128,128]{3,2,1,0:T(8,128)(2,1)} %bitcast.142), calls=%async_computation | async-start | bytes 6291456 | tf_op jit(solution)/shard_map/all_to_all | solution.py:47
  18.7 8.8 %copy.46 = bf16[2,2048,768]{1,2,0:T(8,128)(2,1)} copy(bf16[2,2048,768]{2,1,0:T(8,128)(2,1)} %param.16) | data formatting | bytes 12582912
  27.4 1.4 copy.47
  28.9 61.0 %all-to-all-done = bf16[32,3,128,128]{3,2,1,0:T(8,128)(2,1)} async-done(((bf16[32,3,128,128]{3,2,1,0:T(8,128)(2,1)}), bf16[32,3,128,128]{3,2,1,0:T(8,128)(2,1)}, u32[]{:S(2)}, u32[]{:S(2)}) %all-to-all-start) | async-done | bytes 3145760 | tf_op jit(solution)/shard_map/all_to_all | solution.py:47
  89.9 32.0 %while.28 = (s32[]{:T(128)}, f32[2,2048]{1,0:T(2,128)S(1)}, f32[2,49,128]{2,0,1:T(2,128)S(1)}, s32[2]{0:T(128)S(1)}, s32[2]{0:T(128)S(1)}, /*index=5*/bf16[2,204...) while((s32[]{:T(128)}, f32[2,2048]{1,0:T(2,128)S(1)}, ...), condition=%wide.region_2.3_spmd.clone, body=%wide.region_0.2_spmd.clone.sunk | while | flops 2578884608 | bytes 13258131 | solution.py:73
  92.6 2.7 gather_fusion
  98.0 5.9 %multiply_reduce_fusion.2 = f32[2048]{0:T(1024)S(1)} fusion(bf16[2,2048,768]{1,2,0:T(8,128)(2,1)} %get-tuple-element.691, s32[]{:T(128)S(6)} %select_n.214, pred[768]{0:T(1024)(128)(4,1)S(1)} %fusion.56, bf16[96,8,6,128]{3,2,1,0:T(8,128)(2,1)S(1)} %bitcast.141), kind=kOutput, calls=%fused_computation.35.clone.1 | convolution fusion | flops 2423781376 | bytes 7875584 | tf_op jit(solution)/shard_map/while/body/eval_jaxpr/dot_general | solution.py:66
  104.0 1.6 convolution_bitcast_fusion.3
  108.5 2.7 gather_fusion
  114.0 5.9 %multiply_reduce_fusion.2 = f32[2048]{0:T(1024)S(1)} fusion(bf16[2,2048,768]{1,2,0:T(8,128)(2,1)} %get-tuple-element.691, s32[]{:T(128)S(6)} %select_n.214, pred[768]{0:T(1024)(128)(4,1)S(1)} %fusion.56, bf16[96,8,6,128]{3,2,1,0:T(8,128)(2,1)S(1)} %bitcast.141), kind=kOutput, calls=%fused_computation.35.clone.1 | convolution fusion | flops 2423781376 | bytes 7875584 | tf_op jit(solution)/shard_map/while/body/eval_jaxpr/dot_general | solution.py:66
  120.0 1.6 convolution_bitcast_fusion.3
  121.9 1.2 fusion.32
  124.4 2.5 gather_fusion.2
  126.9 49.1 %all-reduce.3.cloned.1.call-done = f32[16,49,128]{2,0,1:T(8,128)} async-done(((f32[16,49,128]{2,0,1:T(8,128)}), f32[16,49,128]{2,0,1:T(8,128)}) %all-reduce.3.cloned.1.call-update) | async-done | bytes 401424
  176.9 19.6 %psum.7 = f32[2,49,128]{2,0,1:T(2,128)S(1)} all-reduce(f32[2,49,128]{2,0,1:T(2,128)S(1)} %constant_dynamic-slice_fusion.5), channel_id=1, replica_groups=mesh['row'=4,'col'=8] {'row'}, use_global_device_ids=true, to_apply=%region_4.5 | all-reduce | flops 12544 | bytes 100352 | tf_op jit(solution)/shard_map/psum | solution.py:79
  196.5 7.0 %convolution_bitcast_fusion.1 = f32[2,49,128]{2,0,1:T(2,128)S(1)} fusion(f32[2,49,128]{2,0,1:T(2,128)S(1)} %psum.7, f32[49,128,128]{2,1,0:T(8,128)} %gather_fusion.2), kind=kOutput, calls=%fused_computation.69 | convolution fusion | flops 19267584 | bytes 3311616 | tf_op jit(solution)/shard_map/hst,aht->ahs/dot_general | solution.py:21
  203.5 11.6 %all_gather.3 = f32[16,49,128]{2,1,0:T(8,128)} all-gather(f32[2,49,128]{2,1,0:T(8,128)S(1)} %copy.44), channel_id=1, replica_groups=mesh['row'=4,'col'=8] {'col'}, dimensions={0}, use_global_device_ids=true | all-gather | bytes 451584 | tf_op jit(solution)/shard_map/all_gather | solution.py:81
  215.1 3.4 broadcast_in_dim.92
  218.5 48.6 %while.29 = (s32[]{:T(128)}, f32[96,128,128]{2,1,0:T(8,128)}, s32[2]{0:T(128)S(1)}, s32[2,6,6]{2,0,1:T(2,128)S(1)}, s32[2]{0:T(128)S(1)}, /*index=5*/bf16[2,2048...) while((s32[]{:T(128)}, f32[96,128,128]{2,1,0:T(8,128)}, ...), condition=%wide.region_9.10_spmd.clone, body=%wide.region_6.9_spmd.clone.sunk | while | flops 2578009088 | bytes 25762944 | solution.py:101
  223.9 1.9 fusion.62
  227.3 2.8 multiply_convert_fusion.2
  230.8 2.6 convolution_select_fusion.2
  233.6 9.2 %scatter_fusion = f32[96,128,128]{2,1,0:T(8,128)} fusion(f32[96,128,128]{2,1,0:T(8,128)} %get-tuple-element.717, s32[36]{0:T(128)S(1)} %fusion.61, f32[36,128,128]{2,1,0:T(8,128)S(1)} %bitcast.140), kind=kCustom, calls=%fused_computation.3.clone.clone.1 | custom fusion | flops 589824 | bytes 7078032 | tf_op jit(solution)/shard_map/while/body/eval_jaxpr/scatter-add | solution.py:98
  248.2 1.9 fusion.62
  251.6 2.8 multiply_convert_fusion.2
  255.1 2.6 convolution_select_fusion.2
  257.9 9.2 %scatter_fusion = f32[96,128,128]{2,1,0:T(8,128)} fusion(f32[96,128,128]{2,1,0:T(8,128)} %get-tuple-element.717, s32[36]{0:T(128)S(1)} %fusion.61, f32[36,128,128]{2,1,0:T(8,128)S(1)} %bitcast.140), kind=kCustom, calls=%fused_computation.3.clone.clone.1 | custom fusion | flops 589824 | bytes 7078032 | tf_op jit(solution)/shard_map/while/body/eval_jaxpr/scatter-add | solution.py:98
  267.1 3.7 all-to-all-start.1
  271.1 139.5 %all-to-all-done.1 = f32[32,3,128,128]{3,2,1,0:T(8,128)} async-done(((f32[32,3,128,128]{3,2,1,0:T(8,128)}), f32[32,3,128,128]{3,2,1,0:T(8,128)}, u32[]{:S(2)}, u32[]{:S(2)}) %all-to-all-start.1) | async-done | bytes 6291488 | tf_op jit(solution)/shard_map/all_to_all | solution.py:102
  410.8 12.9 %scatter_fusion.1 = f32[32,128,128]{2,1,0:T(8,128)S(1)} fusion(f32[32,128,128]{2,1,0:T(8,128)S(1)} %broadcast_in_dim.91, s32[96]{0:T(128)S(1)} %fusion.36, f32[96,128,128]{2,1,0:T(8,128)} %bitcast.9), kind=kCustom, calls=%fused_computation.4 | custom fusion | flops 1572864 | bytes 18874752 | tf_op jit(solution)/shard_map/scatter-add | solution.py:113
  423.8 1.3 copy-done.1
  (98 shorter events, 18.2 us)
Async XLA Ops:
  7.2 1.2 copy-start
  11.1 78.8 %all-to-all-start = ((bf16[32,3,128,128]{3,2,1,0:T(8,128)(2,1)}), bf16[32,3,128,128]{3,2,1,0:T(8,128)(2,1)}, u32[]{:S(2)}, u32[]{:S(2)}) async-start(bf16[32,3,128,128]{3,2,1,0:T(8,128)(2,1)} %bitcast.142), calls=%async_computation | async-start | bytes 6291456 | tf_op jit(solution)/shard_map/all_to_all | solution.py:47
  18.5 157.4 %all-reduce.3.cloned.1.call-start = ((), (), s32[]{:S(2)}) async-start(), calls=%async_computation.2 | async-start | bytes 802816
  18.6 8.8 %copy-start.3 = (f32[2,49,2048]{2,0,1:T(2,128)S(1)}, f32[2,49,2048]{2,0,1:T(2,128)}, u32[]{:S(2)}) copy-start(f32[2,49,2048]{2,0,1:T(2,128)} %param.20) | copy-start | bytes 2408452
  18.6 71.2 %copy-start.4 = (f32[2,2048]{1,0:T(2,128)S(1)}, f32[2,2048]{1,0:T(2,128)}, u32[]{:S(2)}) copy-start(f32[2,2048]{1,0:T(2,128)} %param.19) | copy-start | bytes 49156
  18.6 71.2 %copy-start.5 = (s32[2,2048]{1,0:T(2,128)S(1)}, s32[2,2048]{1,0:T(2,128)}, u32[]{:S(2)}) copy-start(s32[2,2048]{1,0:T(2,128)} %param.21) | copy-start | bytes 49156
  18.6 71.2 %copy-start.7 = (s32[2,6,6]{2,0,1:T(2,128)S(1)}, s32[2,6,6]{2,0,1:T(2,128)}, u32[]{:S(2)}) copy-start(s32[2,6,6]{2,0,1:T(2,128)} %param.18) | copy-start | bytes 868
  18.7 71.2 %copy-start.10 = (s32[2]{0:T(128)S(1)}, s32[2]{0:T(128)}, u32[]{:S(2)}) copy-start(s32[2]{0:T(128)} %param.17) | copy-start | bytes 28
  89.9 32.0 %copy-start.9 = (s32[2]{0:T(128)S(1)}, s32[2]{0:T(128)}, u32[]{:S(2)}) copy-start(s32[2]{0:T(128)} %param.22) | copy-start | bytes 28
  89.9 33.3 %copy-start.11 = (u32[32]{0:T(128)S(1)}, u32[32]{0:T(128)}, u32[]{:S(2)}) copy-start(u32[32]{0:T(128)} %constant.178) | copy-start | bytes 388
  89.9 34.5 %copy-start.2 = (f32[7,128,128]{2,1,0:T(8,128)S(1)}, f32[7,128,128]{2,1,0:T(8,128)}, u32[]{:S(2)}) copy-start(f32[7,128,128]{2,1,0:T(8,128)} %param.23) | copy-start | bytes 1376260
  203.5 15.0 %copy-start.6 = (f32[2,49,128]{2,0,1:T(2,128)}, f32[2,49,128]{2,0,1:T(2,128)S(1)}, u32[]{:S(2)}) copy-start(f32[2,49,128]{2,0,1:T(2,128)S(1)} %convolution_bitcast_fusion.1) | copy-start | bytes 150532
  267.1 3.8 copy-start.8
  267.1 143.5 %all-to-all-start.1 = ((f32[32,3,128,128]{3,2,1,0:T(8,128)}), f32[32,3,128,128]{3,2,1,0:T(8,128)}, u32[]{:S(2)}, u32[]{:S(2)}) async-start(f32[32,3,128,128]{3,2,1,0:T(8,128)} %bitcast.137), calls=%async_computation.1 | async-start | bytes 12582912 | tf_op jit(solution)/shard_map/all_to_all | solution.py:102
  423.8 1.3 copy-start.1
Sparse Core Ops, SparseCore 0:
  123.3 52.6 all-reduce.2
where the time goes:
time: 434 us; the launch traced here: 432 us
  waiting for transfers between devices  250 us (58%)
  other arithmetic  45.2 us (10%)
  local copies, waits for them, and re-layouts  35.3 us (8%)
  matrix products  32.4 us (7%)
  blocking collectives  31.2 us (7%)
  between operations  14.9 us (3%)
  loops' own time  12.2 us (3%)
  starting transfers between devices  11.2 us (3%)
    all_to_all x1, waiting for transfers between devices, shards(): lax.all_to_all(return_sums.reshape(devices, capacity, block_size, block_s...  140 us
    all_to_all x1, waiting for transfers between devices, shards(): lax.all_to_all(outgoing, ('row', 'col'), split_axis=0, concat_axis=0, til...  61 us
    unnamed x2, waiting for transfers between devices  49.1 us
    psum x1, blocking collectives, shards(): owned_sums = lax.psum(shared, 'row')  19.6 us
    scatter-add x2, other arithmetic, second_pass(): return (return_sums.at[slot_ids.reshape(-1)].add(flat_pieces), None)  18.4 us
    unnamed x29, local copies, waits for them, and re-layouts  13.4 us
    scatter-add x1, other arithmetic, shards(): ham_tiles = jnp.zeros((tiles_dev, block_size, block_size), jnp.float32).a...  12.9 us
    dot_general x2, matrix products, first_pass(): product = jnp.dot(values, matrix, preferred_element_type=jnp.float32)  11.8 us
  transfers between devices with their start and end apart: 3, of which 3 were waited for; matrix products, arithmetic and copies ran while one was open for 3% of the time, Pallas kernels for 0%

commit v1 on v0

v1 whole, which is shorter than its diff:
```python
import jax
import jax.numpy as jnp
from jax import lax
from jax.experimental import pallas as pl
from jax.experimental.pallas import tpu as pltpu
from jax.sharding import PartitionSpec as P

LDEG = 7
ATOM_COL = 2
AXES = ("row", "col")
F32 = jnp.float32
BF16 = jnp.bfloat16
NT = (((1,), (1,)), ((), ()))


def degrees(harm_ids):
    bounds = jnp.arange(1, LDEG) ** 2
    return jnp.sum((harm_ids[:, None] >= bounds[None, :]).astype(jnp.int32), axis=1)


def full(shape):
    return pl.BlockSpec(shape, lambda *_: (0,) * len(shape), pipeline_mode=pl.Buffered(1))


def params(mib):
    return pltpu.CompilerParams(
        dimension_semantics=("arbitrary",), vmem_limit_bytes=mib * 1024 * 1024
    )


def split3(values):
    high = values.astype(BF16)
    rest = values - high.astype(F32)
    mid = rest.astype(BF16)
    low = (rest - mid.astype(F32)).astype(BF16)
    return jnp.concatenate([high, mid, low], axis=0)


def join3(stacked):
    rows = stacked.shape[0] // 3
    return stacked[:rows] + (stacked[rows : 2 * rows] + stacked[2 * rows :])


def gather_tiles(tile_ids, tiles):
    count = tile_ids.shape[0]
    _, blk, _ = tiles.shape
    step = count // 8

    def body(ids, tiles_ref, out_ref):
        first = pl.program_id(0) * step
        for place in range(step):
            out_ref[place] = tiles_ref[ids[first + place]]

    return pl.pallas_call(
        body,
        out_shape=jax.ShapeDtypeStruct((count, blk, blk), tiles.dtype),
        grid_spec=pltpu.PrefetchScalarGridSpec(
            num_scalar_prefetch=1,
            grid=(count // step,),
            in_specs=[full(tiles.shape)],
            out_specs=pl.BlockSpec((step, blk, blk), lambda i, ids: (i, 0, 0)),
        ),
        compiler_params=params(16),
        name="gather_tiles",
    )(tile_ids, tiles)


def sum_tiles(tile_ids, arrived, tiles_dev):
    count, blk, _ = arrived.shape
    step = count // 8

    def body(ids, arrived_ref, out_ref):
        @pl.when(pl.program_id(0) == 0)
        def _():
            out_ref[...] = jnp.zeros_like(out_ref)

        first = pl.program_id(0) * step
        for place in range(step):
            tile = ids[first + place]
            out_ref[tile] = out_ref[tile] + arrived_ref[place].astype(F32)

    return pl.pallas_call(
        body,
        out_shape=jax.ShapeDtypeStruct((tiles_dev, blk, blk), F32),
        grid_spec=pltpu.PrefetchScalarGridSpec(
            num_scalar_prefetch=1,
            grid=(count // step,),
            in_specs=[pl.BlockSpec((step, blk, blk), lambda i, ids: (i, 0, 0))],
            out_specs=full((tiles_dev, blk, blk)),
        ),
        compiler_params=params(16),
        name="sum_tiles",
    )(tile_ids, arrived)


def density_pass(active, slots, atoms, received, basis_t, harmonics, weights, shells, share, devices):
    batches, span, points = basis_t.shape
    slot_count, blk, _ = received.shape
    blocks = span // blk
    rows = harmonics.shape[1]
    radial = share[1]
    held = share[0]
    chunk = min(512, points)
    lines = (held + 1) * batches

    def body(act, slot_ids, atom_ids, recv, phi, harm, wts, shell, rho_out, send, matrix, mom_keep):
        batch = pl.program_id(0)
        count = act[batch]

        for i in range(blocks):
            for j in range(blocks):
                spot = (pl.ds(i * blk, blk), pl.ds(j * blk, blk))
                live = (i < count) & (j < count)

                @pl.when(live)
                def _(i=i, j=j, spot=spot):
                    slot = jnp.clip(slot_ids[batch, i * blocks + j], 0, slot_count - 1)
                    matrix[spot] = recv[slot]

                @pl.when(jnp.logical_not(live))
                def _(spot=spot):
                    matrix[spot] = jnp.zeros((blk, blk), BF16)

        def step(at, moments):
            cols = pl.ds(pl.multiple_of(at * chunk, chunk), chunk)
            phi_c = phi[0, :, cols]
            product = jnp.dot(matrix[...], phi_c, preferred_element_type=F32)
            rho = jnp.sum(product * phi_c.astype(F32), axis=0, keepdims=True)
            rho_out[0, :, cols] = rho
            weighted = harm[0, :, cols] * (wts[0, :, cols] * rho)
            ids = lax.broadcasted_iota(jnp.int32, (radial, chunk), 0)
            onehot = jnp.where(shell[0, :, cols] == ids, 1.0, 0.0).astype(BF16)
            return moments + lax.dot_general(
                split3(weighted), onehot, NT, preferred_element_type=F32
            )

        moments = lax.fori_loop(
            0, points // chunk, step, jnp.zeros((3 * rows, radial), F32)
        )
        mom_keep[...] = join3(moments)

        for b in range(batches):

            @pl.when(batch == b)
            def _(b=b):
                for k in range(held):
                    for d in range(devices):
                        line = d * held + k
                        if line < rows:
                            send[d, pl.ds(k * batches + b, 1), :] = mom_keep[pl.ds(line, 1), :]
                        else:
                            send[d, pl.ds(k * batches + b, 1), :] = jnp.zeros((1, radial), F32)
                send[:, pl.ds(held * batches + b, 1), :] = jnp.full(
                    (devices, 1, radial), atom_ids[b].astype(F32), F32
                )

    return pl.pallas_call(
        body,
        out_shape=(
            jax.ShapeDtypeStruct((batches, 1, points), F32),
            jax.ShapeDtypeStruct((devices, lines, radial), F32),
        ),
        grid_spec=pltpu.PrefetchScalarGridSpec(
            num_scalar_prefetch=3,
            grid=(batches,),
            in_specs=[
                full(received.shape),
                pl.BlockSpec((1, span, points), lambda b, *_: (b, 0, 0)),
                pl.BlockSpec((1, rows, points), lambda b, *_: (b, 0, 0)),
                pl.BlockSpec((1, 1, points), lambda b, *_: (b, 0, 0)),
                pl.BlockSpec((1, 1, points), lambda b, *_: (b, 0, 0)),
            ],
            out_specs=(
                pl.BlockSpec((1, 1, points), lambda b, *_: (b, 0, 0)),
                full((devices, lines, radial)),
            ),
            scratch_shapes=[pltpu.VMEM((span, span), BF16), pltpu.VMEM((rows, radial), F32)],
        ),
        compiler_params=params(32),
        name="density_pass",
    )(active, slots, atoms, received, basis_t, harmonics, weights, shells)


def radial_solve(degree_ids, arrived, green, natoms, held, batches, cols_count):
    devices, lines, radial = arrived.shape
    rows_out = (batches + ATOM_COL) * held

    def body(deg, got, green_ref, out, flat):
        for r in range(lines):
            for d in range(devices):
                flat[r, pl.ds(d, 1), :] = got[d, pl.ds(r, 1), :]
        atom_of = [flat[held * batches + b] for b in range(batches)]
        for k in range(held):
            sums = []
            for a in range(natoms):
                total = jnp.zeros((devices, radial), F32)
                for b in range(batches):
                    total = total + jnp.where(atom_of[b] == float(a), flat[k * batches + b], 0.0)
                sums.append(jnp.sum(total, axis=0, keepdims=True))
            atom_mom = jnp.concatenate(sums, axis=0)
            solved = lax.dot_general(
                atom_mom,
                green_ref[deg[k]],
                NT,
                precision=lax.Precision.HIGHEST,
                preferred_element_type=F32,
            )
            for b in range(batches):
                picked = jnp.zeros((devices, radial), F32)
                for a in range(natoms):
                    picked = jnp.where(atom_of[b] == float(a), solved[a : a + 1, :], picked)
                for d in range(devices):
                    out[d, pl.ds(b * held + k, 1), :] = picked[d : d + 1, :]
            for own in range(ATOM_COL):
                for d in range(devices):
                    a = (d % cols_count) * ATOM_COL + own
                    out[d, pl.ds((batches + own) * held + k, 1), :] = solved[a : a + 1, :]

    return pl.pallas_call(
        body,
        out_shape=jax.ShapeDtypeStruct((devices, rows_out, radial), F32),
        grid_spec=pltpu.PrefetchScalarGridSpec(
            num_scalar_prefetch=1,
            grid=(1,),
            in_specs=[full(arrived.shape), full(green.shape)],
            out_specs=full((devices, rows_out, radial)),
            scratch_shapes=[pltpu.VMEM((lines, devices, radial), F32)],
        ),
        compiler_params=params(16),
        name="radial_solve",
    )(degree_ids, arrived, green)


def potential_pass(active, slots, poles, rho, basis_t, harmonics, weights, shells, slot_count, blk, held):
    batches, span, points = basis_t.shape
    blocks = span // blk
    rows = harmonics.shape[1]
    devices, lines, radial = poles.shape
    chunk = min(512, points)
    wide = 2 * blk if blocks % 2 == 0 else blk

    def body(act, slot_ids, got, rho_ref, phi, harm, wts, shell, out, scaled, poles_keep):
        batch = pl.program_id(0)
        count = act[batch]

        @pl.when(batch == 0)
        def _():
            out[...] = jnp.zeros_like(out)

        for b in range(batches):

            @pl.when(batch == b)
            def _(b=b):
                for k in range(held):
                    for d in range(devices):
                        line = d * held + k
                        if line < rows:
                            poles_keep[pl.ds(line, 1), :] = got[d, pl.ds(b * held + k, 1), :]

        if held * devices < rows:
            poles_keep[pl.ds(held * devices, rows - held * devices), :] = jnp.zeros(
                (rows - held * devices, radial), F32
            )
        stacked = split3(poles_keep[...])

        def step(at, carry):
            cols = pl.ds(pl.multiple_of(at * chunk, chunk), chunk)
            ids = lax.broadcasted_iota(jnp.int32, (radial, chunk), 0)
            onehot = jnp.where(shell[0, :, cols] == ids, 1.0, 0.0).astype(BF16)
            at_points = join3(jnp.dot(stacked, onehot, preferred_element_type=F32))
            hartree = jnp.sum(harm[0, :, cols] * at_points, axis=0, keepdims=True)
            rho_c = rho_ref[0, :, cols]
            root = jnp.exp(jnp.log(1.0 + rho_c * rho_c) * (-1.0 / 3.0))
            factor = wts[0, :, cols] * (hartree - rho_c * root)
            scaled[:, cols] = (phi[0, :, cols].astype(F32) * factor).astype(BF16)
            return carry

        lax.fori_loop(0, points // chunk, step, 0)

        for first in range(0, span, wide):
            piece = lax.dot_general(
                phi[0], scaled[pl.ds(first, wide), :], NT, preferred_element_type=F32
            )
            for i in range(blocks):
                for j in range(first // blk, (first + wide) // blk):

                    @pl.when((i < count) & (j < count))
                    def _(i=i, j=j, piece=piece, first=first):
                        slot = jnp.clip(slot_ids[batch, i * blocks + j], 0, slot_count - 1)
                        left = j * blk - first
                        out[slot] = piece[i * blk : (i + 1) * blk, left : left + blk].astype(BF16)

    return pl.pallas_call(
        body,
        out_shape=jax.ShapeDtypeStruct((slot_count, blk, blk), BF16),
        grid_spec=pltpu.PrefetchScalarGridSpec(
            num_scalar_prefetch=2,
            grid=(batches,),
            in_specs=[
                full(poles.shape),
                pl.BlockSpec((1, 1, points), lambda b, *_: (b, 0, 0)),
                pl.BlockSpec((1, span, points), lambda b, *_: (b, 0, 0)),
                pl.BlockSpec((1, rows, points), lambda b, *_: (b, 0, 0)),
                pl.BlockSpec((1, 1, points), lambda b, *_: (b, 0, 0)),
                pl.BlockSpec((1, 1, points), lambda b, *_: (b, 0, 0)),
            ],
            out_specs=full((slot_count, blk, blk)),
            scratch_shapes=[pltpu.VMEM((span, points), BF16), pltpu.VMEM((rows, radial), F32)],
        ),
        compiler_params=params(32),
        name="potential_pass",
    )(active, slots, poles, rho, basis_t, harmonics, weights, shells)


def exchange(parts):
    return lax.all_to_all(parts, AXES, split_axis=0, concat_axis=0, tiled=True)


def shards(
    density_tiles,
    send_list,
    basis_values,
    active_blocks,
    touch_slots,
    point_weights,
    harmonics,
    shell_index,
    batch_atom,
    radial_green,
):
    devices = lax.axis_size(AXES)
    cols_count = lax.axis_size("col")
    capacity = send_list.shape[2]
    tiles_dev, blk, _ = density_tiles.shape
    batches, points, span = basis_values.shape
    harm_count = harmonics.shape[1]
    radial = radial_green.shape[1]
    slot_count = devices * capacity
    natoms = ATOM_COL * cols_count
    held = -(-harm_count // devices)
    rows = -(-harm_count // 16) * 16

    tile_ids = send_list.reshape(-1)
    outgoing = gather_tiles(tile_ids, density_tiles)
    arrived = exchange(outgoing.reshape(devices, capacity, blk, blk))
    received = arrived.reshape(slot_count, blk, blk)

    basis_t = jnp.transpose(basis_values, (0, 2, 1))
    harm_rows = jnp.pad(harmonics, ((0, 0), (0, rows - harm_count), (0, 0)))
    weights = point_weights[:, None, :]
    shells = shell_index[:, None, :]
    slots = touch_slots.reshape(batches, -1)

    rho, mom_out = density_pass(
        active_blocks, slots, batch_atom, received, basis_t, harm_rows, weights, shells,
        (held, radial), devices,
    )
    mom_in = exchange(mom_out)
    first = lax.axis_index(AXES) * held
    degree_ids = degrees(jnp.minimum(first + jnp.arange(held), harm_count - 1))
    poles_out = radial_solve(
        degree_ids, mom_in, radial_green, natoms, held, batches, cols_count
    )
    poles = exchange(poles_out)
    returning = potential_pass(
        active_blocks, slots, poles, rho, basis_t, harm_rows, weights, shells,
        slot_count, blk, held,
    )
    back = exchange(returning.reshape(devices, capacity, blk, blk))
    ham_tiles = sum_tiles(tile_ids, back.reshape(slot_count, blk, blk), tiles_dev)

    own = poles[:, batches * held :, :].reshape(devices, ATOM_COL, held, radial)
    own = jnp.transpose(own, (1, 0, 2, 3)).reshape(ATOM_COL, devices * held, radial)
    return (ham_tiles, own[:, :harm_count])


def solution(mesh):
    in_specs = (
        P(AXES, None, None),
        P(AXES, None, None),
        P(AXES, None, None),
        P(AXES),
        P(AXES, None, None),
        P(AXES, None),
        P(AXES, None, None),
        P(AXES, None),
        P(AXES),
        P(),
    )
    out_specs = (P(AXES, None, None), P("col", None, None))
    return jax.shard_map(shards, mesh=mesh, in_specs=in_specs, out_specs=out_specs, check_vma=False)
```

time: 434 us -> 222 us (0.51)
  waiting for transfers between devices: 250 us -> 136 us
  other arithmetic: 45.2 us -> 0.19 us
  Pallas kernels: 0 us -> 34.4 us
  matrix products: 32.4 us -> 0 us
  blocking collectives: 31.2 us -> 9.97 us
  between operations: 14.9 us -> 0.75 us
  loops' own time: 12.2 us -> 0 us
  local copies, waits for them, and re-layouts: 35.3 us -> 25.4 us
    all_to_all x2 -> x3, waiting for transfers between devices: 200 us -> 136 us  [exchange(): return lax.all_to_all(parts, AXES, split_axis=0, concat_axis=0, tiled=True)]
    unnamed x2 -> x0, waiting for transfers between devices: 49.1 us -> none
    pallas_call x0 -> x5, Pallas kernels: none -> 34.4 us  [the longest x1 16.1 us: potential_pass(): pl.pallas_call(body, out_shape=jax.ShapeDtypeStruct((slot_count, blk, blk...]
    dot_general x10 -> x0, matrix products: 32.4 us -> none  [the longest x2 11.8 us: first_pass(): product = jnp.dot(values, matrix, preferred_element_type=jnp.float32)]
    scatter-add x3 -> x0, other arithmetic: 31.4 us -> none  [the longest x2 18.4 us: second_pass(): return (return_sums.at[slot_ids.reshape(-1)].add(flat_pieces), None)]
    psum x1 -> x0, blocking collectives: 19.6 us -> none  [shards(): owned_sums = lax.psum(shared, 'row')]
    another operation x2 -> x0, loops' own time: 12.2 us -> none  [the longest x1 8.27 us: shards(): return_sums, _ = lax.scan(second_pass, start, jnp.arange(batches))]
    all_gather x1 -> x0, blocking collectives: 11.6 us -> none  [shards(): everyone = lax.all_gather(multipoles, 'col', axis=0, tiled=True)]
  transfers between devices with their start and end apart: 3 -> 3, of which waited for: 3 -> 3; matrix products, arithmetic and copies ran while one was open for 3% -> 7% of each run, Pallas kernels for 0% -> 0%
where the time goes in v1:
time: 222 us; the launch traced here: 221 us
  waiting for transfers between devices  136 us (61%)
  Pallas kernels  34.4 us (15%)
  local copies, waits for them, and re-layouts  25.4 us (11%)
  starting transfers between devices  13.9 us (6%)
  blocking collectives  9.97 us (4%)
    all_to_all x3, waiting for transfers between devices, exchange(): return lax.all_to_all(parts, AXES, split_axis=0, concat_axis=0, tiled=True)  136 us
    unnamed x26, local copies, waits for them, and re-layouts  22.3 us
    pallas_call x1, Pallas kernels, potential_pass(): pl.pallas_call(body, out_shape=jax.ShapeDtypeStruct((slot_count, blk, blk...  16.1 us
    all_to_all x3, starting transfers between devices, exchange(): return lax.all_to_all(parts, AXES, split_axis=0, concat_axis=0, tiled=True)  13.9 us
    pallas_call x1, Pallas kernels, density_pass(): pl.pallas_call(body, out_shape=(jax.ShapeDtypeStruct((batches, 1, points)...  10.4 us
    all_to_all x1, blocking collectives, exchange(): return lax.all_to_all(parts, AXES, split_axis=0, concat_axis=0, tiled=True)  9.97 us
  transfers between devices with their start and end apart: 3, of which 3 were waited for; matrix products, arithmetic and copies ran while one was open for 7% of the time, Pallas kernels for 0%

profile of v1, /device:TPU:0, one launch (start us, length us, event | category | flops | bytes accessed | tf_op | source)
XLA Modules:
  0.0 221.1 jit_solution(13032470247070760467)
XLA Ops:
  0.6 0.8 copy.22
  1.4 0.1 reshape.38.ids
  1.5 0.0 copy-start.4
  1.5 1.2 copy-done.4
  2.7 3.9 %gather_tiles.1 = bf16[96,128,128]{2,1,0:T(8,128)(2,1)} custom-call(s32[96]{0:T(128)S(1)} %reshape.38.ids, bf16[32,128,128]{2,1,0:T(8,128)(2,1)S(1)} %copy-done.4), custom_call_target="tpu_custom_call" | custom-call | tf_op jit(solution)/shard_map/gather_tiles/pallas_call | solution.py:54
  6.7 7.3 %all-to-all-start = ((bf16[32,3,128,128]{3,2,1,0:T(8,128)(2,1)}), bf16[32,3,128,128]{3,2,1,0:T(8,128)(2,1)S(1)}, u32[]{:S(2)}, u32[]{:S(2)}) async-start(bf16[32,3,128,128]{3,2,1,0:T(8,128)(2,1)} %bitcast), calls=%async_computation | async-start | bytes 6291456 | tf_op jit(solution)/shard_map/all_to_all | solution.py:316
  14.0 0.0 copy-done.10
  14.0 0.1 reshape.39.slot_ids
  14.1 0.0 copy-done.8
  14.1 0.0 copy-done.9
  14.1 2.5 %copy.25 = f32[2,49,2048]{2,1,0:T(8,128)} copy(f32[2,49,2048]{2,0,1:T(2,128)} %param.16) | data formatting | bytes 1605632 | tf_op args[6]
  16.7 8.7 %copy.24 = bf16[2,2048,768]{1,2,0:T(8,128)(2,1)} copy(bf16[2,2048,768]{2,1,0:T(8,128)(2,1)} %param.12) | data formatting | bytes 12582912 | tf_op args[2]
  25.4 2.2 %pad.4.harm = f32[2,64,2048]{2,1,0:T(8,128)} pad(f32[2,49,2048]{2,1,0:T(8,128)} %copy.25, f32[]{:T(128)} %constant.19.clone.1), padding=0_0x0_15x0_0 | pad | bytes 1851396 | tf_op jit(solution)/shard_map/jit(_pad)/pad | solution.py:349
  27.7 57.6 %all-to-all-done = bf16[32,3,128,128]{3,2,1,0:T(8,128)(2,1)S(1)} async-done(((bf16[32,3,128,128]{3,2,1,0:T(8,128)(2,1)}), bf16[32,3,128,128]{3,2,1,0:T(8,128)(2,1)S(1)}, u32[]{:S(2)}, u32[]{:S(2)}) %all-to-all-start) | async-done | bytes 3145760 | tf_op jit(solution)/shard_map/all_to_all | solution.py:316
  85.3 0.0 copy-done.6
  85.3 0.0 copy-done.7
  85.3 2.8 %copy-done = bf16[2,2048,768]{1,2,0:T(8,128)(2,1)S(1)} copy-done((bf16[2,2048,768]{1,2,0:T(8,128)(2,1)S(1)}, bf16[2,2048,768]{1,2,0:T(8,128)(2,1)}, u32[]{:S(2)}) %copy-start) | copy-done | bytes 6291480
  88.1 1.2 copy-done.2
  89.3 10.4 %density_pass.1 = (f32[2,1,2048]{2,1,0:T(1,128)S(1)}, f32[32,6,128]{2,1,0:T(8,128)}) custom-call(s32[2]{0:T(128)S(1)} %copy-done.6, s32[2,36]{1,0:T(2,128)S(1)} %reshape.39.slot_ids, s32[2]{0:T(128)S(1)} %copy-done.7, bf16[96,128,128]{2,1,0:T(8,128)(2,1)S(1)} %bitcast.11, bf16[2,768,2048]{2,1,0:T(8,128)(2,1)S(1)} %bitcast.9, f32[2,64,2048]{2,1,0:T(8,128)S(1)} %copy-done.2, ...), custom_call_target="tpu_custom_call" | custom-call | tf_op jit(solution)/shard_map/density_pass/pallas_call | solution.py:157
  99.7 3.8 %all-to-all-start.1 = ((f32[32,6,128]{2,1,0:T(8,128)}), f32[32,6,128]{2,1,0:T(8,128)S(1)}, u32[]{:S(2)}, u32[]{:S(2)}) async-start(f32[32,6,128]{2,1,0:T(8,128)} %get-tuple-element.4), calls=%async_computation.1 | async-start | bytes 262144 | tf_op jit(solution)/shard_map/all_to_all | solution.py:316
  103.5 0.2 fusion.deg
  103.7 8.0 %all-to-all-done.1.got = f32[32,6,128]{2,1,0:T(8,128)S(1)} async-done(((f32[32,6,128]{2,1,0:T(8,128)}), f32[32,6,128]{2,1,0:T(8,128)S(1)}, u32[]{:S(2)}, u32[]{:S(2)}) %all-to-all-start.1) | async-done | bytes 98336 | tf_op jit(solution)/shard_map/all_to_all | solution.py:316
  111.7 1.0 copy-done.5
  112.7 1.1 radial_solve.1
  113.9 10.0 %all_to_all.20.got = f32[32,8,128]{2,1,0:T(8,128)S(1)} all-to-all(f32[32,8,128]{2,1,0:T(8,128)S(1)} %radial_solve.1), channel_id=1, replica_groups=mesh['row'=4,'col'=8] {'row','col'}, dimensions={0} | all-to-all | bytes 262144 | tf_op jit(solution)/shard_map/all_to_all | solution.py:316
  123.9 2.8 %copy-done.1 = bf16[2,2048,768]{1,2,0:T(8,128)(2,1)S(1)} copy-done((bf16[2,2048,768]{1,2,0:T(8,128)(2,1)S(1)}, bf16[2,2048,768]{1,2,0:T(8,128)(2,1)}, u32[]{:S(2)}) %copy-start.1) | copy-done | bytes 6291480
  126.6 1.2 copy-done.3
  127.9 16.1 %potential_pass.1 = bf16[96,128,128]{2,1,0:T(8,128)(2,1)} custom-call(s32[2]{0:T(128)S(1)} %copy-done.6, s32[2,36]{1,0:T(2,128)S(1)} %reshape.39.slot_ids, f32[32,8,128]{2,1,0:T(8,128)S(1)} %all_to_all.20.got, f32[2,1,2048]{2,1,0:T(1,128)S(1)} %get-tuple-element.5.rho_ref, bf16[2,768,2048]{2,1,0:T(8,128)(2,1)S(1)} %bitcast.10, f32[2,64,2048]{2,1,0:T(8,128)S(1)} %copy-done.3, ...), custom_call_target="tpu_custom_call" | custom-call | tf_op jit(solution)/shard_map/potential_pass/pallas_call | solution.py:293
  144.0 2.8 %all-to-all-start.3 = ((bf16[32,3,128,128]{3,2,1,0:T(8,128)(2,1)}), bf16[32,3,128,128]{3,2,1,0:T(8,128)(2,1)S(1)}, u32[]{:S(2)}, u32[]{:S(2)}) async-start(bf16[32,3,128,128]{3,2,1,0:T(8,128)(2,1)} %bitcast.3), calls=%async_computation.3 | async-start | bytes 6291456 | tf_op jit(solution)/shard_map/all_to_all | solution.py:316
  146.8 0.6 slice.9
  147.4 70.7 %all-to-all-done.3 = bf16[32,3,128,128]{3,2,1,0:T(8,128)(2,1)S(1)} async-done(((bf16[32,3,128,128]{3,2,1,0:T(8,128)(2,1)}), bf16[32,3,128,128]{3,2,1,0:T(8,128)(2,1)S(1)}, u32[]{:S(2)}, u32[]{:S(2)}) %all-to-all-start.3) | async-done | bytes 3145760 | tf_op jit(solution)/shard_map/all_to_all | solution.py:316
  218.2 2.9 %sum_tiles.1 = f32[32,128,128]{2,1,0:T(8,128)} custom-call(s32[96]{0:T(128)S(1)} %reshape.38.ids, bf16[96,128,128]{2,1,0:T(8,128)(2,1)S(1)} %bitcast.12), custom_call_target="tpu_custom_call" | custom-call | tf_op jit(solution)/shard_map/sum_tiles/pallas_call | solution.py:82
  (17 shorter events, 0.1 us)
Async XLA Ops:
  1.5 1.2 copy-start.4
  6.6 7.3 %copy-start.10 = (s32[2,6,6]{2,0,1:T(2,128)S(1)}, s32[2,6,6]{2,0,1:T(2,128)}, u32[]{:S(2)}) copy-start(s32[2,6,6]{2,0,1:T(2,128)} %param.14) | copy-start | bytes 868
  6.6 7.4 %copy-start.8 = (f32[2,2048]{1,0:T(2,128)S(1)}, f32[2,2048]{1,0:T(2,128)}, u32[]{:S(2)}) copy-start(f32[2,2048]{1,0:T(2,128)} %param.15) | copy-start | bytes 49156
  6.7 7.5 %copy-start.9 = (s32[2,2048]{1,0:T(2,128)S(1)}, s32[2,2048]{1,0:T(2,128)}, u32[]{:S(2)}) copy-start(s32[2,2048]{1,0:T(2,128)} %param.17) | copy-start | bytes 49156
  6.7 78.7 %all-to-all-start = ((bf16[32,3,128,128]{3,2,1,0:T(8,128)(2,1)}), bf16[32,3,128,128]{3,2,1,0:T(8,128)(2,1)S(1)}, u32[]{:S(2)}, u32[]{:S(2)}) async-start(bf16[32,3,128,128]{3,2,1,0:T(8,128)(2,1)} %bitcast), calls=%async_computation | async-start | bytes 6291456 | tf_op jit(solution)/shard_map/all_to_all | solution.py:316
  16.7 68.6 %copy-start.6 = (s32[2]{0:T(128)S(1)}, s32[2]{0:T(128)}, u32[]{:S(2)}) copy-start(s32[2]{0:T(128)} %act.3) | copy-start | bytes 28
  16.7 68.6 %copy-start.7 = (s32[2]{0:T(128)S(1)}, s32[2]{0:T(128)}, u32[]{:S(2)}) copy-start(s32[2]{0:T(128)} %atom_ids.1) | copy-start | bytes 28
  85.3 2.8 %copy-start = (bf16[2,2048,768]{1,2,0:T(8,128)(2,1)S(1)}, bf16[2,2048,768]{1,2,0:T(8,128)(2,1)}, u32[]{:S(2)}) copy-start(bf16[2,2048,768]{1,2,0:T(8,128)(2,1)} %copy.24) | copy-start | bytes 18874372
  88.1 1.2 copy-start.2
  99.7 12.0 %all-to-all-start.1 = ((f32[32,6,128]{2,1,0:T(8,128)}), f32[32,6,128]{2,1,0:T(8,128)S(1)}, u32[]{:S(2)}, u32[]{:S(2)}) async-start(f32[32,6,128]{2,1,0:T(8,128)} %get-tuple-element.4), calls=%async_computation.1 | async-start | bytes 262144 | tf_op jit(solution)/shard_map/all_to_all | solution.py:316
  111.7 1.0 copy-start.5
  123.8 2.8 %copy-start.1 = (bf16[2,2048,768]{1,2,0:T(8,128)(2,1)S(1)}, bf16[2,2048,768]{1,2,0:T(8,128)(2,1)}, u32[]{:S(2)}) copy-start(bf16[2,2048,768]{1,2,0:T(8,128)(2,1)} %copy.24) | copy-start | bytes 18874372
  126.6 1.2 copy-start.3
  144.0 74.2 %all-to-all-start.3 = ((bf16[32,3,128,128]{3,2,1,0:T(8,128)(2,1)}), bf16[32,3,128,128]{3,2,1,0:T(8,128)(2,1)S(1)}, u32[]{:S(2)}, u32[]{:S(2)}) async-start(bf16[32,3,128,128]{3,2,1,0:T(8,128)(2,1)} %bitcast.3), calls=%async_computation.3 | async-start | bytes 6291456 | tf_op jit(solution)/shard_map/all_to_all | solution.py:316

commit v2 on v1

v2 whole, which is shorter than its diff:
```python
import jax
import jax.numpy as jnp
from jax import lax
from jax.experimental import pallas as pl
from jax.experimental.pallas import tpu as pltpu
from jax.sharding import PartitionSpec as P

LDEG = 7
ATOM_COL = 2
AXES = ("row", "col")
F32 = jnp.float32
BF16 = jnp.bfloat16
NT = (((1,), (1,)), ((), ()))


def degrees(harm_ids):
    bounds = jnp.arange(1, LDEG) ** 2
    return jnp.sum((harm_ids[:, None] >= bounds[None, :]).astype(jnp.int32), axis=1)


SMEM = pl.BlockSpec(memory_space=pltpu.SMEM)
VMEM = pl.BlockSpec(memory_space=pltpu.VMEM)
HBM = pl.BlockSpec(memory_space=pltpu.HBM)


def params(mib):
    return pltpu.CompilerParams(vmem_limit_bytes=int(mib * 1024 * 1024))


def split2(values):
    high = values.astype(BF16)
    low = (values - high.astype(F32)).astype(BF16)
    return jnp.concatenate([high, low], axis=0)


def join2(stacked):
    rows = stacked.shape[0] // 2
    return stacked[:rows] + stacked[rows:]


def column_copies(source, held, sems, chunk):
    batches, _, points = source.shape
    pieces = points // chunk
    return [
        [
            pltpu.make_async_copy(
                source.at[b, :, pl.ds(c * chunk, chunk)],
                held.at[b, :, pl.ds(c * chunk, chunk)],
                sems.at[b * pieces + c],
            )
            for c in range(pieces)
        ]
        for b in range(batches)
    ]


def gather_tiles(tile_ids, tiles):
    capacity, devices = tile_ids.shape
    count = capacity * devices

    def body(ids, tiles_ref, out_ref, keep, sems):
        load = pltpu.make_async_copy(tiles_ref, keep, sems.at[0])
        load.start()
        load.wait()

        def send(dev, carry):
            for k in range(capacity):
                pltpu.make_async_copy(
                    keep.at[ids[k, dev]], out_ref.at[dev * capacity + k], sems.at[1]
                ).start()
            return carry

        lax.fori_loop(0, devices, send, 0, unroll=4)
        pltpu.make_async_copy(out_ref, out_ref, sems.at[1]).wait()

    return pl.pallas_call(
        body,
        out_shape=jax.ShapeDtypeStruct((count,) + tiles.shape[1:], tiles.dtype),
        in_specs=[SMEM, HBM],
        out_specs=HBM,
        scratch_shapes=[pltpu.VMEM(tiles.shape, tiles.dtype), pltpu.SemaphoreType.DMA((2,))],
        compiler_params=params(63),
        name="gather_tiles",
    )(tile_ids, tiles)


def sum_tiles(tile_ids, arrived, tiles_dev):
    capacity, devices = tile_ids.shape
    _, blk, _ = arrived.shape

    def body(ids, arrived_ref, out_ref):
        out_ref[...] = jnp.zeros_like(out_ref)

        def add(dev, carry):
            for k in range(capacity):
                tile = ids[k, dev]
                out_ref[tile] = out_ref[tile] + arrived_ref[dev * capacity + k].astype(F32)
            return carry

        lax.fori_loop(0, devices, add, 0, unroll=4)

    return pl.pallas_call(
        body,
        out_shape=jax.ShapeDtypeStruct((tiles_dev, blk, blk), F32),
        in_specs=[SMEM, VMEM],
        out_specs=VMEM,
        compiler_params=params(16),
        name="sum_tiles",
    )(tile_ids, arrived)


def density_pass(active, slots, atoms, received, basis_t, harmonics, weights, shells, share, devices):
    batches, span, points = basis_t.shape
    slot_count, blk, _ = received.shape
    blocks = span // blk
    rows = harmonics.shape[1]
    held, radial = share
    chunk = points
    pieces = points // chunk
    lines = (held + 1) * batches

    def body(act, slot_ids, atom_ids, recv, phi_hbm, harm_hbm, wts, shell, rho_out, send,
             phi, harm, matrix, mom_keep, sems, harm_sem):
        copies = column_copies(phi_hbm, phi, sems, chunk)
        harm_copy = pltpu.make_async_copy(harm_hbm, harm, harm_sem)
        for b in range(batches):
            for copy in copies[b]:
                copy.start()
            if b == 0:
                harm_copy.start()

        for b in range(batches):
            count = act[b]
            for i in range(blocks):
                for j in range(blocks):
                    spot = (b, pl.ds(i * blk, blk), pl.ds(j * blk, blk))
                    live = (i < count) & (j < count)

                    @pl.when(live)
                    def _(b=b, i=i, j=j, spot=spot):
                        slot = jnp.clip(slot_ids[b, i * blocks + j], 0, slot_count - 1)
                        matrix[spot] = recv[slot]

                    @pl.when(jnp.logical_not(live))
                    def _(spot=spot):
                        matrix[spot] = jnp.zeros((blk, blk), BF16)

        for b in range(batches):
            send[:, pl.ds(held * batches + b, 1), :] = jnp.full(
                (devices, 1, radial), atom_ids[b].astype(F32), F32
            )

        def moments(b):
            weighted = harm[b] * (wts[b] * rho_out[b])
            ids = lax.broadcasted_iota(jnp.int32, (radial, points), 0)
            onehot = jnp.where(shell[b] == ids, 1.0, 0.0).astype(BF16)
            mom_keep[b] = join2(
                lax.dot_general(split2(weighted), onehot, NT, preferred_element_type=F32)
            )
            for k in range(held):
                for d in range(devices):
                    line = d * held + k
                    if line < rows:
                        send[d, pl.ds(k * batches + b, 1), :] = mom_keep[b, pl.ds(line, 1), :]
                    else:
                        send[d, pl.ds(k * batches + b, 1), :] = jnp.zeros((1, radial), F32)

        for b in range(batches):
            for c in range(pieces):
                copies[b][c].wait()
                cols = pl.ds(c * chunk, chunk)
                phi_c = phi[b, :, cols]
                product = jnp.dot(matrix[b], phi_c, preferred_element_type=F32)
                rho_out[b, :, cols] = jnp.sum(
                    product * phi_c.astype(F32), axis=0, keepdims=True
                )
            if b == 0:
                harm_copy.wait()

        for b in range(batches):
            moments(b)

    return pl.pallas_call(
        body,
        out_shape=(
            jax.ShapeDtypeStruct((batches, 1, points), F32),
            jax.ShapeDtypeStruct((devices, lines, radial), F32),
        ),
        in_specs=[SMEM, SMEM, SMEM, VMEM, HBM, HBM, VMEM, VMEM],
        out_specs=(VMEM, VMEM),
        scratch_shapes=[
            pltpu.VMEM(basis_t.shape, BF16),
            pltpu.VMEM(harmonics.shape, F32),
            pltpu.VMEM((batches, span, span), BF16),
            pltpu.VMEM((batches, rows, radial), F32),
            pltpu.SemaphoreType.DMA((batches * pieces,)),
            pltpu.SemaphoreType.DMA,
        ],
        compiler_params=params(54 - received.size * 2 / 2**20),
        name="density_pass",
    )(active, slots, atoms, received, basis_t, harmonics, weights, shells)


def radial_solve(degree_ids, arrived, green, natoms, held, batches, cols_count):
    devices, lines, radial = arrived.shape
    rows_out = (batches + ATOM_COL) * held

    def body(deg, got, green_hbm, out, flat, green, sems):
        loads = [
            pltpu.make_async_copy(green_hbm.at[deg[k]], green.at[k], sems.at[k])
            for k in range(held)
        ]
        for load in loads:
            load.start()
        for r in range(lines):
            for d in range(devices):
                flat[r, pl.ds(d, 1), :] = got[d, pl.ds(r, 1), :]
        atom_of = [flat[held * batches + b] for b in range(batches)]
        for k in range(held):
            sums = []
            for a in range(natoms):
                total = jnp.zeros((devices, radial), F32)
                for b in range(batches):
                    total = total + jnp.where(atom_of[b] == float(a), flat[k * batches + b], 0.0)
                sums.append(jnp.sum(total, axis=0, keepdims=True))
            atom_mom = jnp.concatenate(sums, axis=0)
            loads[k].wait()
            solved = lax.dot_general(
                atom_mom,
                green[k],
                NT,
                precision=lax.Precision.HIGHEST,
                preferred_element_type=F32,
            )
            for b in range(batches):
                picked = jnp.zeros((devices, radial), F32)
                for a in range(natoms):
                    picked = jnp.where(atom_of[b] == float(a), solved[a : a + 1, :], picked)
                for d in range(devices):
                    out[d, pl.ds(b * held + k, 1), :] = picked[d : d + 1, :]
            for own in range(ATOM_COL):
                for d in range(devices):
                    a = (d % cols_count) * ATOM_COL + own
                    out[d, pl.ds((batches + own) * held + k, 1), :] = solved[a : a + 1, :]

    return pl.pallas_call(
        body,
        out_shape=jax.ShapeDtypeStruct((devices, rows_out, radial), F32),
        in_specs=[SMEM, VMEM, HBM],
        out_specs=VMEM,
        scratch_shapes=[
            pltpu.VMEM((lines, devices, radial), F32),
            pltpu.VMEM((held, radial, radial), F32),
            pltpu.SemaphoreType.DMA((held,)),
        ],
        compiler_params=params(53.5),
        name="radial_solve",
    )(degree_ids, arrived, green)


def potential_pass(active, slots, poles, rho, basis_t, harmonics, weights, shells, slot_count, blk, held):
    batches, span, points = basis_t.shape
    blocks = span // blk
    rows = harmonics.shape[1]
    devices, lines, radial = poles.shape
    chunk = points
    pieces = points // chunk
    wide = 2 * blk if blocks % 2 == 0 else blk

    def body(act, slot_ids, got, rho_ref, phi_hbm, harm_hbm, wts, shell, out,
             phi, harm, scaled, poles_keep, sems, harm_sem):
        copies = column_copies(phi_hbm, phi, sems, chunk)
        harm_copy = pltpu.make_async_copy(harm_hbm, harm, harm_sem)
        harm_copy.start()
        for b in range(batches):
            for copy in copies[b]:
                copy.start()

        out[...] = jnp.zeros_like(out)
        if held * devices < rows:
            poles_keep[...] = jnp.zeros_like(poles_keep)
        for b in range(batches):
            for k in range(held):
                for d in range(devices):
                    line = d * held + k
                    if line < rows:
                        poles_keep[b, pl.ds(line, 1), :] = got[d, pl.ds(b * held + k, 1), :]
        harm_copy.wait()

        for b in range(batches):
            stacked = split2(poles_keep[b])
            for c in range(pieces):
                copies[b][c].wait()
                cols = pl.ds(c * chunk, chunk)
                ids = lax.broadcasted_iota(jnp.int32, (radial, chunk), 0)
                onehot = jnp.where(shell[b, :, cols] == ids, 1.0, 0.0).astype(BF16)
                at_points = join2(jnp.dot(stacked, onehot, preferred_element_type=F32))
                hartree = jnp.sum(harm[b, :, cols] * at_points, axis=0, keepdims=True)
                rho_c = rho_ref[b, :, cols]
                root = jnp.exp(jnp.log(1.0 + rho_c * rho_c) * (-1.0 / 3.0))
                factor = wts[b, :, cols] * (hartree - rho_c * root)
                scaled[b, :, cols] = (phi[b, :, cols].astype(F32) * factor).astype(BF16)

        for b in range(batches):
            count = act[b]
            for first in range(0, span, wide):
                piece = lax.dot_general(
                    phi[b], scaled[b, pl.ds(first, wide), :], NT, preferred_element_type=F32
                )
                for i in range(blocks):
                    for j in range(first // blk, (first + wide) // blk):
                        live = (i < count) & (j < count)
                        slot = jnp.clip(slot_ids[b, i * blocks + j], 0, slot_count - 1)
                        left = j * blk - first
                        tile = piece[i * blk : (i + 1) * blk, left : left + blk].astype(BF16)
                        out[slot] = jnp.where(live, tile, out[slot])

    return pl.pallas_call(
        body,
        out_shape=jax.ShapeDtypeStruct((slot_count, blk, blk), BF16),
        in_specs=[SMEM, SMEM, VMEM, VMEM, HBM, HBM, VMEM, VMEM],
        out_specs=VMEM,
        scratch_shapes=[
            pltpu.VMEM(basis_t.shape, BF16),
            pltpu.VMEM(harmonics.shape, F32),
            pltpu.VMEM(basis_t.shape, BF16),
            pltpu.VMEM((batches, rows, radial), F32),
            pltpu.SemaphoreType.DMA((batches * pieces,)),
            pltpu.SemaphoreType.DMA,
        ],
        compiler_params=params(62),
        name="potential_pass",
    )(active, slots, poles, rho, basis_t, harmonics, weights, shells)


def exchange(parts):
    return lax.all_to_all(parts, AXES, split_axis=0, concat_axis=0, tiled=True)


def shards(
    density_tiles,
    send_list,
    basis_values,
    active_blocks,
    touch_slots,
    point_weights,
    harmonics,
    shell_index,
    batch_atom,
    radial_green,
):
    devices = lax.axis_size(AXES)
    cols_count = lax.axis_size("col")
    capacity = send_list.shape[2]
    tiles_dev, blk, _ = density_tiles.shape
    batches, points, span = basis_values.shape
    harm_count = harmonics.shape[1]
    radial = radial_green.shape[1]
    slot_count = devices * capacity
    natoms = ATOM_COL * cols_count
    held = -(-harm_count // devices)
    rows = -(-harm_count // 16) * 16

    tile_ids = jnp.transpose(send_list, (2, 0, 1)).reshape(capacity, devices)
    outgoing = gather_tiles(tile_ids, density_tiles)
    arrived = exchange(outgoing.reshape(devices, capacity, blk, blk))
    received = arrived.reshape(slot_count, blk, blk)

    basis_t = jnp.transpose(basis_values, (0, 2, 1))
    harm_rows = jnp.pad(harmonics, ((0, 0), (0, rows - harm_count), (0, 0)))
    weights = point_weights[:, None, :]
    shells = shell_index[:, None, :]
    slots = touch_slots.reshape(batches, -1)

    rho, mom_out = density_pass(
        active_blocks, slots, batch_atom, received, basis_t, harm_rows, weights, shells,
        (held, radial), devices,
    )
    mom_in = exchange(mom_out)
    first = lax.axis_index(AXES) * held
    degree_ids = degrees(jnp.minimum(first + jnp.arange(held), harm_count - 1))
    poles_out = radial_solve(
        degree_ids, mom_in, radial_green, natoms, held, batches, cols_count
    )
    poles = exchange(poles_out)
    returning = potential_pass(
        active_blocks, slots, poles, rho, basis_t, harm_rows, weights, shells,
        slot_count, blk, held,
    )
    back = exchange(returning.reshape(devices, capacity, blk, blk))
    ham_tiles = sum_tiles(tile_ids, back.reshape(slot_count, blk, blk), tiles_dev)

    own = poles[:, batches * held :, :].reshape(devices, ATOM_COL, held, radial)
    own = jnp.transpose(own, (1, 0, 2, 3)).reshape(ATOM_COL, devices * held, radial)
    return (ham_tiles, own[:, :harm_count])


def solution(mesh):
    in_specs = (
        P(AXES, None, None),
        P(AXES, None, None),
        P(AXES, None, None),
        P(AXES),
        P(AXES, None, None),
        P(AXES, None),
        P(AXES, None, None),
        P(AXES, None),
        P(AXES),
        P(),
    )
    out_specs = (P(AXES, None, None), P("col", None, None))
    return jax.shard_map(shards, mesh=mesh, in_specs=in_specs, out_specs=out_specs, check_vma=False)
```

time: 222 us -> 209 us (0.941)
  local copies, waits for them, and re-layouts: 25.4 us -> 12 us
  waiting for transfers between devices: 136 us -> 141 us
  Pallas kernels: 34.4 us -> 29.9 us
    unnamed x26 -> x30, local copies, waits for them, and re-layouts: 22.3 us -> 11.1 us
    pallas_call x1, Pallas kernels: 16.1 us -> 11.3 us  [potential_pass(): pl.pallas_call(body, out_shape=jax.ShapeDtypeStruct((slot_count, blk, blk...]
    all_to_all x3, waiting for transfers between devices: 136 us -> 141 us  [exchange(): return lax.all_to_all(parts, AXES, split_axis=0, concat_axis=0, tiled=True)]
  transfers between devices with their start and end apart: 3 -> 3, of which waited for: 3 -> 3; matrix products, arithmetic and copies ran while one was open for 7% -> 5% of each run, Pallas kernels for 0% -> 0%
where the time goes in v2:
time: 209 us
  waiting for transfers between devices  141 us (67%)
  Pallas kernels  29.9 us (14%)
  starting transfers between devices  14.4 us (7%)
  local copies, waits for them, and re-layouts  12 us (6%)
  blocking collectives  10.6 us (5%)
    all_to_all x3, waiting for transfers between devices, exchange(): return lax.all_to_all(parts, AXES, split_axis=0, concat_axis=0, tiled=True)  141 us
    all_to_all x3, starting transfers between devices, exchange(): return lax.all_to_all(parts, AXES, split_axis=0, concat_axis=0, tiled=True)  14.4 us
    pallas_call x1, Pallas kernels, potential_pass(): pl.pallas_call(body, out_shape=jax.ShapeDtypeStruct((slot_count, blk, blk...  11.3 us
    unnamed x30, local copies, waits for them, and re-layouts  11.1 us
    all_to_all x1, blocking collectives, exchange(): return lax.all_to_all(parts, AXES, split_axis=0, concat_axis=0, tiled=True)  10.6 us
    pallas_call x1, Pallas kernels, density_pass(): pl.pallas_call(body, out_shape=(jax.ShapeDtypeStruct((batches, 1, points)...  10.1 us
  transfers between devices with their start and end apart: 3, of which 3 were waited for; matrix products, arithmetic and copies ran while one was open for 5% of the time, Pallas kernels for 0%

profile of v2, /device:TPU:0, one launch (start us, length us, event | category | flops | bytes accessed | tf_op | source)
XLA Modules:
  0.0 208.5 jit_solution(2846348335321794827)
XLA Ops:
  0.6 1.3 copy.26
  1.9 3.6 %gather_tiles.1 = bf16[96,128,128]{2,1,0:T(8,128)(2,1)} custom-call(s32[3,32]{1,0:T(4,128)} %bitcast.14, bf16[32,128,128]{2,1,0:T(8,128)(2,1)} %tiles_ref.1), custom_call_target="tpu_custom_call" | custom-call | tf_op jit(solution)/shard_map/gather_tiles/pallas_call | solution.py:76
  5.5 0.0 copy-start.12
  5.5 0.0 copy-start.10
  5.5 0.0 copy-start.11
  5.5 0.0 copy-start.9
  5.5 7.4 %all-to-all-start = ((bf16[32,3,128,128]{3,2,1,0:T(8,128)(2,1)}), bf16[32,3,128,128]{3,2,1,0:T(8,128)(2,1)}, u32[]{:S(2)}, u32[]{:S(2)}) async-start(bf16[32,3,128,128]{3,2,1,0:T(8,128)(2,1)} %bitcast.18), calls=%async_computation | async-start | bytes 6291456 | tf_op jit(solution)/shard_map/all_to_all | solution.py:337
  13.0 0.0 copy-done.12
  13.0 0.1 reshape.39.slot_ids
  13.1 0.0 copy-done.10
  13.2 0.0 copy-done.9
  13.2 0.0 copy-start.2
  13.2 0.5 copy.22
  13.7 0.0 copy-start.6
  13.7 0.0 copy-start.7
  13.7 8.7 %copy.21 = bf16[2,2048,768]{1,2,0:T(8,128)(2,1)} copy(bf16[2,2048,768]{2,1,0:T(8,128)(2,1)} %param.12) | data formatting | bytes 12582912 | tf_op args[2]
  22.4 0.1 pad.4.harm_hbm
  22.5 0.0 copy-start
  22.5 61.8 %all-to-all-done = bf16[32,3,128,128]{3,2,1,0:T(8,128)(2,1)} async-done(((bf16[32,3,128,128]{3,2,1,0:T(8,128)(2,1)}), bf16[32,3,128,128]{3,2,1,0:T(8,128)(2,1)}, u32[]{:S(2)}, u32[]{:S(2)}) %all-to-all-start) | async-done | bytes 3145760 | tf_op jit(solution)/shard_map/all_to_all | solution.py:337
  84.3 10.1 %density_pass.1 = (f32[2,1,2048]{2,1,0:T(1,128)S(1)}, f32[32,6,128]{2,1,0:T(8,128)}) custom-call(s32[2]{0:T(128)S(1)} %copy-done.6, s32[2,36]{1,0:T(2,128)S(1)} %reshape.39.slot_ids, s32[2]{0:T(128)S(1)} %copy-done.7, bf16[96,128,128]{2,1,0:T(8,128)(2,1)} %bitcast.2.recv, bf16[2,768,2048]{2,1,0:T(8,128)(2,1)} %bitcast.16, f32[2,64,2048]{2,1,0:T(8,128)S(1)} %pad.4.harm_hbm, ...), custom_call_target="tpu_custom_call" | custom-call | tf_op jit(solution)/shard_map/density_pass/pallas_call | solution.py:183
  94.5 0.0 copy-start.4
  94.5 0.6 copy-done.4
  95.1 4.0 %all-to-all-start.1 = ((f32[32,6,128]{2,1,0:T(8,128)}), f32[32,6,128]{2,1,0:T(8,128)S(1)}, u32[]{:S(2)}, u32[]{:S(2)}) async-start(f32[32,6,128]{2,1,0:T(8,128)} %get-tuple-element.4), calls=%async_computation.1 | async-start | bytes 262144 | tf_op jit(solution)/shard_map/all_to_all | solution.py:337
  99.1 0.2 fusion.deg
  99.3 8.0 %all-to-all-done.1.got = f32[32,6,128]{2,1,0:T(8,128)S(1)} async-done(((f32[32,6,128]{2,1,0:T(8,128)}), f32[32,6,128]{2,1,0:T(8,128)S(1)}, u32[]{:S(2)}, u32[]{:S(2)}) %all-to-all-start.1) | async-done | bytes 98336 | tf_op jit(solution)/shard_map/all_to_all | solution.py:337
  107.3 2.2 %radial_solve.1 = f32[32,8,128]{2,1,0:T(8,128)S(1)} custom-call(s32[2]{0:T(128)S(1)} %fusion.deg, f32[32,6,128]{2,1,0:T(8,128)S(1)} %all-to-all-done.1.got, f32[7,128,128]{2,1,0:T(8,128)} %green_hbm.1), custom_call_target="tpu_custom_call" | custom-call | tf_op jit(solution)/shard_map/radial_solve/pallas_call | solution.py:246
  109.5 10.6 %all_to_all.20.got = f32[32,8,128]{2,1,0:T(8,128)} all-to-all(f32[32,8,128]{2,1,0:T(8,128)S(1)} %radial_solve.1), channel_id=1, replica_groups=mesh['row'=4,'col'=8] {'row','col'}, dimensions={0} | all-to-all | bytes 262144 | tf_op jit(solution)/shard_map/all_to_all | solution.py:337
  120.1 11.3 %potential_pass.1 = bf16[96,128,128]{2,1,0:T(8,128)(2,1)} custom-call(s32[2]{0:T(128)} %act.3, s32[2,36]{1,0:T(2,128)} %copy-done.5, f32[32,8,128]{2,1,0:T(8,128)} %all_to_all.20.got, f32[2,1,2048]{2,1,0:T(1,128)} %copy-done.4, bf16[2,768,2048]{2,1,0:T(8,128)(2,1)} %bitcast.17, f32[2,64,2048]{2,1,0:T(8,128)} %copy-done, f32[2,1,2048]{2,1,0:T(1,128)} %copy-done.1, ...), custom_call_target="tpu_custom_call" | custom-call | tf_op jit(solution)/shard_map/potential_pass/pallas_call | solution.py:318
  131.4 2.9 %all-to-all-start.3 = ((bf16[32,3,128,128]{3,2,1,0:T(8,128)(2,1)}), bf16[32,3,128,128]{3,2,1,0:T(8,128)(2,1)S(1)}, u32[]{:S(2)}, u32[]{:S(2)}) async-start(bf16[32,3,128,128]{3,2,1,0:T(8,128)(2,1)} %bitcast.19), calls=%async_computation.3 | async-start | bytes 6291456 | tf_op jit(solution)/shard_map/all_to_all | solution.py:337
  134.4 0.6 slice.9
  135.0 70.7 %all-to-all-done.3 = bf16[32,3,128,128]{3,2,1,0:T(8,128)(2,1)S(1)} async-done(((bf16[32,3,128,128]{3,2,1,0:T(8,128)(2,1)}), bf16[32,3,128,128]{3,2,1,0:T(8,128)(2,1)S(1)}, u32[]{:S(2)}, u32[]{:S(2)}) %all-to-all-start.3) | async-done | bytes 3145760 | tf_op jit(solution)/shard_map/all_to_all | solution.py:337
  205.8 2.8 %sum_tiles.1 = f32[32,128,128]{2,1,0:T(8,128)} custom-call(s32[3,32]{1,0:T(4,128)S(1)} %bitcast.15, bf16[96,128,128]{2,1,0:T(8,128)(2,1)S(1)} %bitcast.13), custom_call_target="tpu_custom_call" | custom-call | tf_op jit(solution)/shard_map/sum_tiles/pallas_call | solution.py:102
  (20 shorter events, 0.1 us)
Async XLA Ops:
  5.5 7.5 %copy-start.12 = (s32[2,6,6]{2,0,1:T(2,128)S(1)}, s32[2,6,6]{2,0,1:T(2,128)}, u32[]{:S(2)}) copy-start(s32[2,6,6]{2,0,1:T(2,128)} %param.14) | copy-start | bytes 868
  5.5 7.6 %copy-start.10 = (f32[2,2048]{1,0:T(2,128)S(1)}, f32[2,2048]{1,0:T(2,128)}, u32[]{:S(2)}) copy-start(f32[2,2048]{1,0:T(2,128)} %param.15) | copy-start | bytes 49156
  5.5 7.6 %copy-start.11 = (s32[2,2048]{1,0:T(2,128)S(1)}, s32[2,2048]{1,0:T(2,128)}, u32[]{:S(2)}) copy-start(s32[2,2048]{1,0:T(2,128)} %param.17) | copy-start | bytes 49156
  5.5 7.6 %copy-start.9 = (f32[2,49,2048]{2,0,1:T(2,128)S(1)}, f32[2,49,2048]{2,0,1:T(2,128)}, u32[]{:S(2)}) copy-start(f32[2,49,2048]{2,0,1:T(2,128)} %param.16) | copy-start | bytes 2408452
  5.5 78.8 %all-to-all-start = ((bf16[32,3,128,128]{3,2,1,0:T(8,128)(2,1)}), bf16[32,3,128,128]{3,2,1,0:T(8,128)(2,1)}, u32[]{:S(2)}, u32[]{:S(2)}) async-start(bf16[32,3,128,128]{3,2,1,0:T(8,128)(2,1)} %bitcast.18), calls=%async_computation | async-start | bytes 6291456 | tf_op jit(solution)/shard_map/all_to_all | solution.py:337
  13.1 71.2 %copy-start.5 = (s32[2,36]{1,0:T(2,128)}, s32[2,36]{1,0:T(2,128)S(1)}, u32[]{:S(2)}) copy-start(s32[2,36]{1,0:T(2,128)S(1)} %reshape.39.slot_ids) | copy-start | bytes 868
  13.1 71.2 %copy-start.1 = (f32[2,1,2048]{2,1,0:T(1,128)}, f32[2,1,2048]{2,1,0:T(1,128)S(1)}, u32[]{:S(2)}) copy-start(f32[2,1,2048]{2,1,0:T(1,128)S(1)} %broadcast_in_dim.8.wts) | copy-start | bytes 49156
  13.2 71.2 %copy-start.2 = (s32[2,1,2048]{2,1,0:T(1,128)}, s32[2,1,2048]{2,1,0:T(1,128)S(1)}, u32[]{:S(2)}) copy-start(s32[2,1,2048]{2,1,0:T(1,128)S(1)} %broadcast_in_dim.9.shell) | copy-start | bytes 49156
  13.7 70.7 %copy-start.6 = (s32[2]{0:T(128)S(1)}, s32[2]{0:T(128)}, u32[]{:S(2)}) copy-start(s32[2]{0:T(128)} %act.3) | copy-start | bytes 28
  13.7 70.7 %copy-start.7 = (s32[2]{0:T(128)S(1)}, s32[2]{0:T(128)}, u32[]{:S(2)}) copy-start(s32[2]{0:T(128)} %atom_ids.1) | copy-start | bytes 28
  22.5 72.0 %copy-start = (f32[2,64,2048]{2,1,0:T(8,128)}, f32[2,64,2048]{2,1,0:T(8,128)S(1)}, u32[]{:S(2)}) copy-start(f32[2,64,2048]{2,1,0:T(8,128)S(1)} %pad.4.harm_hbm) | copy-start | bytes 3145732
  94.5 0.6 copy-start.4
  95.1 12.2 %all-to-all-start.1 = ((f32[32,6,128]{2,1,0:T(8,128)}), f32[32,6,128]{2,1,0:T(8,128)S(1)}, u32[]{:S(2)}, u32[]{:S(2)}) async-start(f32[32,6,128]{2,1,0:T(8,128)} %get-tuple-element.4), calls=%async_computation.1 | async-start | bytes 262144 | tf_op jit(solution)/shard_map/all_to_all | solution.py:337
  131.4 3.0 %copy-start.8 = (f32[32,8,128]{2,1,0:T(8,128)S(1)}, f32[32,8,128]{2,1,0:T(8,128)}, u32[]{:S(2)}) copy-start(f32[32,8,128]{2,1,0:T(8,128)} %all_to_all.20.got) | copy-start | bytes 393220
  131.4 74.4 %copy-start.3 = (s32[3,1,32]{2,0,1:T(4,128)S(1)}, s32[3,1,32]{2,0,1:T(4,128)}, u32[]{:S(2)}) copy-start(s32[3,1,32]{2,0,1:T(4,128)} %copy.26) | copy-start | bytes 1156
  131.4 74.4 %all-to-all-start.3 = ((bf16[32,3,128,128]{3,2,1,0:T(8,128)(2,1)}), bf16[32,3,128,128]{3,2,1,0:T(8,128)(2,1)S(1)}, u32[]{:S(2)}, u32[]{:S(2)}) async-start(bf16[32,3,128,128]{3,2,1,0:T(8,128)(2,1)} %bitcast.19), calls=%async_computation.3 | async-start | bytes 6291456 | tf_op jit(solution)/shard_map/all_to_all | solution.py:337

commit v3 on v2

--- a/solution.py
+++ b/solution.py
@@ -11,6 +11,7 @@
 F32 = jnp.float32
 BF16 = jnp.bfloat16
 NT = (((1,), (1,)), ((), ()))
+SPARE = 256
 
 
 def degrees(harm_ids):
@@ -38,24 +39,15 @@
     return stacked[:rows] + stacked[rows:]
 
 
-def column_copies(source, held, sems, chunk):
-    batches, _, points = source.shape
-    pieces = points // chunk
+def loads_of(source, held, sems):
     return [
-        [
-            pltpu.make_async_copy(
-                source.at[b, :, pl.ds(c * chunk, chunk)],
-                held.at[b, :, pl.ds(c * chunk, chunk)],
-                sems.at[b * pieces + c],
-            )
-            for c in range(pieces)
-        ]
-        for b in range(batches)
+        pltpu.make_async_copy(source.at[b], held.at[b], sems.at[b])
+        for b in range(sems.shape[0])
     ]
 
 
 def gather_tiles(tile_ids, tiles):
-    capacity, devices = tile_ids.shape
+    capacity, _, devices = tile_ids.shape
     count = capacity * devices
 
     def body(ids, tiles_ref, out_ref, keep, sems):
@@ -66,7 +58,7 @@
         def send(dev, carry):
             for k in range(capacity):
                 pltpu.make_async_copy(
-                    keep.at[ids[k, dev]], out_ref.at[dev * capacity + k], sems.at[1]
+                    keep.at[ids[k, 0, dev]], out_ref.at[dev * capacity + k], sems.at[1]
                 ).start()
             return carry
 
@@ -85,7 +77,7 @@
 
 
 def sum_tiles(tile_ids, arrived, tiles_dev):
-    capacity, devices = tile_ids.shape
+    capacity, _, devices = tile_ids.shape
     _, blk, _ = arrived.shape
 
     def body(ids, arrived_ref, out_ref):
@@ -93,7 +85,7 @@
 
         def add(dev, carry):
             for k in range(capacity):
-                tile = ids[k, dev]
+                tile = ids[k, 0, dev]
                 out_ref[tile] = out_ref[tile] + arrived_ref[dev * capacity + k].astype(F32)
             return carry
 
@@ -115,19 +107,15 @@
     blocks = span // blk
     rows = harmonics.shape[1]
     held, radial = share
-    chunk = points
-    pieces = points // chunk
     lines = (held + 1) * batches
 
-    def body(act, slot_ids, atom_ids, recv, phi_hbm, harm_hbm, wts, shell, rho_out, send,
-             phi, harm, matrix, mom_keep, sems, harm_sem):
-        copies = column_copies(phi_hbm, phi, sems, chunk)
-        harm_copy = pltpu.make_async_copy(harm_hbm, harm, harm_sem)
-        for b in range(batches):
-            for copy in copies[b]:
-                copy.start()
-            if b == 0:
-                harm_copy.start()
+    def body(act, slot_ids, atom_ids, recv, phi_hbm, harm_hbm, wts, shell, rho_hbm, send,
+             phi, harm, rho, matrix, mom_keep, phi_sems, harm_sems, rho_sems):
+        phi_loads = loads_of(phi_hbm, phi, phi_sems)
+        harm_loads = loads_of(harm_hbm, harm, harm_sems)
+        rho_stores = loads_of(rho, rho_hbm, rho_sems)
+        for load in phi_loads + harm_loads:
+            load.start()
 
         for b in range(batches):
             count = act[b]
@@ -151,7 +139,7 @@
             )
 
         def moments(b):
-            weighted = harm[b] * (wts[b] * rho_out[b])
+            weighted = harm[b] * (wts[b] * rho[b])
             ids = lax.broadcasted_iota(jnp.int32, (radial, points), 0)
             onehot = jnp.where(shell[b] == ids, 1.0, 0.0).astype(BF16)
             mom_keep[b] = join2(
@@ -166,37 +154,36 @@
                         send[d, pl.ds(k * batches + b, 1), :] = jnp.zeros((1, radial), F32)
 
         for b in range(batches):
-            for c in range(pieces):
-                copies[b][c].wait()
-                cols = pl.ds(c * chunk, chunk)
-                phi_c = phi[b, :, cols]
-                product = jnp.dot(matrix[b], phi_c, preferred_element_type=F32)
-                rho_out[b, :, cols] = jnp.sum(
-                    product * phi_c.astype(F32), axis=0, keepdims=True
-                )
-            if b == 0:
-                harm_copy.wait()
-
-        for b in range(batches):
+            phi_loads[b].wait()
+            product = jnp.dot(matrix[b], phi[b], preferred_element_type=F32)
+            rho[b] = jnp.sum(product * phi[b].astype(F32), axis=0, keepdims=True)
+            rho_stores[b].start()
+
+        for b in range(batches):
+            harm_loads[b].wait()
             moments(b)
+        for store in rho_stores:
+            store.wait()
 
     return pl.pallas_call(
         body,
         out_shape=(
-            jax.ShapeDtypeStruct((batches, 1, points), F32),
+            jax.ShapeDtypeStruct((SPARE * batches, 1, points), F32),
             jax.ShapeDtypeStruct((devices, lines, radial), F32),
         ),
         in_specs=[SMEM, SMEM, SMEM, VMEM, HBM, HBM, VMEM, VMEM],
-        out_specs=(VMEM, VMEM),
+        out_specs=(HBM, VMEM),
         scratch_shapes=[
             pltpu.VMEM(basis_t.shape, BF16),
-            pltpu.VMEM(harmonics.shape, F32),
+            pltpu.VMEM((batches, rows, points), F32),
+            pltpu.VMEM((batches, 1, points), F32),
             pltpu.VMEM((batches, span, span), BF16),
             pltpu.VMEM((batches, rows, radial), F32),
-            pltpu.SemaphoreType.DMA((batches * pieces,)),
-            pltpu.SemaphoreType.DMA,
+            pltpu.SemaphoreType.DMA((batches,)),
+            pltpu.SemaphoreType.DMA((batches,)),
+            pltpu.SemaphoreType.DMA((batches,)),
         ],
-        compiler_params=params(54 - received.size * 2 / 2**20),
+        compiler_params=params(52 - received.size * 2 / 2**20),
         name="density_pass",
     )(active, slots, atoms, received, basis_t, harmonics, weights, shells)
 
@@ -263,18 +250,15 @@
     blocks = span // blk
     rows = harmonics.shape[1]
     devices, lines, radial = poles.shape
-    chunk = points
-    pieces = points // chunk
     wide = 2 * blk if blocks % 2 == 0 else blk
 
-    def body(act, slot_ids, got, rho_ref, phi_hbm, harm_hbm, wts, shell, out,
-             phi, harm, scaled, poles_keep, sems, harm_sem):
-        copies = column_copies(phi_hbm, phi, sems, chunk)
-        harm_copy = pltpu.make_async_copy(harm_hbm, harm, harm_sem)
-        harm_copy.start()
-        for b in range(batches):
-            for copy in copies[b]:
-                copy.start()
+    def body(act, slot_ids, got, rho_hbm, phi_hbm, harm_hbm, wts, shell, out,
+             phi, harm, rho, scaled, poles_keep, phi_sems, harm_sems, rho_sems):
+        phi_loads = loads_of(phi_hbm, phi, phi_sems)
+        harm_loads = loads_of(harm_hbm, harm, harm_sems)
+        rho_loads = loads_of(rho_hbm, rho, rho_sems)
+        for load in rho_loads + harm_loads + phi_loads:
+            load.start()
 
         out[...] = jnp.zeros_like(out)
         if held * devices < rows:
@@ -285,21 +269,23 @@
                     line = d * held + k
                     if line < rows:
                         poles_keep[b, pl.ds(line, 1), :] = got[d, pl.ds(b * held + k, 1), :]
-        harm_copy.wait()
-
-        for b in range(batches):
-            stacked = split2(poles_keep[b])
-            for c in range(pieces):
-                copies[b][c].wait()
-                cols = pl.ds(c * chunk, chunk)
-                ids = lax.broadcasted_iota(jnp.int32, (radial, chunk), 0)
-                onehot = jnp.where(shell[b, :, cols] == ids, 1.0, 0.0).astype(BF16)
-                at_points = join2(jnp.dot(stacked, onehot, preferred_element_type=F32))
-                hartree = jnp.sum(harm[b, :, cols] * at_points, axis=0, keepdims=True)
-                rho_c = rho_ref[b, :, cols]
-                root = jnp.exp(jnp.log(1.0 + rho_c * rho_c) * (-1.0 / 3.0))
-                factor = wts[b, :, cols] * (hartree - rho_c * root)
-                scaled[b, :, cols] = (phi[b, :, cols].astype(F32) * factor).astype(BF16)
+
+        factors = []
+        for b in range(batches):
+            rho_loads[b].wait()
+            harm_loads[b].wait()
+            ids = lax.broadcasted_iota(jnp.int32, (radial, points), 0)
+            onehot = jnp.where(shell[b] == ids, 1.0, 0.0).astype(BF16)
+            at_points = join2(
+                jnp.dot(split2(poles_keep[b]), onehot, preferred_element_type=F32)
+            )
+            hartree = jnp.sum(harm[b] * at_points, axis=0, keepdims=True)
+            root = jnp.exp(jnp.log(1.0 + rho[b] * rho[b]) * (-1.0 / 3.0))
+            factors.append(wts[b] * (hartree - rho[b] * root))
+
+        for b in range(batches):
+            phi_loads[b].wait()
+            scaled[b] = (phi[b].astype(F32) * factors[b]).astype(BF16)
 
         for b in range(batches):
             count = act[b]
@@ -322,11 +308,13 @@
         out_specs=VMEM,
         scratch_shapes=[
             pltpu.VMEM(basis_t.shape, BF16),
-            pltpu.VMEM(harmonics.shape, F32),
+            pltpu.VMEM((batches, rows, points), F32),
+            pltpu.VMEM((batches, 1, points), F32),
             pltpu.VMEM(basis_t.shape, BF16),
             pltpu.VMEM((batches, rows, radial), F32),
-            pltpu.SemaphoreType.DMA((batches * pieces,)),
-            pltpu.SemaphoreType.DMA,
+            pltpu.SemaphoreType.DMA((batches,)),
+            pltpu.SemaphoreType.DMA((batches,)),
+            pltpu.SemaphoreType.DMA((batches,)),
         ],
         compiler_params=params(62),
         name="potential_pass",
@@ -361,13 +349,13 @@
     held = -(-harm_count // devices)
     rows = -(-harm_count // 16) * 16
 
-    tile_ids = jnp.transpose(send_list, (2, 0, 1)).reshape(capacity, devices)
+    tile_ids = jnp.transpose(send_list, (2, 0, 1))
     outgoing = gather_tiles(tile_ids, density_tiles)
     arrived = exchange(outgoing.reshape(devices, capacity, blk, blk))
     received = arrived.reshape(slot_count, blk, blk)
 
     basis_t = jnp.transpose(basis_values, (0, 2, 1))
-    harm_rows = jnp.pad(harmonics, ((0, 0), (0, rows - harm_count), (0, 0)))
+    harm_rows = jnp.pad(harmonics, ((0, 2 * batches), (0, rows - harm_count), (0, 0)))
     weights = point_weights[:, None, :]
     shells = shell_index[:, None, :]
     slots = touch_slots.reshape(batches, -1)

time: 209 us -> 207 us (level)
  waiting for transfers between devices: 141 us -> 135 us
  local copies, waits for them, and re-layouts: 12 us -> 15.5 us
    all_to_all x3, waiting for transfers between devices: 141 us -> 135 us  [exchange(): return lax.all_to_all(parts, AXES, split_axis=0, concat_axis=0, tiled=True)]
    pad x1, local copies, waits for them, and re-layouts: 0.09 us -> 3.32 us  [shards(): jnp.pad(harmonics, ((0, 2 * batches), (0, rows - harm_count), (0, 0)))]
    unnamed x30 -> x23, local copies, waits for them, and re-layouts: 11.1 us -> 11.4 us
  transfers between devices with their start and end apart: 3 -> 3, of which waited for: 3 -> 3; matrix products, arithmetic and copies ran while one was open for 5% -> 8% of each run, Pallas kernels for 0% -> 0%
where the time goes in v3:
time: 207 us
  waiting for transfers between devices  135 us (65%)
  Pallas kernels  30.2 us (15%)
  local copies, waits for them, and re-layouts  15.5 us (7%)
  starting transfers between devices  14.3 us (7%)
  blocking collectives  10.6 us (5%)
    all_to_all x3, waiting for transfers between devices, exchange(): return lax.all_to_all(parts, AXES, split_axis=0, concat_axis=0, tiled=True)  135 us
    all_to_all x3, starting transfers between devices, exchange(): return lax.all_to_all(parts, AXES, split_axis=0, concat_axis=0, tiled=True)  14.3 us
    pallas_call x1, Pallas kernels, potential_pass(): pl.pallas_call(body, out_shape=jax.ShapeDtypeStruct((slot_count, blk, blk...  12.3 us
    unnamed x23, local copies, waits for them, and re-layouts  11.4 us
    all_to_all x1, blocking collectives, exchange(): return lax.all_to_all(parts, AXES, split_axis=0, concat_axis=0, tiled=True)  10.6 us
    pallas_call x1, Pallas kernels, density_pass(): pl.pallas_call(body, out_shape=(jax.ShapeDtypeStruct((SPARE * batches, 1,...  9.28 us
  transfers between devices with their start and end apart: 3, of which 3 were waited for; matrix products, arithmetic and copies ran while one was open for 8% of the time, Pallas kernels for 0%

profile of v3, /device:TPU:0, one launch (start us, length us, event | category | flops | bytes accessed | tf_op | source)
XLA Modules:
  0.0 206.8 jit_solution(8854792935988687750)
XLA Ops:
  0.6 3.6 %gather_tiles.1 = bf16[96,128,128]{2,1,0:T(8,128)(2,1)} custom-call(s32[3,1,32]{2,1,0:T(1,128)} %bitcast.12, bf16[32,128,128]{2,1,0:T(8,128)(2,1)} %tiles_ref.1), custom_call_target="tpu_custom_call" | custom-call | tf_op jit(solution)/shard_map/gather_tiles/pallas_call | solution.py:68
  4.3 7.3 %all-to-all-start = ((bf16[32,3,128,128]{3,2,1,0:T(8,128)(2,1)}), bf16[32,3,128,128]{3,2,1,0:T(8,128)(2,1)S(1)}, u32[]{:S(2)}, u32[]{:S(2)}) async-start(bf16[32,3,128,128]{3,2,1,0:T(8,128)(2,1)} %bitcast.17), calls=%async_computation | async-start | bytes 6291456 | tf_op jit(solution)/shard_map/all_to_all | solution.py:325
  11.6 0.0 copy-start.7
  11.6 0.0 copy-start.8
  11.7 0.0 copy-start.9
  11.7 8.8 %copy.21 = bf16[2,2048,768]{1,2,0:T(8,128)(2,1)} copy(bf16[2,2048,768]{2,1,0:T(8,128)(2,1)} %param.12) | data formatting | bytes 12582912 | tf_op args[2]
  20.4 2.6 %copy.22 = f32[2,49,2048]{2,1,0:T(8,128)} copy(f32[2,49,2048]{2,0,1:T(2,128)} %param.16) | data formatting | bytes 1605632 | tf_op args[6]
  23.0 0.0 copy-done.7
  23.0 0.0 copy-done.8
  23.0 0.0 copy-start
  23.1 0.0 copy-done.9
  23.1 0.0 copy-start.1
  23.1 0.1 reshape.35.slot_ids
  23.2 3.3 %pad.4.harm_hbm = f32[6,64,2048]{2,1,0:T(8,128)} pad(f32[2,49,2048]{2,1,0:T(8,128)} %copy.22, f32[]{:T(128)} %constant.19.clone.1), padding=0_4x0_15x0_0 | pad | bytes 3948548 | tf_op jit(solution)/shard_map/jit(_pad)/pad | solution.py:358
  26.5 56.5 %all-to-all-done = bf16[32,3,128,128]{3,2,1,0:T(8,128)(2,1)S(1)} async-done(((bf16[32,3,128,128]{3,2,1,0:T(8,128)(2,1)}), bf16[32,3,128,128]{3,2,1,0:T(8,128)(2,1)S(1)}, u32[]{:S(2)}, u32[]{:S(2)}) %all-to-all-start) | async-done | bytes 3145760 | tf_op jit(solution)/shard_map/all_to_all | solution.py:325
  83.0 0.0 copy-done.4
  83.0 0.0 copy-done.5
  83.0 9.3 %density_pass.1 = (f32[512,1,2048]{2,1,0:T(1,128)}, f32[32,6,128]{2,1,0:T(8,128)}) custom-call(s32[2]{0:T(128)S(1)} %copy-done.4, s32[2,36]{1,0:T(2,128)S(1)} %reshape.35.slot_ids, s32[2]{0:T(128)S(1)} %copy-done.5, bf16[96,128,128]{2,1,0:T(8,128)(2,1)S(1)} %bitcast.11, bf16[2,768,2048]{2,1,0:T(8,128)(2,1)} %bitcast.14, f32[6,64,2048]{2,1,0:T(8,128)} %pad.4.harm_hbm, ...), custom_call_target="tpu_custom_call" | custom-call | tf_op jit(solution)/shard_map/density_pass/pallas_call | solution.py:168
  92.3 0.0 copy-done
  92.3 4.0 %all-to-all-start.1 = ((f32[32,6,128]{2,1,0:T(8,128)}), f32[32,6,128]{2,1,0:T(8,128)S(1)}, u32[]{:S(2)}, u32[]{:S(2)}) async-start(f32[32,6,128]{2,1,0:T(8,128)} %get-tuple-element.4), calls=%async_computation.1 | async-start | bytes 262144 | tf_op jit(solution)/shard_map/all_to_all | solution.py:325
  96.3 0.2 fusion.deg
  96.5 8.0 %all-to-all-done.1.got = f32[32,6,128]{2,1,0:T(8,128)S(1)} async-done(((f32[32,6,128]{2,1,0:T(8,128)}), f32[32,6,128]{2,1,0:T(8,128)S(1)}, u32[]{:S(2)}, u32[]{:S(2)}) %all-to-all-start.1) | async-done | bytes 98336 | tf_op jit(solution)/shard_map/all_to_all | solution.py:325
  104.5 2.2 %radial_solve.1 = f32[32,8,128]{2,1,0:T(8,128)S(1)} custom-call(s32[2]{0:T(128)S(1)} %fusion.deg, f32[32,6,128]{2,1,0:T(8,128)S(1)} %all-to-all-done.1.got, f32[7,128,128]{2,1,0:T(8,128)} %green_hbm.1), custom_call_target="tpu_custom_call" | custom-call | tf_op jit(solution)/shard_map/radial_solve/pallas_call | solution.py:233
  106.7 10.6 %all_to_all.20.got = f32[32,8,128]{2,1,0:T(8,128)} all-to-all(f32[32,8,128]{2,1,0:T(8,128)S(1)} %radial_solve.1), channel_id=1, replica_groups=mesh['row'=4,'col'=8] {'row','col'}, dimensions={0} | all-to-all | bytes 262144 | tf_op jit(solution)/shard_map/all_to_all | solution.py:325
  117.3 12.3 %potential_pass.1 = bf16[96,128,128]{2,1,0:T(8,128)(2,1)} custom-call(s32[2]{0:T(128)} %act.3, s32[2,36]{1,0:T(2,128)} %copy-done.2, f32[32,8,128]{2,1,0:T(8,128)} %all_to_all.20.got, f32[512,1,2048]{2,1,0:T(1,128)} %get-tuple-element.5.rho_hbm, bf16[2,768,2048]{2,1,0:T(8,128)(2,1)} %bitcast.15, f32[6,64,2048]{2,1,0:T(8,128)} %pad.4.harm_hbm, ...), custom_call_target="tpu_custom_call" | custom-call | tf_op jit(solution)/shard_map/potential_pass/pallas_call | solution.py:304
  129.6 0.0 copy-start.6
  129.7 0.0 copy-start.3
  129.7 2.9 %all-to-all-start.3 = ((bf16[32,3,128,128]{3,2,1,0:T(8,128)(2,1)}), bf16[32,3,128,128]{3,2,1,0:T(8,128)(2,1)S(1)}, u32[]{:S(2)}, u32[]{:S(2)}) async-start(bf16[32,3,128,128]{3,2,1,0:T(8,128)(2,1)} %bitcast.16), calls=%async_computation.3 | async-start | bytes 6291456 | tf_op jit(solution)/shard_map/all_to_all | solution.py:325
  132.7 0.6 slice.9
  133.3 70.7 %all-to-all-done.3 = bf16[32,3,128,128]{3,2,1,0:T(8,128)(2,1)S(1)} async-done(((bf16[32,3,128,128]{3,2,1,0:T(8,128)(2,1)}), bf16[32,3,128,128]{3,2,1,0:T(8,128)(2,1)S(1)}, u32[]{:S(2)}, u32[]{:S(2)}) %all-to-all-start.3) | async-done | bytes 3145760 | tf_op jit(solution)/shard_map/all_to_all | solution.py:325
  204.0 0.0 copy-done.3
  204.0 2.8 %sum_tiles.1 = f32[32,128,128]{2,1,0:T(8,128)} custom-call(s32[3,1,32]{2,1,0:T(1,128)S(1)} %bitcast.13, bf16[96,128,128]{2,1,0:T(8,128)(2,1)S(1)} %bitcast.10), custom_call_target="tpu_custom_call" | custom-call | tf_op jit(solution)/shard_map/sum_tiles/pallas_call | solution.py:94
  (13 shorter events, 0.1 us)
Async XLA Ops:
  4.3 78.7 %all-to-all-start = ((bf16[32,3,128,128]{3,2,1,0:T(8,128)(2,1)}), bf16[32,3,128,128]{3,2,1,0:T(8,128)(2,1)S(1)}, u32[]{:S(2)}, u32[]{:S(2)}) async-start(bf16[32,3,128,128]{3,2,1,0:T(8,128)(2,1)} %bitcast.17), calls=%async_computation | async-start | bytes 6291456 | tf_op jit(solution)/shard_map/all_to_all | solution.py:325
  11.6 11.4 %copy-start.7 = (f32[2,2048]{1,0:T(2,128)S(1)}, f32[2,2048]{1,0:T(2,128)}, u32[]{:S(2)}) copy-start(f32[2,2048]{1,0:T(2,128)} %param.15) | copy-start | bytes 49156
  11.6 11.4 %copy-start.8 = (s32[2,2048]{1,0:T(2,128)S(1)}, s32[2,2048]{1,0:T(2,128)}, u32[]{:S(2)}) copy-start(s32[2,2048]{1,0:T(2,128)} %param.17) | copy-start | bytes 49156
  11.7 11.4 %copy-start.9 = (s32[2,6,6]{2,0,1:T(2,128)S(1)}, s32[2,6,6]{2,0,1:T(2,128)}, u32[]{:S(2)}) copy-start(s32[2,6,6]{2,0,1:T(2,128)} %param.14) | copy-start | bytes 868
  20.4 62.5 %copy-start.4 = (s32[2]{0:T(128)S(1)}, s32[2]{0:T(128)}, u32[]{:S(2)}) copy-start(s32[2]{0:T(128)} %act.3) | copy-start | bytes 28
  20.4 62.5 %copy-start.5 = (s32[2]{0:T(128)S(1)}, s32[2]{0:T(128)}, u32[]{:S(2)}) copy-start(s32[2]{0:T(128)} %atom_ids.1) | copy-start | bytes 28
  23.0 69.2 %copy-start = (f32[2,1,2048]{2,1,0:T(1,128)}, f32[2,1,2048]{2,1,0:T(1,128)S(1)}, u32[]{:S(2)}) copy-start(f32[2,1,2048]{2,1,0:T(1,128)S(1)} %broadcast_in_dim.8.wts) | copy-start | bytes 49156
  23.1 69.2 %copy-start.1 = (s32[2,1,2048]{2,1,0:T(1,128)}, s32[2,1,2048]{2,1,0:T(1,128)S(1)}, u32[]{:S(2)}) copy-start(s32[2,1,2048]{2,1,0:T(1,128)S(1)} %broadcast_in_dim.9.shell) | copy-start | bytes 49156
  23.2 69.1 %copy-start.2 = (s32[2,36]{1,0:T(2,128)}, s32[2,36]{1,0:T(2,128)S(1)}, u32[]{:S(2)}) copy-start(s32[2,36]{1,0:T(2,128)S(1)} %reshape.35.slot_ids) | copy-start | bytes 868
  92.3 12.2 %all-to-all-start.1 = ((f32[32,6,128]{2,1,0:T(8,128)}), f32[32,6,128]{2,1,0:T(8,128)S(1)}, u32[]{:S(2)}, u32[]{:S(2)}) async-start(f32[32,6,128]{2,1,0:T(8,128)} %get-tuple-element.4), calls=%async_computation.1 | async-start | bytes 262144 | tf_op jit(solution)/shard_map/all_to_all | solution.py:325
  129.6 3.0 %copy-start.6 = (f32[32,8,128]{2,1,0:T(8,128)S(1)}, f32[32,8,128]{2,1,0:T(8,128)}, u32[]{:S(2)}) copy-start(f32[32,8,128]{2,1,0:T(8,128)} %all_to_all.20.got) | copy-start | bytes 393220
  129.7 74.4 %copy-start.3 = (s32[1,32,3]{1,0,2:T(1,128)S(1)}, s32[1,32,3]{1,0,2:T(1,128)}, u32[]{:S(2)}) copy-start(s32[1,32,3]{1,0,2:T(1,128)} %param.11) | copy-start | bytes 1156
  129.7 74.4 %all-to-all-start.3 = ((bf16[32,3,128,128]{3,2,1,0:T(8,128)(2,1)}), bf16[32,3,128,128]{3,2,1,0:T(8,128)(2,1)S(1)}, u32[]{:S(2)}, u32[]{:S(2)}) async-start(bf16[32,3,128,128]{3,2,1,0:T(8,128)(2,1)} %bitcast.16), calls=%async_computation.3 | async-start | bytes 6291456 | tf_op jit(solution)/shard_map/all_to_all | solution.py:325

commit v4 on v3

--- a/solution.py
+++ b/solution.py
@@ -304,7 +304,7 @@
     return pl.pallas_call(
         body,
         out_shape=jax.ShapeDtypeStruct((slot_count, blk, blk), BF16),
-        in_specs=[SMEM, SMEM, VMEM, VMEM, HBM, HBM, VMEM, VMEM],
+        in_specs=[SMEM, SMEM, VMEM, HBM, HBM, HBM, VMEM, VMEM],
         out_specs=VMEM,
         scratch_shapes=[
             pltpu.VMEM(basis_t.shape, BF16),

time: 207 us -> 206 us (level)
  no operation moved by 1% of the time
where the time goes in v4:
time: 206 us
  waiting for transfers between devices  135 us (66%)
  Pallas kernels  28.9 us (14%)
  local copies, waits for them, and re-layouts  15.5 us (8%)
  starting transfers between devices  14.3 us (7%)
  blocking collectives  10.6 us (5%)
    all_to_all x3, waiting for transfers between devices, exchange(): return lax.all_to_all(parts, AXES, split_axis=0, concat_axis=0, tiled=True)  135 us
    all_to_all x3, starting transfers between devices, exchange(): return lax.all_to_all(parts, AXES, split_axis=0, concat_axis=0, tiled=True)  14.3 us
    unnamed x23, local copies, waits for them, and re-layouts  11.4 us
    pallas_call x1, Pallas kernels, potential_pass(): pl.pallas_call(body, out_shape=jax.ShapeDtypeStruct((slot_count, blk, blk...  11.1 us
    all_to_all x1, blocking collectives, exchange(): return lax.all_to_all(parts, AXES, split_axis=0, concat_axis=0, tiled=True)  10.6 us
    pallas_call x1, Pallas kernels, density_pass(): pl.pallas_call(body, out_shape=(jax.ShapeDtypeStruct((SPARE * batches, 1,...  9.28 us
  transfers between devices with their start and end apart: 3, of which 3 were waited for; matrix products, arithmetic and copies ran while one was open for 8% of the time, Pallas kernels for 0%

profile of v4, /device:TPU:0, one launch (start us, length us, event | category | flops | bytes accessed | tf_op | source)
XLA Modules:
  0.0 205.5 jit_solution(4246533317160508986)
XLA Ops:
  0.6 3.6 %gather_tiles.1 = bf16[96,128,128]{2,1,0:T(8,128)(2,1)} custom-call(s32[3,1,32]{2,1,0:T(1,128)} %bitcast.12, bf16[32,128,128]{2,1,0:T(8,128)(2,1)} %tiles_ref.1), custom_call_target="tpu_custom_call" | custom-call | tf_op jit(solution)/shard_map/gather_tiles/pallas_call | solution.py:68
  4.3 7.3 %all-to-all-start = ((bf16[32,3,128,128]{3,2,1,0:T(8,128)(2,1)}), bf16[32,3,128,128]{3,2,1,0:T(8,128)(2,1)S(1)}, u32[]{:S(2)}, u32[]{:S(2)}) async-start(bf16[32,3,128,128]{3,2,1,0:T(8,128)(2,1)} %bitcast.17), calls=%async_computation | async-start | bytes 6291456 | tf_op jit(solution)/shard_map/all_to_all | solution.py:325
  11.6 0.0 copy-start.7
  11.6 0.0 copy-start.8
  11.7 0.0 copy-start.9
  11.7 8.8 %copy.21 = bf16[2,2048,768]{1,2,0:T(8,128)(2,1)} copy(bf16[2,2048,768]{2,1,0:T(8,128)(2,1)} %param.12) | data formatting | bytes 12582912 | tf_op args[2]
  20.4 2.6 %copy.22 = f32[2,49,2048]{2,1,0:T(8,128)} copy(f32[2,49,2048]{2,0,1:T(2,128)} %param.16) | data formatting | bytes 1605632 | tf_op args[6]
  23.0 0.0 copy-done.7
  23.0 0.0 copy-done.8
  23.0 0.0 copy-start
  23.1 0.0 copy-done.9
  23.1 0.0 copy-start.1
  23.1 0.1 reshape.35.slot_ids
  23.2 3.3 %pad.4.harm_hbm = f32[6,64,2048]{2,1,0:T(8,128)} pad(f32[2,49,2048]{2,1,0:T(8,128)} %copy.22, f32[]{:T(128)} %constant.19.clone.1), padding=0_4x0_15x0_0 | pad | bytes 3948548 | tf_op jit(solution)/shard_map/jit(_pad)/pad | solution.py:358
  26.5 56.5 %all-to-all-done = bf16[32,3,128,128]{3,2,1,0:T(8,128)(2,1)S(1)} async-done(((bf16[32,3,128,128]{3,2,1,0:T(8,128)(2,1)}), bf16[32,3,128,128]{3,2,1,0:T(8,128)(2,1)S(1)}, u32[]{:S(2)}, u32[]{:S(2)}) %all-to-all-start) | async-done | bytes 3145760 | tf_op jit(solution)/shard_map/all_to_all | solution.py:325
  83.0 0.0 copy-done.4
  83.0 0.0 copy-done.5
  83.0 9.3 %density_pass.1 = (f32[512,1,2048]{2,1,0:T(1,128)}, f32[32,6,128]{2,1,0:T(8,128)}) custom-call(s32[2]{0:T(128)S(1)} %copy-done.4, s32[2,36]{1,0:T(2,128)S(1)} %reshape.35.slot_ids, s32[2]{0:T(128)S(1)} %copy-done.5, bf16[96,128,128]{2,1,0:T(8,128)(2,1)S(1)} %bitcast.11, bf16[2,768,2048]{2,1,0:T(8,128)(2,1)} %bitcast.14, f32[6,64,2048]{2,1,0:T(8,128)} %pad.4.harm_hbm, ...), custom_call_target="tpu_custom_call" | custom-call | tf_op jit(solution)/shard_map/density_pass/pallas_call | solution.py:168
  92.3 0.0 copy-done
  92.3 0.0 copy-done.1
  92.3 4.0 %all-to-all-start.1 = ((f32[32,6,128]{2,1,0:T(8,128)}), f32[32,6,128]{2,1,0:T(8,128)S(1)}, u32[]{:S(2)}, u32[]{:S(2)}) async-start(f32[32,6,128]{2,1,0:T(8,128)} %get-tuple-element.4), calls=%async_computation.1 | async-start | bytes 262144 | tf_op jit(solution)/shard_map/all_to_all | solution.py:325
  96.3 0.2 fusion.deg
  96.5 8.0 %all-to-all-done.1.got = f32[32,6,128]{2,1,0:T(8,128)S(1)} async-done(((f32[32,6,128]{2,1,0:T(8,128)}), f32[32,6,128]{2,1,0:T(8,128)S(1)}, u32[]{:S(2)}, u32[]{:S(2)}) %all-to-all-start.1) | async-done | bytes 98336 | tf_op jit(solution)/shard_map/all_to_all | solution.py:325
  104.5 2.2 %radial_solve.1 = f32[32,8,128]{2,1,0:T(8,128)S(1)} custom-call(s32[2]{0:T(128)S(1)} %fusion.deg, f32[32,6,128]{2,1,0:T(8,128)S(1)} %all-to-all-done.1.got, f32[7,128,128]{2,1,0:T(8,128)} %green_hbm.1), custom_call_target="tpu_custom_call" | custom-call | tf_op jit(solution)/shard_map/radial_solve/pallas_call | solution.py:233
  106.7 10.6 %all_to_all.20.got = f32[32,8,128]{2,1,0:T(8,128)} all-to-all(f32[32,8,128]{2,1,0:T(8,128)S(1)} %radial_solve.1), channel_id=1, replica_groups=mesh['row'=4,'col'=8] {'row','col'}, dimensions={0} | all-to-all | bytes 262144 | tf_op jit(solution)/shard_map/all_to_all | solution.py:325
  117.3 11.1 %potential_pass.1 = bf16[96,128,128]{2,1,0:T(8,128)(2,1)} custom-call(s32[2]{0:T(128)} %act.3, s32[2,36]{1,0:T(2,128)} %copy-done.2, f32[32,8,128]{2,1,0:T(8,128)} %all_to_all.20.got, f32[512,1,2048]{2,1,0:T(1,128)} %get-tuple-element.5.rho_hbm, bf16[2,768,2048]{2,1,0:T(8,128)(2,1)} %bitcast.15, f32[6,64,2048]{2,1,0:T(8,128)} %pad.4.harm_hbm, ...), custom_call_target="tpu_custom_call" | custom-call | tf_op jit(solution)/shard_map/potential_pass/pallas_call | solution.py:304
  128.4 0.0 copy-start.3
  128.4 2.9 %all-to-all-start.3 = ((bf16[32,3,128,128]{3,2,1,0:T(8,128)(2,1)}), bf16[32,3,128,128]{3,2,1,0:T(8,128)(2,1)S(1)}, u32[]{:S(2)}, u32[]{:S(2)}) async-start(bf16[32,3,128,128]{3,2,1,0:T(8,128)(2,1)} %bitcast.16), calls=%async_computation.3 | async-start | bytes 6291456 | tf_op jit(solution)/shard_map/all_to_all | solution.py:325
  131.4 0.6 slice.9
  132.0 70.7 %all-to-all-done.3 = bf16[32,3,128,128]{3,2,1,0:T(8,128)(2,1)S(1)} async-done(((bf16[32,3,128,128]{3,2,1,0:T(8,128)(2,1)}), bf16[32,3,128,128]{3,2,1,0:T(8,128)(2,1)S(1)}, u32[]{:S(2)}, u32[]{:S(2)}) %all-to-all-start.3) | async-done | bytes 3145760 | tf_op jit(solution)/shard_map/all_to_all | solution.py:325
  202.8 0.0 copy-done.3
  202.8 2.8 %sum_tiles.1 = f32[32,128,128]{2,1,0:T(8,128)} custom-call(s32[3,1,32]{2,1,0:T(1,128)S(1)} %bitcast.13, bf16[96,128,128]{2,1,0:T(8,128)(2,1)S(1)} %bitcast.10), custom_call_target="tpu_custom_call" | custom-call | tf_op jit(solution)/shard_map/sum_tiles/pallas_call | solution.py:94
  (13 shorter events, 0.1 us)
Async XLA Ops:
  4.3 78.7 %all-to-all-start = ((bf16[32,3,128,128]{3,2,1,0:T(8,128)(2,1)}), bf16[32,3,128,128]{3,2,1,0:T(8,128)(2,1)S(1)}, u32[]{:S(2)}, u32[]{:S(2)}) async-start(bf16[32,3,128,128]{3,2,1,0:T(8,128)(2,1)} %bitcast.17), calls=%async_computation | async-start | bytes 6291456 | tf_op jit(solution)/shard_map/all_to_all | solution.py:325
  11.6 11.4 %copy-start.7 = (f32[2,2048]{1,0:T(2,128)S(1)}, f32[2,2048]{1,0:T(2,128)}, u32[]{:S(2)}) copy-start(f32[2,2048]{1,0:T(2,128)} %param.15) | copy-start | bytes 49156
  11.6 11.4 %copy-start.8 = (s32[2,2048]{1,0:T(2,128)S(1)}, s32[2,2048]{1,0:T(2,128)}, u32[]{:S(2)}) copy-start(s32[2,2048]{1,0:T(2,128)} %param.17) | copy-start | bytes 49156
  11.7 11.4 %copy-start.9 = (s32[2,6,6]{2,0,1:T(2,128)S(1)}, s32[2,6,6]{2,0,1:T(2,128)}, u32[]{:S(2)}) copy-start(s32[2,6,6]{2,0,1:T(2,128)} %param.14) | copy-start | bytes 868
  20.4 62.5 %copy-start.4 = (s32[2]{0:T(128)S(1)}, s32[2]{0:T(128)}, u32[]{:S(2)}) copy-start(s32[2]{0:T(128)} %act.3) | copy-start | bytes 28
  20.4 62.5 %copy-start.5 = (s32[2]{0:T(128)S(1)}, s32[2]{0:T(128)}, u32[]{:S(2)}) copy-start(s32[2]{0:T(128)} %atom_ids.1) | copy-start | bytes 28
  23.0 69.2 %copy-start = (f32[2,1,2048]{2,1,0:T(1,128)}, f32[2,1,2048]{2,1,0:T(1,128)S(1)}, u32[]{:S(2)}) copy-start(f32[2,1,2048]{2,1,0:T(1,128)S(1)} %broadcast_in_dim.8.wts) | copy-start | bytes 49156
  23.1 69.2 %copy-start.1 = (s32[2,1,2048]{2,1,0:T(1,128)}, s32[2,1,2048]{2,1,0:T(1,128)S(1)}, u32[]{:S(2)}) copy-start(s32[2,1,2048]{2,1,0:T(1,128)S(1)} %broadcast_in_dim.9.shell) | copy-start | bytes 49156
  23.2 69.1 %copy-start.2 = (s32[2,36]{1,0:T(2,128)}, s32[2,36]{1,0:T(2,128)S(1)}, u32[]{:S(2)}) copy-start(s32[2,36]{1,0:T(2,128)S(1)} %reshape.35.slot_ids) | copy-start | bytes 868
  92.3 12.2 %all-to-all-start.1 = ((f32[32,6,128]{2,1,0:T(8,128)}), f32[32,6,128]{2,1,0:T(8,128)S(1)}, u32[]{:S(2)}, u32[]{:S(2)}) async-start(f32[32,6,128]{2,1,0:T(8,128)} %get-tuple-element.4), calls=%async_computation.1 | async-start | bytes 262144 | tf_op jit(solution)/shard_map/all_to_all | solution.py:325
  128.4 3.0 %copy-start.6 = (f32[32,8,128]{2,1,0:T(8,128)S(1)}, f32[32,8,128]{2,1,0:T(8,128)}, u32[]{:S(2)}) copy-start(f32[32,8,128]{2,1,0:T(8,128)} %all_to_all.20.got) | copy-start | bytes 393220
  128.4 74.4 %copy-start.3 = (s32[1,32,3]{1,0,2:T(1,128)S(1)}, s32[1,32,3]{1,0,2:T(1,128)}, u32[]{:S(2)}) copy-start(s32[1,32,3]{1,0,2:T(1,128)} %param.11) | copy-start | bytes 1156
  128.4 74.4 %all-to-all-start.3 = ((bf16[32,3,128,128]{3,2,1,0:T(8,128)(2,1)}), bf16[32,3,128,128]{3,2,1,0:T(8,128)(2,1)S(1)}, u32[]{:S(2)}, u32[]{:S(2)}) async-start(bf16[32,3,128,128]{3,2,1,0:T(8,128)(2,1)} %bitcast.16), calls=%async_computation.3 | async-start | bytes 6291456 | tf_op jit(solution)/shard_map/all_to_all | solution.py:325

commit v5 on v4

--- a/solution.py
+++ b/solution.py
@@ -46,14 +46,28 @@
     ]
 
 
+def plan_views(plan, blocks):
+    pairs = blocks * blocks
+    return (
+        lambda b: plan[b, pairs],
+        lambda b, pair: plan[b, pair],
+        lambda b: plan[b, pairs + 1],
+    )
+
+
 def gather_tiles(tile_ids, tiles):
     capacity, _, devices = tile_ids.shape
     count = capacity * devices
 
-    def body(ids, tiles_ref, out_ref, keep, sems):
-        load = pltpu.make_async_copy(tiles_ref, keep, sems.at[0])
-        load.start()
-        load.wait()
+    def body(ids_hbm, tiles_ref, out_ref, keep, ids, sems):
+        loads = [
+            pltpu.make_async_copy(ids_hbm, ids, sems.at[2]),
+            pltpu.make_async_copy(tiles_ref, keep, sems.at[0]),
+        ]
+        for load in loads:
+            load.start()
+        for load in loads:
+            load.wait()
 
         def send(dev, carry):
             for k in range(capacity):
@@ -68,9 +82,13 @@
     return pl.pallas_call(
         body,
         out_shape=jax.ShapeDtypeStruct((count,) + tiles.shape[1:], tiles.dtype),
-        in_specs=[SMEM, HBM],
+        in_specs=[HBM, HBM],
         out_specs=HBM,
-        scratch_shapes=[pltpu.VMEM(tiles.shape, tiles.dtype), pltpu.SemaphoreType.DMA((2,))],
+        scratch_shapes=[
+            pltpu.VMEM(tiles.shape, tiles.dtype),
+            pltpu.SMEM(tile_ids.shape, jnp.int32),
+            pltpu.SemaphoreType.DMA((3,)),
+        ],
         compiler_params=params(63),
         name="gather_tiles",
     )(tile_ids, tiles)
@@ -80,8 +98,11 @@
     capacity, _, devices = tile_ids.shape
     _, blk, _ = arrived.shape
 
-    def body(ids, arrived_ref, out_ref):
+    def body(ids_hbm, arrived_ref, out_ref, ids, sem):
+        load = pltpu.make_async_copy(ids_hbm, ids, sem)
+        load.start()
         out_ref[...] = jnp.zeros_like(out_ref)
+        load.wait()
 
         def add(dev, carry):
             for k in range(capacity):
@@ -94,14 +115,15 @@
     return pl.pallas_call(
         body,
         out_shape=jax.ShapeDtypeStruct((tiles_dev, blk, blk), F32),
-        in_specs=[SMEM, VMEM],
+        in_specs=[HBM, VMEM],
         out_specs=VMEM,
+        scratch_shapes=[pltpu.SMEM(tile_ids.shape, jnp.int32), pltpu.SemaphoreType.DMA],
         compiler_params=params(16),
         name="sum_tiles",
     )(tile_ids, arrived)
 
 
-def density_pass(active, slots, atoms, received, basis_t, harmonics, weights, shells, share, devices):
+def density_pass(plan, received, basis_t, harmonics, weights, shells, share, devices):
     batches, span, points = basis_t.shape
     slot_count, blk, _ = received.shape
     blocks = span // blk
@@ -109,16 +131,24 @@
     held, radial = share
     lines = (held + 1) * batches
 
-    def body(act, slot_ids, atom_ids, recv, phi_hbm, harm_hbm, wts, shell, rho_hbm, send,
-             phi, harm, rho, matrix, mom_keep, phi_sems, harm_sems, rho_sems):
+    def body(plan_hbm, recv, phi_hbm, harm_hbm, wts_hbm, shell_hbm, rho_hbm, send,
+             phi, harm, rho, matrix, mom_keep, plan_keep, wts, shell,
+             phi_sems, harm_sems, rho_sems, sems):
         phi_loads = loads_of(phi_hbm, phi, phi_sems)
         harm_loads = loads_of(harm_hbm, harm, harm_sems)
         rho_stores = loads_of(rho, rho_hbm, rho_sems)
-        for load in phi_loads + harm_loads:
+        plan_load = pltpu.make_async_copy(plan_hbm, plan_keep, sems.at[0])
+        point_loads = [
+            pltpu.make_async_copy(wts_hbm, wts, sems.at[1]),
+            pltpu.make_async_copy(shell_hbm, shell, sems.at[2]),
+        ]
+        for load in [plan_load] + phi_loads[:1] + point_loads + phi_loads[1:] + harm_loads:
             load.start()
-
-        for b in range(batches):
-            count = act[b]
+        act, slot_ids, atom_ids = plan_views(plan_keep, blocks)
+        plan_load.wait()
+
+        for b in range(batches):
+            count = act(b)
             for i in range(blocks):
                 for j in range(blocks):
                     spot = (b, pl.ds(i * blk, blk), pl.ds(j * blk, blk))
@@ -126,7 +156,7 @@
 
                     @pl.when(live)
                     def _(b=b, i=i, j=j, spot=spot):
-                        slot = jnp.clip(slot_ids[b, i * blocks + j], 0, slot_count - 1)
+                        slot = jnp.clip(slot_ids(b, i * blocks + j), 0, slot_count - 1)
                         matrix[spot] = recv[slot]
 
                     @pl.when(jnp.logical_not(live))
@@ -135,7 +165,7 @@
 
         for b in range(batches):
             send[:, pl.ds(held * batches + b, 1), :] = jnp.full(
-                (devices, 1, radial), atom_ids[b].astype(F32), F32
+                (devices, 1, radial), atom_ids(b).astype(F32), F32
             )
 
         def moments(b):
@@ -159,6 +189,8 @@
             rho[b] = jnp.sum(product * phi[b].astype(F32), axis=0, keepdims=True)
             rho_stores[b].start()
 
+        for load in point_loads:
+            load.wait()
         for b in range(batches):
             harm_loads[b].wait()
             moments(b)
@@ -171,7 +203,7 @@
             jax.ShapeDtypeStruct((SPARE * batches, 1, points), F32),
             jax.ShapeDtypeStruct((devices, lines, radial), F32),
         ),
-        in_specs=[SMEM, SMEM, SMEM, VMEM, HBM, HBM, VMEM, VMEM],
+        in_specs=[HBM, VMEM, HBM, HBM, HBM, HBM],
         out_specs=(HBM, VMEM),
         scratch_shapes=[
             pltpu.VMEM(basis_t.shape, BF16),
@@ -179,13 +211,17 @@
             pltpu.VMEM((batches, 1, points), F32),
             pltpu.VMEM((batches, span, span), BF16),
             pltpu.VMEM((batches, rows, radial), F32),
-            pltpu.SemaphoreType.DMA((batches,)),
-            pltpu.SemaphoreType.DMA((batches,)),
-            pltpu.SemaphoreType.DMA((batches,)),
+            pltpu.SMEM(plan.shape, jnp.int32),
+            pltpu.VMEM((batches, 1, points), F32),
+            pltpu.VMEM((batches, 1, points), jnp.int32),
+            pltpu.SemaphoreType.DMA((batches,)),
+            pltpu.SemaphoreType.DMA((batches,)),
+            pltpu.SemaphoreType.DMA((batches,)),
+            pltpu.SemaphoreType.DMA((3,)),
         ],
         compiler_params=params(52 - received.size * 2 / 2**20),
         name="density_pass",
-    )(active, slots, atoms, received, basis_t, harmonics, weights, shells)
+    )(plan, received, basis_t, harmonics, weights, shells)
 
 
 def radial_solve(degree_ids, arrived, green, natoms, held, batches, cols_count):
@@ -245,20 +281,27 @@
     )(degree_ids, arrived, green)
 
 
-def potential_pass(active, slots, poles, rho, basis_t, harmonics, weights, shells, slot_count, blk, held):
+def potential_pass(plan, poles, rho, basis_t, harmonics, weights, shells, slot_count, blk, held):
     batches, span, points = basis_t.shape
     blocks = span // blk
     rows = harmonics.shape[1]
     devices, lines, radial = poles.shape
     wide = 2 * blk if blocks % 2 == 0 else blk
 
-    def body(act, slot_ids, got, rho_hbm, phi_hbm, harm_hbm, wts, shell, out,
-             phi, harm, rho, scaled, poles_keep, phi_sems, harm_sems, rho_sems):
+    def body(plan_hbm, got, rho_hbm, phi_hbm, harm_hbm, wts_hbm, shell_hbm, out,
+             phi, harm, rho, scaled, poles_keep, plan_keep, wts, shell,
+             phi_sems, harm_sems, rho_sems, sems):
         phi_loads = loads_of(phi_hbm, phi, phi_sems)
         harm_loads = loads_of(harm_hbm, harm, harm_sems)
         rho_loads = loads_of(rho_hbm, rho, rho_sems)
-        for load in rho_loads + harm_loads + phi_loads:
+        point_loads = [
+            pltpu.make_async_copy(plan_hbm, plan_keep, sems.at[0]),
+            pltpu.make_async_copy(wts_hbm, wts, sems.at[1]),
+            pltpu.make_async_copy(shell_hbm, shell, sems.at[2]),
+        ]
+        for load in rho_loads + point_loads + harm_loads + phi_loads:
             load.start()
+        act, slot_ids, _ = plan_views(plan_keep, blocks)
 
         out[...] = jnp.zeros_like(out)
         if held * devices < rows:
@@ -270,6 +313,8 @@
                     if line < rows:
                         poles_keep[b, pl.ds(line, 1), :] = got[d, pl.ds(b * held + k, 1), :]
 
+        for load in point_loads:
+            load.wait()
         factors = []
         for b in range(batches):
             rho_loads[b].wait()
@@ -283,12 +328,11 @@
             root = jnp.exp(jnp.log(1.0 + rho[b] * rho[b]) * (-1.0 / 3.0))
             factors.append(wts[b] * (hartree - rho[b] * root))
 
-        for b in range(batches):
-            phi_loads[b].wait()
+        for load in phi_loads:
+            load.wait()
+        for b in range(batches):
             scaled[b] = (phi[b].astype(F32) * factors[b]).astype(BF16)
-
-        for b in range(batches):
-            count = act[b]
+            count = act(b)
             for first in range(0, span, wide):
                 piece = lax.dot_general(
                     phi[b], scaled[b, pl.ds(first, wide), :], NT, preferred_element_type=F32
@@ -296,7 +340,7 @@
                 for i in range(blocks):
                     for j in range(first // blk, (first + wide) // blk):
                         live = (i < count) & (j < count)
-                        slot = jnp.clip(slot_ids[b, i * blocks + j], 0, slot_count - 1)
+                        slot = jnp.clip(slot_ids(b, i * blocks + j), 0, slot_count - 1)
                         left = j * blk - first
                         tile = piece[i * blk : (i + 1) * blk, left : left + blk].astype(BF16)
                         out[slot] = jnp.where(live, tile, out[slot])
@@ -304,7 +348,7 @@
     return pl.pallas_call(
         body,
         out_shape=jax.ShapeDtypeStruct((slot_count, blk, blk), BF16),
-        in_specs=[SMEM, SMEM, VMEM, HBM, HBM, HBM, VMEM, VMEM],
+        in_specs=[HBM, VMEM, HBM, HBM, HBM, HBM, HBM],
         out_specs=VMEM,
         scratch_shapes=[
             pltpu.VMEM(basis_t.shape, BF16),
@@ -312,13 +356,17 @@
             pltpu.VMEM((batches, 1, points), F32),
             pltpu.VMEM(basis_t.shape, BF16),
             pltpu.VMEM((batches, rows, radial), F32),
-            pltpu.SemaphoreType.DMA((batches,)),
-            pltpu.SemaphoreType.DMA((batches,)),
-            pltpu.SemaphoreType.DMA((batches,)),
+            pltpu.SMEM(plan.shape, jnp.int32),
+            pltpu.VMEM((batches, 1, points), F32),
+            pltpu.VMEM((batches, 1, points), jnp.int32),
+            pltpu.SemaphoreType.DMA((batches,)),
+            pltpu.SemaphoreType.DMA((batches,)),
+            pltpu.SemaphoreType.DMA((batches,)),
+            pltpu.SemaphoreType.DMA((3,)),
         ],
         compiler_params=params(62),
         name="potential_pass",
-    )(active, slots, poles, rho, basis_t, harmonics, weights, shells)
+    )(plan, poles, rho, basis_t, harmonics, weights, shells)
 
 
 def exchange(parts):
@@ -358,10 +406,12 @@
     harm_rows = jnp.pad(harmonics, ((0, 2 * batches), (0, rows - harm_count), (0, 0)))
     weights = point_weights[:, None, :]
     shells = shell_index[:, None, :]
-    slots = touch_slots.reshape(batches, -1)
+    plan = jnp.concatenate(
+        [touch_slots.reshape(batches, -1), active_blocks[:, None], batch_atom[:, None]], axis=1
+    )
 
     rho, mom_out = density_pass(
-        active_blocks, slots, batch_atom, received, basis_t, harm_rows, weights, shells,
+        plan, received, basis_t, harm_rows, weights, shells,
         (held, radial), devices,
     )
     mom_in = exchange(mom_out)
@@ -372,7 +422,7 @@
     )
     poles = exchange(poles_out)
     returning = potential_pass(
-        active_blocks, slots, poles, rho, basis_t, harm_rows, weights, shells,
+        plan, poles, rho, basis_t, harm_rows, weights, shells,
         slot_count, blk, held,
     )
     back = exchange(returning.reshape(devices, capacity, blk, blk))

time: 206 us -> 205 us (level)
  no operation moved by 1% of the time
where the time goes in v5:
time: 205 us; the launch traced here: 204 us
  waiting for transfers between devices  135 us (66%)
  Pallas kernels  27.6 us (13%)
  local copies, waits for them, and re-layouts  15.6 us (8%)
  starting transfers between devices  14.3 us (7%)
  blocking collectives  10.6 us (5%)
    all_to_all x3, waiting for transfers between devices, exchange(): return lax.all_to_all(parts, AXES, split_axis=0, concat_axis=0, tiled=True)  135 us
    all_to_all x3, starting transfers between devices, exchange(): return lax.all_to_all(parts, AXES, split_axis=0, concat_axis=0, tiled=True)  14.3 us
    unnamed x23, local copies, waits for them, and re-layouts  11.4 us
    pallas_call x1, Pallas kernels, potential_pass(): pl.pallas_call(body, out_shape=jax.ShapeDtypeStruct((slot_count, blk, blk...  11 us
    all_to_all x1, blocking collectives, exchange(): return lax.all_to_all(parts, AXES, split_axis=0, concat_axis=0, tiled=True)  10.6 us
    pallas_call x1, Pallas kernels, density_pass(): pl.pallas_call(body, out_shape=(jax.ShapeDtypeStruct((SPARE * batches, 1,...  8.77 us
  transfers between devices with their start and end apart: 3, of which 3 were waited for; matrix products, arithmetic and copies ran while one was open for 8% of the time, Pallas kernels for 0%

profile of v5, /device:TPU:0, one launch (start us, length us, event | category | flops | bytes accessed | tf_op | source)
XLA Modules:
  0.0 204.3 jit_solution(13389372284920210871)
XLA Ops:
  0.6 3.0 %gather_tiles.1 = bf16[96,128,128]{2,1,0:T(8,128)(2,1)} custom-call(s32[3,1,32]{2,1,0:T(1,128)} %bitcast.14, bf16[32,128,128]{2,1,0:T(8,128)(2,1)} %tiles_ref.1), custom_call_target="tpu_custom_call" | custom-call | tf_op jit(solution)/shard_map/gather_tiles/pallas_call | solution.py:82
  3.6 7.3 %all-to-all-start = ((bf16[32,3,128,128]{3,2,1,0:T(8,128)(2,1)}), bf16[32,3,128,128]{3,2,1,0:T(8,128)(2,1)S(1)}, u32[]{:S(2)}, u32[]{:S(2)}) async-start(bf16[32,3,128,128]{3,2,1,0:T(8,128)(2,1)} %bitcast.19), calls=%async_computation | async-start | bytes 6291456 | tf_op jit(solution)/shard_map/all_to_all | solution.py:373
  10.9 0.0 copy-start.5
  11.0 0.0 copy-start.6
  11.0 0.0 copy-start.7
  11.0 0.0 copy-start.8
  11.0 0.0 copy-start.9
  11.0 8.8 %copy.27 = bf16[2,2048,768]{1,2,0:T(8,128)(2,1)} copy(bf16[2,2048,768]{2,1,0:T(8,128)(2,1)} %param.12) | data formatting | bytes 12582912 | tf_op args[2]
  19.8 2.5 %copy.28 = f32[2,49,2048]{2,1,0:T(8,128)} copy(f32[2,49,2048]{2,0,1:T(2,128)} %param.16) | data formatting | bytes 1605632 | tf_op args[6]
  22.3 0.0 copy-done.5
  22.3 0.0 copy-done.6
  22.3 0.0 copy-start
  22.4 0.0 copy-done.7
  22.4 0.1 reshape.35
  22.5 0.1 copy.25
  22.6 0.1 copy.26
  22.7 3.3 %pad.4.harm_hbm = f32[6,64,2048]{2,1,0:T(8,128)} pad(f32[2,49,2048]{2,1,0:T(8,128)} %copy.28, f32[]{:T(128)} %constant.19.clone.1), padding=0_4x0_15x0_0 | pad | bytes 3948548 | tf_op jit(solution)/shard_map/jit(_pad)/pad | solution.py:406
  26.0 0.1 pad_add_fusion.plan_hbm
  26.1 56.2 %all-to-all-done = bf16[32,3,128,128]{3,2,1,0:T(8,128)(2,1)S(1)} async-done(((bf16[32,3,128,128]{3,2,1,0:T(8,128)(2,1)}), bf16[32,3,128,128]{3,2,1,0:T(8,128)(2,1)S(1)}, u32[]{:S(2)}, u32[]{:S(2)}) %all-to-all-start) | async-done | bytes 3145760 | tf_op jit(solution)/shard_map/all_to_all | solution.py:373
  82.3 8.8 %density_pass.1 = (f32[512,1,2048]{2,1,0:T(1,128)}, f32[32,6,128]{2,1,0:T(8,128)}) custom-call(s32[2,38]{1,0:T(2,128)S(1)} %pad_add_fusion.plan_hbm, bf16[96,128,128]{2,1,0:T(8,128)(2,1)S(1)} %bitcast.13, bf16[2,768,2048]{2,1,0:T(8,128)(2,1)} %bitcast.16, f32[6,64,2048]{2,1,0:T(8,128)} %pad.4.harm_hbm, f32[2,1,2048]{2,1,0:T(1,128)S(1)} %broadcast_in_dim.16.wts_hbm, ...), custom_call_target="tpu_custom_call" | custom-call | tf_op jit(solution)/shard_map/density_pass/pallas_call | solution.py:200
  91.1 4.0 %all-to-all-start.1 = ((f32[32,6,128]{2,1,0:T(8,128)}), f32[32,6,128]{2,1,0:T(8,128)S(1)}, u32[]{:S(2)}, u32[]{:S(2)}) async-start(f32[32,6,128]{2,1,0:T(8,128)} %get-tuple-element.4), calls=%async_computation.1 | async-start | bytes 262144 | tf_op jit(solution)/shard_map/all_to_all | solution.py:373
  95.1 0.2 fusion.deg
  95.3 8.0 %all-to-all-done.1.got = f32[32,6,128]{2,1,0:T(8,128)S(1)} async-done(((f32[32,6,128]{2,1,0:T(8,128)}), f32[32,6,128]{2,1,0:T(8,128)S(1)}, u32[]{:S(2)}, u32[]{:S(2)}) %all-to-all-start.1) | async-done | bytes 98336 | tf_op jit(solution)/shard_map/all_to_all | solution.py:373
  103.3 2.2 %radial_solve.1 = f32[32,8,128]{2,1,0:T(8,128)S(1)} custom-call(s32[2]{0:T(128)S(1)} %fusion.deg, f32[32,6,128]{2,1,0:T(8,128)S(1)} %all-to-all-done.1.got, f32[7,128,128]{2,1,0:T(8,128)} %green_hbm.1), custom_call_target="tpu_custom_call" | custom-call | tf_op jit(solution)/shard_map/radial_solve/pallas_call | solution.py:269
  105.5 10.6 %all_to_all.20.got = f32[32,8,128]{2,1,0:T(8,128)} all-to-all(f32[32,8,128]{2,1,0:T(8,128)S(1)} %radial_solve.1), channel_id=1, replica_groups=mesh['row'=4,'col'=8] {'row','col'}, dimensions={0} | all-to-all | bytes 262144 | tf_op jit(solution)/shard_map/all_to_all | solution.py:373
  116.1 11.0 %potential_pass.1 = bf16[96,128,128]{2,1,0:T(8,128)(2,1)} custom-call(s32[2,38]{1,0:T(2,128)} %copy-done.2, f32[32,8,128]{2,1,0:T(8,128)} %all_to_all.20.got, f32[512,1,2048]{2,1,0:T(1,128)} %get-tuple-element.5.rho_hbm, bf16[2,768,2048]{2,1,0:T(8,128)(2,1)} %bitcast.17, f32[6,64,2048]{2,1,0:T(8,128)} %pad.4.harm_hbm, f32[2,1,2048]{2,1,0:T(1,128)} %copy-done, ...), custom_call_target="tpu_custom_call" | custom-call | tf_op jit(solution)/shard_map/potential_pass/pallas_call | solution.py:348
  127.1 0.0 copy-start.3
  127.1 2.9 %all-to-all-start.3 = ((bf16[32,3,128,128]{3,2,1,0:T(8,128)(2,1)}), bf16[32,3,128,128]{3,2,1,0:T(8,128)(2,1)S(1)}, u32[]{:S(2)}, u32[]{:S(2)}) async-start(bf16[32,3,128,128]{3,2,1,0:T(8,128)(2,1)} %bitcast.18), calls=%async_computation.3 | async-start | bytes 6291456 | tf_op jit(solution)/shard_map/all_to_all | solution.py:373
  130.2 0.6 slice.9
  130.8 70.7 %all-to-all-done.3 = bf16[32,3,128,128]{3,2,1,0:T(8,128)(2,1)S(1)} async-done(((bf16[32,3,128,128]{3,2,1,0:T(8,128)(2,1)}), bf16[32,3,128,128]{3,2,1,0:T(8,128)(2,1)S(1)}, u32[]{:S(2)}, u32[]{:S(2)}) %all-to-all-start.3) | async-done | bytes 3145760 | tf_op jit(solution)/shard_map/all_to_all | solution.py:373
  201.5 0.0 copy-done.3
  201.5 2.6 %sum_tiles.1 = f32[32,128,128]{2,1,0:T(8,128)} custom-call(s32[3,1,32]{2,1,0:T(1,128)S(1)} %bitcast.15, bf16[96,128,128]{2,1,0:T(8,128)(2,1)S(1)} %bitcast.12), custom_call_target="tpu_custom_call" | custom-call | tf_op jit(solution)/shard_map/sum_tiles/pallas_call | solution.py:115
  (16 shorter events, 0.1 us)
Async XLA Ops:
  3.6 78.7 %all-to-all-start = ((bf16[32,3,128,128]{3,2,1,0:T(8,128)(2,1)}), bf16[32,3,128,128]{3,2,1,0:T(8,128)(2,1)S(1)}, u32[]{:S(2)}, u32[]{:S(2)}) async-start(bf16[32,3,128,128]{3,2,1,0:T(8,128)(2,1)} %bitcast.19), calls=%async_computation | async-start | bytes 6291456 | tf_op jit(solution)/shard_map/all_to_all | solution.py:373
  10.9 11.4 %copy-start.5 = (f32[2,2048]{1,0:T(2,128)S(1)}, f32[2,2048]{1,0:T(2,128)}, u32[]{:S(2)}) copy-start(f32[2,2048]{1,0:T(2,128)} %param.15) | copy-start | bytes 49156
  11.0 11.4 %copy-start.6 = (s32[2,2048]{1,0:T(2,128)S(1)}, s32[2,2048]{1,0:T(2,128)}, u32[]{:S(2)}) copy-start(s32[2,2048]{1,0:T(2,128)} %param.17) | copy-start | bytes 49156
  11.0 11.4 %copy-start.7 = (s32[2,6,6]{2,0,1:T(2,128)S(1)}, s32[2,6,6]{2,0,1:T(2,128)}, u32[]{:S(2)}) copy-start(s32[2,6,6]{2,0,1:T(2,128)} %param.14) | copy-start | bytes 868
  11.0 11.5 %copy-start.8 = (s32[2]{0:T(128)S(1)}, s32[2]{0:T(128)}, u32[]{:S(2)}) copy-start(s32[2]{0:T(128)} %param.13) | copy-start | bytes 28
  11.0 11.6 %copy-start.9 = (s32[2]{0:T(128)S(1)}, s32[2]{0:T(128)}, u32[]{:S(2)}) copy-start(s32[2]{0:T(128)} %param.18) | copy-start | bytes 28
  22.3 68.7 %copy-start = (f32[2,1,2048]{2,1,0:T(1,128)}, f32[2,1,2048]{2,1,0:T(1,128)S(1)}, u32[]{:S(2)}) copy-start(f32[2,1,2048]{2,1,0:T(1,128)S(1)} %broadcast_in_dim.16.wts_hbm) | copy-start | bytes 49156
  22.4 68.7 %copy-start.1 = (s32[2,1,2048]{2,1,0:T(1,128)}, s32[2,1,2048]{2,1,0:T(1,128)S(1)}, u32[]{:S(2)}) copy-start(s32[2,1,2048]{2,1,0:T(1,128)S(1)} %broadcast_in_dim.17.shell_hbm) | copy-start | bytes 49156
  26.1 65.0 %copy-start.2 = (s32[2,38]{1,0:T(2,128)}, s32[2,38]{1,0:T(2,128)S(1)}, u32[]{:S(2)}) copy-start(s32[2,38]{1,0:T(2,128)S(1)} %pad_add_fusion.plan_hbm) | copy-start | bytes 916
  91.1 12.2 %all-to-all-start.1 = ((f32[32,6,128]{2,1,0:T(8,128)}), f32[32,6,128]{2,1,0:T(8,128)S(1)}, u32[]{:S(2)}, u32[]{:S(2)}) async-start(f32[32,6,128]{2,1,0:T(8,128)} %get-tuple-element.4), calls=%async_computation.1 | async-start | bytes 262144 | tf_op jit(solution)/shard_map/all_to_all | solution.py:373
  127.1 3.0 %copy-start.4 = (f32[32,8,128]{2,1,0:T(8,128)S(1)}, f32[32,8,128]{2,1,0:T(8,128)}, u32[]{:S(2)}) copy-start(f32[32,8,128]{2,1,0:T(8,128)} %all_to_all.20.got) | copy-start | bytes 393220
  127.1 74.4 %copy-start.3 = (s32[1,32,3]{1,0,2:T(1,128)S(1)}, s32[1,32,3]{1,0,2:T(1,128)}, u32[]{:S(2)}) copy-start(s32[1,32,3]{1,0,2:T(1,128)} %param.11) | copy-start | bytes 1156
  127.1 74.4 %all-to-all-start.3 = ((bf16[32,3,128,128]{3,2,1,0:T(8,128)(2,1)}), bf16[32,3,128,128]{3,2,1,0:T(8,128)(2,1)S(1)}, u32[]{:S(2)}, u32[]{:S(2)}) async-start(bf16[32,3,128,128]{3,2,1,0:T(8,128)(2,1)} %bitcast.18), calls=%async_computation.3 | async-start | bytes 6291456 | tf_op jit(solution)/shard_map/all_to_all | solution.py:373

commit v6 on v5

--- a/solution.py
+++ b/solution.py
@@ -224,14 +224,13 @@
     )(plan, received, basis_t, harmonics, weights, shells)
 
 
-def radial_solve(degree_ids, arrived, green, natoms, held, batches, cols_count):
+def radial_solve(arrived, green, natoms, held, batches, cols_count):
     devices, lines, radial = arrived.shape
     rows_out = (batches + ATOM_COL) * held
 
-    def body(deg, got, green_hbm, out, flat, green, sems):
+    def body(got, green_hbm, out, flat, green, sems):
         loads = [
-            pltpu.make_async_copy(green_hbm.at[deg[k]], green.at[k], sems.at[k])
-            for k in range(held)
+            pltpu.make_async_copy(green_hbm.at[k], green.at[k], sems.at[k]) for k in range(held)
         ]
         for load in loads:
             load.start()
@@ -269,7 +268,7 @@
     return pl.pallas_call(
         body,
         out_shape=jax.ShapeDtypeStruct((devices, rows_out, radial), F32),
-        in_specs=[SMEM, VMEM, HBM],
+        in_specs=[VMEM, HBM],
         out_specs=VMEM,
         scratch_shapes=[
             pltpu.VMEM((lines, devices, radial), F32),
@@ -278,7 +277,7 @@
         ],
         compiler_params=params(53.5),
         name="radial_solve",
-    )(degree_ids, arrived, green)
+    )(arrived, green)
 
 
 def potential_pass(plan, poles, rho, basis_t, harmonics, weights, shells, slot_count, blk, held):
@@ -328,22 +327,29 @@
             root = jnp.exp(jnp.log(1.0 + rho[b] * rho[b]) * (-1.0 / 3.0))
             factors.append(wts[b] * (hartree - rho[b] * root))
 
+        def keep(b, i, j, tile):
+            live = (i < act(b)) & (j < act(b))
+            slot = jnp.clip(slot_ids(b, i * blocks + j), 0, slot_count - 1)
+            out[slot] = jnp.where(live, tile, out[slot])
+
         for load in phi_loads:
             load.wait()
         for b in range(batches):
             scaled[b] = (phi[b].astype(F32) * factors[b]).astype(BF16)
-            count = act(b)
             for first in range(0, span, wide):
                 piece = lax.dot_general(
-                    phi[b], scaled[b, pl.ds(first, wide), :], NT, preferred_element_type=F32
+                    phi[b, pl.ds(first, span - first), :],
+                    scaled[b, pl.ds(first, wide), :],
+                    NT,
+                    preferred_element_type=F32,
                 )
-                for i in range(blocks):
+                for i in range(first // blk, blocks):
                     for j in range(first // blk, (first + wide) // blk):
-                        live = (i < count) & (j < count)
-                        slot = jnp.clip(slot_ids(b, i * blocks + j), 0, slot_count - 1)
-                        left = j * blk - first
-                        tile = piece[i * blk : (i + 1) * blk, left : left + blk].astype(BF16)
-                        out[slot] = jnp.where(live, tile, out[slot])
+                        top, left = i * blk - first, j * blk - first
+                        tile = piece[top : top + blk, left : left + blk].astype(BF16)
+                        keep(b, i, j, tile)
+                        if i * blk >= first + wide:
+                            keep(b, j, i, tile.T)
 
     return pl.pallas_call(
         body,
@@ -417,8 +423,11 @@
     mom_in = exchange(mom_out)
     first = lax.axis_index(AXES) * held
     degree_ids = degrees(jnp.minimum(first + jnp.arange(held), harm_count - 1))
+    green_own = jnp.concatenate(
+        [lax.dynamic_slice_in_dim(radial_green, degree_ids[k], 1) for k in range(held)]
+    )
     poles_out = radial_solve(
-        degree_ids, mom_in, radial_green, natoms, held, batches, cols_count
+        mom_in, green_own, natoms, held, batches, cols_count
     )
     poles = exchange(poles_out)
     returning = potential_pass(

time: 205 us -> 202 us (0.985)
  between operations: 1.02 us -> 4.84 us
  waiting for transfers between devices: 135 us -> 132 us
  Pallas kernels: 27.6 us -> 25 us
    all_to_all x3, waiting for transfers between devices: 135 us -> 132 us  [exchange(): return lax.all_to_all(parts, AXES, split_axis=0, concat_axis=0, tiled=True)]
where the time goes in v6:
time: 202 us
  waiting for transfers between devices  132 us (65%)
  Pallas kernels  25 us (12%)
  local copies, waits for them, and re-layouts  15.1 us (7%)
  starting transfers between devices  14.3 us (7%)
  blocking collectives  10.6 us (5%)
  between operations  4.84 us (2%)
    all_to_all x3, waiting for transfers between devices, exchange(): return lax.all_to_all(parts, AXES, split_axis=0, concat_axis=0, tiled=True)  132 us
    all_to_all x3, starting transfers between devices, exchange(): return lax.all_to_all(parts, AXES, split_axis=0, concat_axis=0, tiled=True)  14.3 us
    all_to_all x1, blocking collectives, exchange(): return lax.all_to_all(parts, AXES, split_axis=0, concat_axis=0, tiled=True)  10.6 us
    unnamed x23, local copies, waits for them, and re-layouts  10.5 us
    pallas_call x1, Pallas kernels, potential_pass(): pl.pallas_call(body, out_shape=jax.ShapeDtypeStruct((slot_count, blk, blk...  9.55 us
    pallas_call x1, Pallas kernels, density_pass(): pl.pallas_call(body, out_shape=(jax.ShapeDtypeStruct((SPARE * batches, 1,...  8.76 us
  transfers between devices with their start and end apart: 3, of which 3 were waited for; matrix products, arithmetic and copies ran while one was open for 8% of the time, Pallas kernels for 0%

profile of v6, /device:TPU:0, one launch (start us, length us, event | category | flops | bytes accessed | tf_op | source)
XLA Modules:
  0.0 201.8 jit_solution(13961932435675295778)
XLA Ops:
  0.6 3.0 %gather_tiles.1 = bf16[96,128,128]{2,1,0:T(8,128)(2,1)} custom-call(s32[3,1,32]{2,1,0:T(1,128)} %bitcast.16, bf16[32,128,128]{2,1,0:T(8,128)(2,1)} %tiles_ref.1), custom_call_target="tpu_custom_call" | custom-call | tf_op jit(solution)/shard_map/gather_tiles/pallas_call | solution.py:82
  3.6 0.0 copy-start.8
  3.6 0.0 copy-start.9
  3.6 0.0 copy-start.7
  3.6 7.3 %all-to-all-start = ((bf16[32,3,128,128]{3,2,1,0:T(8,128)(2,1)}), bf16[32,3,128,128]{3,2,1,0:T(8,128)(2,1)S(1)}, u32[]{:S(2)}, u32[]{:S(2)}) async-start(bf16[32,3,128,128]{3,2,1,0:T(8,128)(2,1)} %bitcast.21), calls=%async_computation | async-start | bytes 6291456 | tf_op jit(solution)/shard_map/all_to_all | solution.py:379
  11.0 0.2 fusion
  11.2 0.6 fusion.1
  14.4 0.0 copy-done.8
  14.4 0.1 copy.26
  14.5 0.1 copy.25
  14.6 0.1 reshape.35
  14.7 8.8 %copy.27 = bf16[2,2048,768]{1,2,0:T(8,128)(2,1)} copy(bf16[2,2048,768]{2,1,0:T(8,128)(2,1)} %param.12) | data formatting | bytes 12582912 | tf_op args[2]
  23.4 1.6 copy.28
  25.1 0.0 copy-done.6
  25.1 0.0 copy-start
  25.1 0.0 copy-start.1
  25.1 2.1 %pad.4.harm_hbm = f32[6,64,2048]{2,1,0:T(8,128)} pad(f32[2,49,2048]{2,1,0:T(8,128)S(1)} %copy.28, f32[]{:T(128)} %constant.4.clone.1), padding=0_4x0_15x0_0 | pad | bytes 3948548 | tf_op jit(solution)/shard_map/jit(_pad)/pad | solution.py:412
  28.5 0.1 pad_add_fusion.plan_hbm
  28.6 53.7 %all-to-all-done = bf16[32,3,128,128]{3,2,1,0:T(8,128)(2,1)S(1)} async-done(((bf16[32,3,128,128]{3,2,1,0:T(8,128)(2,1)}), bf16[32,3,128,128]{3,2,1,0:T(8,128)(2,1)S(1)}, u32[]{:S(2)}, u32[]{:S(2)}) %all-to-all-start) | async-done | bytes 3145760 | tf_op jit(solution)/shard_map/all_to_all | solution.py:379
  82.3 8.8 %density_pass.1 = (f32[512,1,2048]{2,1,0:T(1,128)}, f32[32,6,128]{2,1,0:T(8,128)}) custom-call(s32[2,38]{1,0:T(2,128)S(1)} %pad_add_fusion.plan_hbm, bf16[96,128,128]{2,1,0:T(8,128)(2,1)S(1)} %bitcast.15, bf16[2,768,2048]{2,1,0:T(8,128)(2,1)} %bitcast.18, f32[6,64,2048]{2,1,0:T(8,128)} %pad.4.harm_hbm, f32[2,1,2048]{2,1,0:T(1,128)S(1)} %broadcast_in_dim.16.wts_hbm, ...), custom_call_target="tpu_custom_call" | custom-call | tf_op jit(solution)/shard_map/density_pass/pallas_call | solution.py:200
  91.1 4.0 %all-to-all-start.1 = ((f32[32,6,128]{2,1,0:T(8,128)}), f32[32,6,128]{2,1,0:T(8,128)S(1)}, u32[]{:S(2)}, u32[]{:S(2)}) async-start(f32[32,6,128]{2,1,0:T(8,128)} %get-tuple-element.4), calls=%async_computation.1 | async-start | bytes 262144 | tf_op jit(solution)/shard_map/all_to_all | solution.py:379
  95.1 0.9 constant_dynamic-slice_fusion.1
  96.1 7.3 %all-to-all-done.1.got = f32[32,6,128]{2,1,0:T(8,128)S(1)} async-done(((f32[32,6,128]{2,1,0:T(8,128)}), f32[32,6,128]{2,1,0:T(8,128)S(1)}, u32[]{:S(2)}, u32[]{:S(2)}) %all-to-all-start.1) | async-done | bytes 98336 | tf_op jit(solution)/shard_map/all_to_all | solution.py:379
  103.3 1.1 radial_solve.1
  104.5 10.6 %all_to_all.20.got = f32[32,8,128]{2,1,0:T(8,128)} all-to-all(f32[32,8,128]{2,1,0:T(8,128)S(1)} %radial_solve.1), channel_id=1, replica_groups=mesh['row'=4,'col'=8] {'row','col'}, dimensions={0} | all-to-all | bytes 262144 | tf_op jit(solution)/shard_map/all_to_all | solution.py:379
  115.0 9.5 %potential_pass.1 = bf16[96,128,128]{2,1,0:T(8,128)(2,1)} custom-call(s32[2,38]{1,0:T(2,128)} %copy-done.2, f32[32,8,128]{2,1,0:T(8,128)} %all_to_all.20.got, f32[512,1,2048]{2,1,0:T(1,128)} %get-tuple-element.5.rho_hbm, bf16[2,768,2048]{2,1,0:T(8,128)(2,1)} %bitcast.19, f32[6,64,2048]{2,1,0:T(8,128)} %pad.4.harm_hbm, f32[2,1,2048]{2,1,0:T(1,128)} %copy-done, ...), custom_call_target="tpu_custom_call" | custom-call | tf_op jit(solution)/shard_map/potential_pass/pallas_call | solution.py:354
  124.6 0.0 copy-start.3
  124.6 2.9 %all-to-all-start.3 = ((bf16[32,3,128,128]{3,2,1,0:T(8,128)(2,1)}), bf16[32,3,128,128]{3,2,1,0:T(8,128)(2,1)S(1)}, u32[]{:S(2)}, u32[]{:S(2)}) async-start(bf16[32,3,128,128]{3,2,1,0:T(8,128)(2,1)} %bitcast.20), calls=%async_computation.3 | async-start | bytes 6291456 | tf_op jit(solution)/shard_map/all_to_all | solution.py:379
  127.6 0.0 copy-done.4
  127.6 0.6 slice.17
  128.3 70.7 %all-to-all-done.3 = bf16[32,3,128,128]{3,2,1,0:T(8,128)(2,1)S(1)} async-done(((bf16[32,3,128,128]{3,2,1,0:T(8,128)(2,1)}), bf16[32,3,128,128]{3,2,1,0:T(8,128)(2,1)S(1)}, u32[]{:S(2)}, u32[]{:S(2)}) %all-to-all-start.3) | async-done | bytes 3145760 | tf_op jit(solution)/shard_map/all_to_all | solution.py:379
  199.0 2.6 %sum_tiles.1 = f32[32,128,128]{2,1,0:T(8,128)} custom-call(s32[3,1,32]{2,1,0:T(1,128)S(1)} %bitcast.17, bf16[96,128,128]{2,1,0:T(8,128)(2,1)S(1)} %bitcast.14), custom_call_target="tpu_custom_call" | custom-call | tf_op jit(solution)/shard_map/sum_tiles/pallas_call | solution.py:115
  (19 shorter events, 0.1 us)
Async XLA Ops:
  3.6 10.8 %copy-start.8 = (s32[2]{0:T(128)S(1)}, s32[2]{0:T(128)}, u32[]{:S(2)}) copy-start(s32[2]{0:T(128)} %param.18) | copy-start | bytes 28
  3.6 10.9 %copy-start.9 = (s32[2]{0:T(128)S(1)}, s32[2]{0:T(128)}, u32[]{:S(2)}) copy-start(s32[2]{0:T(128)} %param.13) | copy-start | bytes 28
  3.6 10.9 %copy-start.7 = (s32[2,6,6]{2,0,1:T(2,128)S(1)}, s32[2,6,6]{2,0,1:T(2,128)}, u32[]{:S(2)}) copy-start(s32[2,6,6]{2,0,1:T(2,128)} %param.14) | copy-start | bytes 868
  3.6 78.7 %all-to-all-start = ((bf16[32,3,128,128]{3,2,1,0:T(8,128)(2,1)}), bf16[32,3,128,128]{3,2,1,0:T(8,128)(2,1)S(1)}, u32[]{:S(2)}, u32[]{:S(2)}) async-start(bf16[32,3,128,128]{3,2,1,0:T(8,128)(2,1)} %bitcast.21), calls=%async_computation | async-start | bytes 6291456 | tf_op jit(solution)/shard_map/all_to_all | solution.py:379
  14.6 10.4 %copy-start.5 = (f32[2,2048]{1,0:T(2,128)S(1)}, f32[2,2048]{1,0:T(2,128)}, u32[]{:S(2)}) copy-start(f32[2,2048]{1,0:T(2,128)} %param.15) | copy-start | bytes 49156
  14.7 10.4 %copy-start.6 = (s32[2,2048]{1,0:T(2,128)S(1)}, s32[2,2048]{1,0:T(2,128)}, u32[]{:S(2)}) copy-start(s32[2,2048]{1,0:T(2,128)} %param.17) | copy-start | bytes 49156
  25.1 66.0 %copy-start = (f32[2,1,2048]{2,1,0:T(1,128)}, f32[2,1,2048]{2,1,0:T(1,128)S(1)}, u32[]{:S(2)}) copy-start(f32[2,1,2048]{2,1,0:T(1,128)S(1)} %broadcast_in_dim.16.wts_hbm) | copy-start | bytes 49156
  25.1 65.9 %copy-start.1 = (s32[2,1,2048]{2,1,0:T(1,128)}, s32[2,1,2048]{2,1,0:T(1,128)S(1)}, u32[]{:S(2)}) copy-start(s32[2,1,2048]{2,1,0:T(1,128)S(1)} %broadcast_in_dim.17.shell_hbm) | copy-start | bytes 49156
  28.6 62.5 %copy-start.2 = (s32[2,38]{1,0:T(2,128)}, s32[2,38]{1,0:T(2,128)S(1)}, u32[]{:S(2)}) copy-start(s32[2,38]{1,0:T(2,128)S(1)} %pad_add_fusion.plan_hbm) | copy-start | bytes 916
  91.1 12.2 %all-to-all-start.1 = ((f32[32,6,128]{2,1,0:T(8,128)}), f32[32,6,128]{2,1,0:T(8,128)S(1)}, u32[]{:S(2)}, u32[]{:S(2)}) async-start(f32[32,6,128]{2,1,0:T(8,128)} %get-tuple-element.4), calls=%async_computation.1 | async-start | bytes 262144 | tf_op jit(solution)/shard_map/all_to_all | solution.py:379
  124.6 3.0 %copy-start.4 = (f32[32,8,128]{2,1,0:T(8,128)S(1)}, f32[32,8,128]{2,1,0:T(8,128)}, u32[]{:S(2)}) copy-start(f32[32,8,128]{2,1,0:T(8,128)} %all_to_all.20.got) | copy-start | bytes 393220
  124.6 74.4 %copy-start.3 = (s32[1,32,3]{1,0,2:T(1,128)S(1)}, s32[1,32,3]{1,0,2:T(1,128)}, u32[]{:S(2)}) copy-start(s32[1,32,3]{1,0,2:T(1,128)} %param.11) | copy-start | bytes 1156
  124.6 74.4 %all-to-all-start.3 = ((bf16[32,3,128,128]{3,2,1,0:T(8,128)(2,1)}), bf16[32,3,128,128]{3,2,1,0:T(8,128)(2,1)S(1)}, u32[]{:S(2)}, u32[]{:S(2)}) async-start(bf16[32,3,128,128]{3,2,1,0:T(8,128)(2,1)} %bitcast.20), calls=%async_computation.3 | async-start | bytes 6291456 | tf_op jit(solution)/shard_map/all_to_all | solution.py:379

commit v7 on v6

--- a/solution.py
+++ b/solution.py
@@ -48,11 +48,7 @@
 
 def plan_views(plan, blocks):
     pairs = blocks * blocks
-    return (
-        lambda b: plan[b, pairs],
-        lambda b, pair: plan[b, pair],
-        lambda b: plan[b, pairs + 1],
-    )
+    return lambda b: plan[b, pairs], lambda b, pair: plan[b, pair]
 
 
 def gather_tiles(tile_ids, tiles):
@@ -129,7 +125,7 @@
     blocks = span // blk
     rows = harmonics.shape[1]
     held, radial = share
-    lines = (held + 1) * batches
+    lines = held * batches
 
     def body(plan_hbm, recv, phi_hbm, harm_hbm, wts_hbm, shell_hbm, rho_hbm, send,
              phi, harm, rho, matrix, mom_keep, plan_keep, wts, shell,
@@ -144,7 +140,7 @@
         ]
         for load in [plan_load] + phi_loads[:1] + point_loads + phi_loads[1:] + harm_loads:
             load.start()
-        act, slot_ids, atom_ids = plan_views(plan_keep, blocks)
+        act, slot_ids = plan_views(plan_keep, blocks)
         plan_load.wait()
 
         for b in range(batches):
@@ -162,11 +158,6 @@
                     @pl.when(jnp.logical_not(live))
                     def _(spot=spot):
                         matrix[spot] = jnp.zeros((blk, blk), BF16)
-
-        for b in range(batches):
-            send[:, pl.ds(held * batches + b, 1), :] = jnp.full(
-                (devices, 1, radial), atom_ids(b).astype(F32), F32
-            )
 
         def moments(b):
             weighted = harm[b] * (wts[b] * rho[b])
@@ -189,10 +180,9 @@
             rho[b] = jnp.sum(product * phi[b].astype(F32), axis=0, keepdims=True)
             rho_stores[b].start()
 
-        for load in point_loads:
+        for load in point_loads + harm_loads:
             load.wait()
         for b in range(batches):
-            harm_loads[b].wait()
             moments(b)
         for store in rho_stores:
             store.wait()
@@ -224,11 +214,11 @@
     )(plan, received, basis_t, harmonics, weights, shells)
 
 
-def radial_solve(arrived, green, natoms, held, batches, cols_count):
+def radial_solve(arrived, green, atoms, natoms, held, batches, cols_count):
     devices, lines, radial = arrived.shape
     rows_out = (batches + ATOM_COL) * held
 
-    def body(got, green_hbm, out, flat, green, sems):
+    def body(got, green_hbm, atom_ref, out, flat, green, sems):
         loads = [
             pltpu.make_async_copy(green_hbm.at[k], green.at[k], sems.at[k]) for k in range(held)
         ]
@@ -237,13 +227,13 @@
         for r in range(lines):
             for d in range(devices):
                 flat[r, pl.ds(d, 1), :] = got[d, pl.ds(r, 1), :]
-        atom_of = [flat[held * batches + b] for b in range(batches)]
+        atom_of = [atom_ref[b] for b in range(batches)]
         for k in range(held):
             sums = []
             for a in range(natoms):
                 total = jnp.zeros((devices, radial), F32)
                 for b in range(batches):
-                    total = total + jnp.where(atom_of[b] == float(a), flat[k * batches + b], 0.0)
+                    total = total + jnp.where(atom_of[b] == a, flat[k * batches + b], 0.0)
                 sums.append(jnp.sum(total, axis=0, keepdims=True))
             atom_mom = jnp.concatenate(sums, axis=0)
             loads[k].wait()
@@ -257,7 +247,7 @@
             for b in range(batches):
                 picked = jnp.zeros((devices, radial), F32)
                 for a in range(natoms):
-                    picked = jnp.where(atom_of[b] == float(a), solved[a : a + 1, :], picked)
+                    picked = jnp.where(atom_of[b] == a, solved[a : a + 1, :], picked)
                 for d in range(devices):
                     out[d, pl.ds(b * held + k, 1), :] = picked[d : d + 1, :]
             for own in range(ATOM_COL):
@@ -268,7 +258,7 @@
     return pl.pallas_call(
         body,
         out_shape=jax.ShapeDtypeStruct((devices, rows_out, radial), F32),
-        in_specs=[VMEM, HBM],
+        in_specs=[VMEM, HBM, VMEM],
         out_specs=VMEM,
         scratch_shapes=[
             pltpu.VMEM((lines, devices, radial), F32),
@@ -277,7 +267,7 @@
         ],
         compiler_params=params(53.5),
         name="radial_solve",
-    )(arrived, green)
+    )(arrived, green, atoms)
 
 
 def potential_pass(plan, poles, rho, basis_t, harmonics, weights, shells, slot_count, blk, held):
@@ -300,7 +290,7 @@
         ]
         for load in rho_loads + point_loads + harm_loads + phi_loads:
             load.start()
-        act, slot_ids, _ = plan_views(plan_keep, blocks)
+        act, slot_ids = plan_views(plan_keep, blocks)
 
         out[...] = jnp.zeros_like(out)
         if held * devices < rows:
@@ -373,6 +363,18 @@
         compiler_params=params(62),
         name="potential_pass",
     )(plan, poles, rho, basis_t, harmonics, weights, shells)
+
+
+def gathered(values, devices):
+    me = lax.axis_index(AXES)
+    reach = 1
+    while reach < devices:
+        other = lax.ppermute(values, AXES, [(d, d ^ reach) for d in range(devices)])
+        upper = (me & reach) > 0
+        low, high = jnp.where(upper, other, values), jnp.where(upper, values, other)
+        values = jnp.concatenate([low, high])
+        reach *= 2
+    return values
 
 
 def exchange(parts):
@@ -405,7 +407,10 @@
 
     tile_ids = jnp.transpose(send_list, (2, 0, 1))
     outgoing = gather_tiles(tile_ids, density_tiles)
+    outgoing, own_atoms = lax.optimization_barrier((outgoing, batch_atom))
     arrived = exchange(outgoing.reshape(devices, capacity, blk, blk))
+    all_atoms = gathered(own_atoms, devices).reshape(devices, batches)
+    atom_rows = jnp.broadcast_to(all_atoms.T[:, :, None], (batches, devices, radial))
     received = arrived.reshape(slot_count, blk, blk)
 
     basis_t = jnp.transpose(basis_values, (0, 2, 1))
@@ -413,7 +418,7 @@
     weights = point_weights[:, None, :]
     shells = shell_index[:, None, :]
     plan = jnp.concatenate(
-        [touch_slots.reshape(batches, -1), active_blocks[:, None], batch_atom[:, None]], axis=1
+        [touch_slots.reshape(batches, -1), active_blocks[:, None]], axis=1
     )
 
     rho, mom_out = density_pass(
@@ -427,7 +432,7 @@
         [lax.dynamic_slice_in_dim(radial_green, degree_ids[k], 1) for k in range(held)]
     )
     poles_out = radial_solve(
-        mom_in, green_own, natoms, held, batches, cols_count
+        mom_in, green_own, atom_rows, natoms, held, batches, cols_count
     )
     poles = exchange(poles_out)
     returning = potential_pass(

time: 202 us -> 201 us (level)
  waiting for transfers between devices: 132 us -> 119 us
  starting transfers between devices: 14.3 us -> 23.7 us
  local copies, waits for them, and re-layouts: 15.1 us -> 17.4 us
    all_to_all x3, waiting for transfers between devices: 132 us -> 92.7 us  [exchange(): return lax.all_to_all(parts, AXES, split_axis=0, concat_axis=0, tiled=True)]
    ppermute x0 -> x5, waiting for transfers between devices: none -> 25.8 us  [gathered(): other = lax.ppermute(values, AXES, [(d, d ^ reach) for d in range(devices)])]
    ppermute x0 -> x5, starting transfers between devices: none -> 9.39 us  [gathered(): other = lax.ppermute(values, AXES, [(d, d ^ reach) for d in range(devices)])]
  transfers between devices with their start and end apart: 3 -> 8, of which waited for: 3 -> 6; matrix products, arithmetic and copies ran while one was open for 8% -> 9% of each run, Pallas kernels for 0% -> 4%
where the time goes in v7:
time: 201 us
  waiting for transfers between devices  119 us (59%)
  Pallas kernels  24.7 us (12%)
  starting transfers between devices  23.7 us (12%)
  local copies, waits for them, and re-layouts  17.4 us (9%)
  blocking collectives  10.6 us (5%)
  between operations  4.85 us (2%)
    all_to_all x3, waiting for transfers between devices, exchange(): return lax.all_to_all(parts, AXES, split_axis=0, concat_axis=0, tiled=True)  92.7 us
    ppermute x5, waiting for transfers between devices, gathered(): other = lax.ppermute(values, AXES, [(d, d ^ reach) for d in range(devices)])  25.8 us
    all_to_all x3, starting transfers between devices, exchange(): return lax.all_to_all(parts, AXES, split_axis=0, concat_axis=0, tiled=True)  14.3 us
    unnamed x23, local copies, waits for them, and re-layouts  11.4 us
    all_to_all x1, blocking collectives, exchange(): return lax.all_to_all(parts, AXES, split_axis=0, concat_axis=0, tiled=True)  10.6 us
    pallas_call x1, Pallas kernels, potential_pass(): pl.pallas_call(body, out_shape=jax.ShapeDtypeStruct((slot_count, blk, blk...  9.53 us
    ppermute x5, starting transfers between devices, gathered(): other = lax.ppermute(values, AXES, [(d, d ^ reach) for d in range(devices)])  9.39 us
    pallas_call x1, Pallas kernels, density_pass(): pl.pallas_call(body, out_shape=(jax.ShapeDtypeStruct((SPARE * batches, 1,...  8.43 us
  transfers between devices with their start and end apart: 8, of which 6 were waited for; matrix products, arithmetic and copies ran while one was open for 9% of the time, Pallas kernels for 4%

profile of v7, /device:TPU:0, one launch (start us, length us, event | category | flops | bytes accessed | tf_op | source)
XLA Modules:
  0.0 200.7 jit_solution(11946855278173882149)
XLA Ops:
  0.6 3.0 %gather_tiles.1 = bf16[96,128,128]{2,1,0:T(8,128)(2,1)} custom-call(s32[3,1,32]{2,1,0:T(1,128)} %bitcast.17, bf16[32,128,128]{2,1,0:T(8,128)(2,1)} %tiles_ref.1), custom_call_target="tpu_custom_call" | custom-call | tf_op jit(solution)/shard_map/gather_tiles/pallas_call | solution.py:78
  3.7 7.3 %all-to-all-start = ((bf16[32,3,128,128]{3,2,1,0:T(8,128)(2,1)}), bf16[32,3,128,128]{3,2,1,0:T(8,128)(2,1)S(1)}, u32[]{:S(2)}, u32[]{:S(2)}) async-start(bf16[32,3,128,128]{3,2,1,0:T(8,128)(2,1)} %bitcast.22), calls=%async_computation | async-start | bytes 6291456 | tf_op jit(solution)/shard_map/all_to_all | solution.py:381
  11.0 0.3 collective-permute-start
  11.3 0.2 fusion
  11.5 0.6 fusion.1
  14.7 0.1 copy.32
  14.8 0.1 reshape.39
  14.8 8.8 %copy.33 = bf16[2,2048,768]{1,2,0:T(8,128)(2,1)} copy(bf16[2,2048,768]{2,1,0:T(8,128)(2,1)} %param.12) | data formatting | bytes 12582912 | tf_op args[2]
  23.6 2.5 %copy.34 = f32[2,49,2048]{2,1,0:T(8,128)} copy(f32[2,49,2048]{2,0,1:T(2,128)} %param.16) | data formatting | bytes 1605632 | tf_op args[6]
  27.6 0.9 constant_dynamic-slice_fusion.1
  28.6 1.7 collective-permute-start.1
  30.3 1.9 collective-permute-done.1
  32.3 1.6 collective-permute-start.2
  34.0 1.9 collective-permute-done.2
  36.0 1.7 collective-permute-start.3
  37.7 3.3 %pad.4.harm_hbm = f32[6,64,2048]{2,1,0:T(8,128)} pad(f32[2,49,2048]{2,1,0:T(8,128)} %copy.34, f32[]{:T(128)} %constant.11.clone.1), padding=0_4x0_15x0_0 | pad | bytes 3948548 | tf_op jit(solution)/shard_map/jit(_pad)/pad | solution.py:417
  41.0 22.0 %collective-permute-done.3 = s32[16]{0:T(128)S(1)} collective-permute-done((s32[16]{0:T(128)S(1)}, s32[16]{0:T(128)S(1)}, u32[]{:S(2)}, u32[]{:S(2)}) %collective-permute-start.3) | collective-permute-done | bytes 96 | tf_op jit(solution)/shard_map/ppermute | solution.py:372
  63.2 4.1 %collective-permute-start.4 = (s32[32]{0:T(128)S(1)}, s32[32]{0:T(128)S(1)}, u32[]{:S(2)}, u32[]{:S(2)}) collective-permute-start(s32[32]{0:T(128)S(1)} %pad_add_fusion.4), channel_id=1, source_target_pairs={{0,16},{1,17},{2,18},{3,19},{4,20},{5,21},{6,22},{7,23},{8,24},{9,... | collective-permute-start | bytes 392 | tf_op jit(solution)/shard_map/ppermute | solution.py:372
  67.3 15.1 %all-to-all-done = bf16[32,3,128,128]{3,2,1,0:T(8,128)(2,1)S(1)} async-done(((bf16[32,3,128,128]{3,2,1,0:T(8,128)(2,1)}), bf16[32,3,128,128]{3,2,1,0:T(8,128)(2,1)S(1)}, u32[]{:S(2)}, u32[]{:S(2)}) %all-to-all-start) | async-done | bytes 3145760 | tf_op jit(solution)/shard_map/all_to_all | solution.py:381
  82.3 8.4 %density_pass.1 = (f32[512,1,2048]{2,1,0:T(1,128)}, f32[32,4,128]{2,1,0:T(4,128)}) custom-call(s32[2,37]{1,0:T(2,128)S(1)} %pad_add_fusion.plan_hbm, bf16[96,128,128]{2,1,0:T(8,128)(2,1)S(1)} %bitcast.16, bf16[2,768,2048]{2,1,0:T(8,128)(2,1)} %bitcast.19, f32[6,64,2048]{2,1,0:T(8,128)} %pad.4.harm_hbm, f32[2,1,2048]{2,1,0:T(1,128)S(1)} %broadcast_in_dim.18.wts_hbm, ...), custom_call_target="tpu_custom_call" | custom-call | tf_op jit(solution)/shard_map/density_pass/pallas_call | solution.py:190
  90.8 4.0 %all-to-all-start.1 = ((f32[32,4,128]{2,1,0:T(4,128)}), f32[32,4,128]{2,1,0:T(4,128)S(1)}, u32[]{:S(2)}, u32[]{:S(2)}) async-start(f32[32,4,128]{2,1,0:T(4,128)} %get-tuple-element.7), calls=%async_computation.1 | async-start | bytes 131072 | tf_op jit(solution)/shard_map/all_to_all | solution.py:381
  94.9 0.1 concatenate.33
  95.0 0.1 copy.36
  95.2 0.1 copy.35
  95.4 6.9 %all-to-all-done.1.got = f32[32,4,128]{2,1,0:T(4,128)S(1)} async-done(((f32[32,4,128]{2,1,0:T(4,128)}), f32[32,4,128]{2,1,0:T(4,128)S(1)}, u32[]{:S(2)}, u32[]{:S(2)}) %all-to-all-start.1) | async-done | bytes 65568 | tf_op jit(solution)/shard_map/all_to_all | solution.py:381
  102.3 1.1 radial_solve.1
  103.4 10.6 %all_to_all.20.got = f32[32,8,128]{2,1,0:T(8,128)} all-to-all(f32[32,8,128]{2,1,0:T(8,128)S(1)} %radial_solve.1), channel_id=1, replica_groups=mesh['row'=4,'col'=8] {'row','col'}, dimensions={0} | all-to-all | bytes 262144 | tf_op jit(solution)/shard_map/all_to_all | solution.py:381
  114.0 9.5 %potential_pass.1 = bf16[96,128,128]{2,1,0:T(8,128)(2,1)} custom-call(s32[2,37]{1,0:T(2,128)} %copy-done.2, f32[32,8,128]{2,1,0:T(8,128)} %all_to_all.20.got, f32[512,1,2048]{2,1,0:T(1,128)} %get-tuple-element.9.rho_hbm, bf16[2,768,2048]{2,1,0:T(8,128)(2,1)} %bitcast.20, f32[6,64,2048]{2,1,0:T(8,128)} %pad.4.harm_hbm, f32[2,1,2048]{2,1,0:T(1,128)} %copy-done, ...), custom_call_target="tpu_custom_call" | custom-call | tf_op jit(solution)/shard_map/potential_pass/pallas_call | solution.py:344
  123.6 2.9 %all-to-all-start.3 = ((bf16[32,3,128,128]{3,2,1,0:T(8,128)(2,1)}), bf16[32,3,128,128]{3,2,1,0:T(8,128)(2,1)S(1)}, u32[]{:S(2)}, u32[]{:S(2)}) async-start(bf16[32,3,128,128]{3,2,1,0:T(8,128)(2,1)} %bitcast.21), calls=%async_computation.3 | async-start | bytes 6291456 | tf_op jit(solution)/shard_map/all_to_all | solution.py:381
  126.6 0.6 slice.17
  127.2 70.7 %all-to-all-done.3 = bf16[32,3,128,128]{3,2,1,0:T(8,128)(2,1)S(1)} async-done(((bf16[32,3,128,128]{3,2,1,0:T(8,128)(2,1)}), bf16[32,3,128,128]{3,2,1,0:T(8,128)(2,1)S(1)}, u32[]{:S(2)}, u32[]{:S(2)}) %all-to-all-start.3) | async-done | bytes 3145760 | tf_op jit(solution)/shard_map/all_to_all | solution.py:381
  197.9 2.6 %sum_tiles.1 = f32[32,128,128]{2,1,0:T(8,128)} custom-call(s32[3,1,32]{2,1,0:T(1,128)S(1)} %bitcast.18, bf16[96,128,128]{2,1,0:T(8,128)(2,1)S(1)} %bitcast.15), custom_call_target="tpu_custom_call" | custom-call | tf_op jit(solution)/shard_map/sum_tiles/pallas_call | solution.py:111
  (43 shorter events, 1.1 us)
Async XLA Ops:
  3.6 7.4 %copy-start.8 = (s32[2]{0:T(128)S(1)}, s32[2]{0:T(128)}, u32[]{:S(2)}) copy-start(s32[2]{0:T(128)} %param.18) | copy-start | bytes 28
  3.6 11.0 %copy-start.9 = (s32[2]{0:T(128)S(1)}, s32[2]{0:T(128)}, u32[]{:S(2)}) copy-start(s32[2]{0:T(128)} %param.13) | copy-start | bytes 28
  3.6 11.1 %copy-start.7 = (s32[2,6,6]{2,0,1:T(2,128)S(1)}, s32[2,6,6]{2,0,1:T(2,128)}, u32[]{:S(2)}) copy-start(s32[2,6,6]{2,0,1:T(2,128)} %param.14) | copy-start | bytes 868
  3.7 78.7 %all-to-all-start = ((bf16[32,3,128,128]{3,2,1,0:T(8,128)(2,1)}), bf16[32,3,128,128]{3,2,1,0:T(8,128)(2,1)S(1)}, u32[]{:S(2)}, u32[]{:S(2)}) async-start(bf16[32,3,128,128]{3,2,1,0:T(8,128)(2,1)} %bitcast.22), calls=%async_computation | async-start | bytes 6291456 | tf_op jit(solution)/shard_map/all_to_all | solution.py:381
  11.0 17.5 %collective-permute-start = (s32[2]{0:T(128)S(1)}, s32[2]{0:T(128)S(1)}, u32[]{:S(2)}, u32[]{:S(2)}) collective-permute-start(s32[2]{0:T(128)S(1)} %copy-done.8), channel_id=1, source_target_pairs={{0,1},{1,0},{2,3},{3,2},{4,5},{5,4},{6,7},{7,6},{8,9},{9,8},{10,11... | collective-permute-start | bytes 32 | tf_op jit(solution)/shard_map/ppermute | solution.py:372
  14.8 11.3 %copy-start.5 = (f32[2,2048]{1,0:T(2,128)S(1)}, f32[2,2048]{1,0:T(2,128)}, u32[]{:S(2)}) copy-start(f32[2,2048]{1,0:T(2,128)} %param.15) | copy-start | bytes 49156
  14.8 11.3 %copy-start.6 = (s32[2,2048]{1,0:T(2,128)S(1)}, s32[2,2048]{1,0:T(2,128)}, u32[]{:S(2)}) copy-start(s32[2,2048]{1,0:T(2,128)} %param.17) | copy-start | bytes 49156
  26.2 64.6 %copy-start = (f32[2,1,2048]{2,1,0:T(1,128)}, f32[2,1,2048]{2,1,0:T(1,128)S(1)}, u32[]{:S(2)}) copy-start(f32[2,1,2048]{2,1,0:T(1,128)S(1)} %broadcast_in_dim.18.wts_hbm) | copy-start | bytes 49156
  26.2 64.6 %copy-start.1 = (s32[2,1,2048]{2,1,0:T(1,128)}, s32[2,1,2048]{2,1,0:T(1,128)S(1)}, u32[]{:S(2)}) copy-start(s32[2,1,2048]{2,1,0:T(1,128)S(1)} %broadcast_in_dim.19.shell_hbm) | copy-start | bytes 49156
  27.6 63.2 %copy-start.2 = (s32[2,37]{1,0:T(2,128)}, s32[2,37]{1,0:T(2,128)S(1)}, u32[]{:S(2)}) copy-start(s32[2,37]{1,0:T(2,128)S(1)} %pad_add_fusion.plan_hbm) | copy-start | bytes 892
  28.6 3.6 %collective-permute-start.1 = (s32[4]{0:T(128)S(1)}, s32[4]{0:T(128)S(1)}, u32[]{:S(2)}, u32[]{:S(2)}) collective-permute-start(s32[4]{0:T(128)S(1)} %pad_add_fusion.1), channel_id=1, source_target_pairs={{0,2},{1,3},{2,0},{3,1},{4,6},{5,7},{6,4},{7,5},{8,10},{9,11},{10,... | collective-permute-start | bytes 56 | tf_op jit(solution)/shard_map/ppermute | solution.py:372
  32.3 3.6 %collective-permute-start.2 = (s32[8]{0:T(128)S(1)}, s32[8]{0:T(128)S(1)}, u32[]{:S(2)}, u32[]{:S(2)}) collective-permute-start(s32[8]{0:T(128)S(1)} %pad_add_fusion.2), channel_id=1, source_target_pairs={{0,4},{1,5},{2,6},{3,7},{4,0},{5,1},{6,2},{7,3},{8,12},{9,13},{10,... | collective-permute-start | bytes 104 | tf_op jit(solution)/shard_map/ppermute | solution.py:372
  36.0 27.0 %collective-permute-start.3 = (s32[16]{0:T(128)S(1)}, s32[16]{0:T(128)S(1)}, u32[]{:S(2)}, u32[]{:S(2)}) collective-permute-start(s32[16]{0:T(128)S(1)} %pad_add_fusion.3), channel_id=1, source_target_pairs={{0,8},{1,9},{2,10},{3,11},{4,12},{5,13},{6,14},{7,15},{8,0},{9,1},... | collective-permute-start | bytes 200 | tf_op jit(solution)/shard_map/ppermute | solution.py:372
  63.2 31.7 %collective-permute-start.4 = (s32[32]{0:T(128)S(1)}, s32[32]{0:T(128)S(1)}, u32[]{:S(2)}, u32[]{:S(2)}) collective-permute-start(s32[32]{0:T(128)S(1)} %pad_add_fusion.4), channel_id=1, source_target_pairs={{0,16},{1,17},{2,18},{3,19},{4,20},{5,21},{6,22},{7,23},{8,24},{9,... | collective-permute-start | bytes 392 | tf_op jit(solution)/shard_map/ppermute | solution.py:372
  90.8 11.4 %all-to-all-start.1 = ((f32[32,4,128]{2,1,0:T(4,128)}), f32[32,4,128]{2,1,0:T(4,128)S(1)}, u32[]{:S(2)}, u32[]{:S(2)}) async-start(f32[32,4,128]{2,1,0:T(4,128)} %get-tuple-element.7), calls=%async_computation.1 | async-start | bytes 131072 | tf_op jit(solution)/shard_map/all_to_all | solution.py:381
  123.5 3.0 %copy-start.4 = (f32[32,8,128]{2,1,0:T(8,128)S(1)}, f32[32,8,128]{2,1,0:T(8,128)}, u32[]{:S(2)}) copy-start(f32[32,8,128]{2,1,0:T(8,128)} %all_to_all.20.got) | copy-start | bytes 393220
  123.5 74.4 %copy-start.3 = (s32[1,32,3]{1,0,2:T(1,128)S(1)}, s32[1,32,3]{1,0,2:T(1,128)}, u32[]{:S(2)}) copy-start(s32[1,32,3]{1,0,2:T(1,128)} %param.11) | copy-start | bytes 1156
  123.6 74.4 %all-to-all-start.3 = ((bf16[32,3,128,128]{3,2,1,0:T(8,128)(2,1)}), bf16[32,3,128,128]{3,2,1,0:T(8,128)(2,1)S(1)}, u32[]{:S(2)}, u32[]{:S(2)}) async-start(bf16[32,3,128,128]{3,2,1,0:T(8,128)(2,1)} %bitcast.21), calls=%async_computation.3 | async-start | bytes 6291456 | tf_op jit(solution)/shard_map/all_to_all | solution.py:381

commit v8 on v7

--- a/solution.py
+++ b/solution.py
@@ -277,8 +277,8 @@
     devices, lines, radial = poles.shape
     wide = 2 * blk if blocks % 2 == 0 else blk
 
-    def body(plan_hbm, got, rho_hbm, phi_hbm, harm_hbm, wts_hbm, shell_hbm, out,
-             phi, harm, rho, scaled, poles_keep, plan_keep, wts, shell,
+    def body(plan_hbm, got, rho_hbm, phi_hbm, harm_hbm, wts_hbm, shell_hbm, out_hbm,
+             out, last, last_sems, phi, harm, rho, scaled, poles_keep, plan_keep, wts, shell,
              phi_sems, harm_sems, rho_sems, sems):
         phi_loads = loads_of(phi_hbm, phi, phi_sems)
         harm_loads = loads_of(harm_hbm, harm, harm_sems)
@@ -320,12 +320,33 @@
         def keep(b, i, j, tile):
             live = (i < act(b)) & (j < act(b))
             slot = jnp.clip(slot_ids(b, i * blocks + j), 0, slot_count - 1)
-            out[slot] = jnp.where(live, tile, out[slot])
-
+            if b < batches - 1:
+                out[slot] = jnp.where(live, tile, out[slot])
+            else:
+                last[i * blocks + j] = tile
+
+        def last_tiles(act_on):
+            for i in range(blocks):
+                for j in range(blocks):
+                    pair = i * blocks + j
+
+                    @pl.when((i < act(batches - 1)) & (j < act(batches - 1)))
+                    def _(pair=pair):
+                        slot = jnp.clip(slot_ids(batches - 1, pair), 0, slot_count - 1)
+                        act_on(
+                            pltpu.make_async_copy(
+                                last.at[pair], out_hbm.at[slot], last_sems.at[pair]
+                            )
+                        )
+
+        bulk = pltpu.make_async_copy(out, out_hbm, sems.at[3])
         for load in phi_loads:
             load.wait()
         for b in range(batches):
             scaled[b] = (phi[b].astype(F32) * factors[b]).astype(BF16)
+        for b in range(batches):
+            if b == batches - 1:
+                bulk.start()
             for first in range(0, span, wide):
                 piece = lax.dot_general(
                     phi[b, pl.ds(first, span - first), :],
@@ -340,13 +361,19 @@
                         keep(b, i, j, tile)
                         if i * blk >= first + wide:
                             keep(b, j, i, tile.T)
+        bulk.wait()
+        last_tiles(lambda copy: copy.start())
+        last_tiles(lambda copy: copy.wait())
 
     return pl.pallas_call(
         body,
         out_shape=jax.ShapeDtypeStruct((slot_count, blk, blk), BF16),
         in_specs=[HBM, VMEM, HBM, HBM, HBM, HBM, HBM],
-        out_specs=VMEM,
+        out_specs=HBM,
         scratch_shapes=[
+            pltpu.VMEM((slot_count, blk, blk), BF16),
+            pltpu.VMEM((blocks * blocks, blk, blk), BF16),
+            pltpu.SemaphoreType.DMA((blocks * blocks,)),
             pltpu.VMEM(basis_t.shape, BF16),
             pltpu.VMEM((batches, rows, points), F32),
             pltpu.VMEM((batches, 1, points), F32),
@@ -358,7 +385,7 @@
             pltpu.SemaphoreType.DMA((batches,)),
             pltpu.SemaphoreType.DMA((batches,)),
             pltpu.SemaphoreType.DMA((batches,)),
-            pltpu.SemaphoreType.DMA((3,)),
+            pltpu.SemaphoreType.DMA((4,)),
         ],
         compiler_params=params(62),
         name="potential_pass",

time: 201 us -> 201 us (level)
  no operation moved by 1% of the time
where the time goes in v8:
time: 201 us
  waiting for transfers between devices  119 us (59%)
  Pallas kernels  24.5 us (12%)
  starting transfers between devices  23.7 us (12%)
  local copies, waits for them, and re-layouts  17.4 us (9%)
  blocking collectives  10.6 us (5%)
  between operations  4.85 us (2%)
    all_to_all x3, waiting for transfers between devices, exchange(): return lax.all_to_all(parts, AXES, split_axis=0, concat_axis=0, tiled=True)  92.7 us
    ppermute x5, waiting for transfers between devices, gathered(): other = lax.ppermute(values, AXES, [(d, d ^ reach) for d in range(devices)])  25.8 us
    all_to_all x3, starting transfers between devices, exchange(): return lax.all_to_all(parts, AXES, split_axis=0, concat_axis=0, tiled=True)  14.3 us
    unnamed x23, local copies, waits for them, and re-layouts  11.4 us
    all_to_all x1, blocking collectives, exchange(): return lax.all_to_all(parts, AXES, split_axis=0, concat_axis=0, tiled=True)  10.6 us
    pallas_call x1, Pallas kernels, potential_pass(): pl.pallas_call(body, out_shape=jax.ShapeDtypeStruct((slot_count, blk, blk...  9.4 us
    ppermute x5, starting transfers between devices, gathered(): other = lax.ppermute(values, AXES, [(d, d ^ reach) for d in range(devices)])  9.39 us
    pallas_call x1, Pallas kernels, density_pass(): pl.pallas_call(body, out_shape=(jax.ShapeDtypeStruct((SPARE * batches, 1,...  8.43 us
  transfers between devices with their start and end apart: 8, of which 6 were waited for; matrix products, arithmetic and copies ran while one was open for 9% of the time, Pallas kernels for 4%

profile of v8, /device:TPU:0, one launch (start us, length us, event | category | flops | bytes accessed | tf_op | source)
XLA Modules:
  0.0 200.6 jit_solution(17099159480715571829)
XLA Ops:
  0.6 3.0 %gather_tiles.1 = bf16[96,128,128]{2,1,0:T(8,128)(2,1)} custom-call(s32[3,1,32]{2,1,0:T(1,128)} %bitcast.17, bf16[32,128,128]{2,1,0:T(8,128)(2,1)} %tiles_ref.1), custom_call_target="tpu_custom_call" | custom-call | tf_op jit(solution)/shard_map/gather_tiles/pallas_call | solution.py:78
  3.7 7.3 %all-to-all-start = ((bf16[32,3,128,128]{3,2,1,0:T(8,128)(2,1)}), bf16[32,3,128,128]{3,2,1,0:T(8,128)(2,1)S(1)}, u32[]{:S(2)}, u32[]{:S(2)}) async-start(bf16[32,3,128,128]{3,2,1,0:T(8,128)(2,1)} %bitcast.22), calls=%async_computation | async-start | bytes 6291456 | tf_op jit(solution)/shard_map/all_to_all | solution.py:408
  11.0 0.3 collective-permute-start
  11.3 0.2 fusion
  11.5 0.6 fusion.1
  14.7 0.1 copy.32
  14.8 0.1 reshape.39
  14.8 8.8 %copy.33 = bf16[2,2048,768]{1,2,0:T(8,128)(2,1)} copy(bf16[2,2048,768]{2,1,0:T(8,128)(2,1)} %param.12) | data formatting | bytes 12582912 | tf_op args[2]
  23.6 2.5 %copy.34 = f32[2,49,2048]{2,1,0:T(8,128)} copy(f32[2,49,2048]{2,0,1:T(2,128)} %param.16) | data formatting | bytes 1605632 | tf_op args[6]
  27.6 0.9 constant_dynamic-slice_fusion.1
  28.6 1.7 collective-permute-start.1
  30.3 1.9 collective-permute-done.1
  32.3 1.6 collective-permute-start.2
  34.0 1.9 collective-permute-done.2
  36.0 1.7 collective-permute-start.3
  37.7 3.3 %pad.4.harm_hbm = f32[6,64,2048]{2,1,0:T(8,128)} pad(f32[2,49,2048]{2,1,0:T(8,128)} %copy.34, f32[]{:T(128)} %constant.11.clone.1), padding=0_4x0_15x0_0 | pad | bytes 3948548 | tf_op jit(solution)/shard_map/jit(_pad)/pad | solution.py:444
  41.0 22.0 %collective-permute-done.3 = s32[16]{0:T(128)S(1)} collective-permute-done((s32[16]{0:T(128)S(1)}, s32[16]{0:T(128)S(1)}, u32[]{:S(2)}, u32[]{:S(2)}) %collective-permute-start.3) | collective-permute-done | bytes 96 | tf_op jit(solution)/shard_map/ppermute | solution.py:399
  63.2 4.1 %collective-permute-start.4 = (s32[32]{0:T(128)S(1)}, s32[32]{0:T(128)S(1)}, u32[]{:S(2)}, u32[]{:S(2)}) collective-permute-start(s32[32]{0:T(128)S(1)} %pad_add_fusion.4), channel_id=1, source_target_pairs={{0,16},{1,17},{2,18},{3,19},{4,20},{5,21},{6,22},{7,23},{8,24},{9,... | collective-permute-start | bytes 392 | tf_op jit(solution)/shard_map/ppermute | solution.py:399
  67.3 15.1 %all-to-all-done = bf16[32,3,128,128]{3,2,1,0:T(8,128)(2,1)S(1)} async-done(((bf16[32,3,128,128]{3,2,1,0:T(8,128)(2,1)}), bf16[32,3,128,128]{3,2,1,0:T(8,128)(2,1)S(1)}, u32[]{:S(2)}, u32[]{:S(2)}) %all-to-all-start) | async-done | bytes 3145760 | tf_op jit(solution)/shard_map/all_to_all | solution.py:408
  82.3 8.4 %density_pass.1 = (f32[512,1,2048]{2,1,0:T(1,128)}, f32[32,4,128]{2,1,0:T(4,128)}) custom-call(s32[2,37]{1,0:T(2,128)S(1)} %pad_add_fusion.plan_hbm, bf16[96,128,128]{2,1,0:T(8,128)(2,1)S(1)} %bitcast.16, bf16[2,768,2048]{2,1,0:T(8,128)(2,1)} %bitcast.19, f32[6,64,2048]{2,1,0:T(8,128)} %pad.4.harm_hbm, f32[2,1,2048]{2,1,0:T(1,128)S(1)} %broadcast_in_dim.18.wts_hbm, ...), custom_call_target="tpu_custom_call" | custom-call | tf_op jit(solution)/shard_map/density_pass/pallas_call | solution.py:190
  90.8 4.0 %all-to-all-start.1 = ((f32[32,4,128]{2,1,0:T(4,128)}), f32[32,4,128]{2,1,0:T(4,128)S(1)}, u32[]{:S(2)}, u32[]{:S(2)}) async-start(f32[32,4,128]{2,1,0:T(4,128)} %get-tuple-element.7), calls=%async_computation.1 | async-start | bytes 131072 | tf_op jit(solution)/shard_map/all_to_all | solution.py:408
  94.9 0.1 concatenate.33
  95.0 0.1 copy.36
  95.2 0.1 copy.35
  95.4 6.9 %all-to-all-done.1.got = f32[32,4,128]{2,1,0:T(4,128)S(1)} async-done(((f32[32,4,128]{2,1,0:T(4,128)}), f32[32,4,128]{2,1,0:T(4,128)S(1)}, u32[]{:S(2)}, u32[]{:S(2)}) %all-to-all-start.1) | async-done | bytes 65568 | tf_op jit(solution)/shard_map/all_to_all | solution.py:408
  102.3 1.1 radial_solve.1
  103.4 10.6 %all_to_all.20.got = f32[32,8,128]{2,1,0:T(8,128)} all-to-all(f32[32,8,128]{2,1,0:T(8,128)S(1)} %radial_solve.1), channel_id=1, replica_groups=mesh['row'=4,'col'=8] {'row','col'}, dimensions={0} | all-to-all | bytes 262144 | tf_op jit(solution)/shard_map/all_to_all | solution.py:408
  114.0 9.4 %potential_pass.1 = bf16[96,128,128]{2,1,0:T(8,128)(2,1)} custom-call(s32[2,37]{1,0:T(2,128)} %copy-done.2, f32[32,8,128]{2,1,0:T(8,128)} %all_to_all.20.got, f32[512,1,2048]{2,1,0:T(1,128)} %get-tuple-element.9.rho_hbm, bf16[2,768,2048]{2,1,0:T(8,128)(2,1)} %bitcast.20, f32[6,64,2048]{2,1,0:T(8,128)} %pad.4.harm_hbm, f32[2,1,2048]{2,1,0:T(1,128)} %copy-done, ...), custom_call_target="tpu_custom_call" | custom-call | tf_op jit(solution)/shard_map/potential_pass/pallas_call | solution.py:368
  123.4 2.9 %all-to-all-start.3 = ((bf16[32,3,128,128]{3,2,1,0:T(8,128)(2,1)}), bf16[32,3,128,128]{3,2,1,0:T(8,128)(2,1)S(1)}, u32[]{:S(2)}, u32[]{:S(2)}) async-start(bf16[32,3,128,128]{3,2,1,0:T(8,128)(2,1)} %bitcast.21), calls=%async_computation.3 | async-start | bytes 6291456 | tf_op jit(solution)/shard_map/all_to_all | solution.py:408
  126.4 0.6 slice.17
  127.1 70.7 %all-to-all-done.3 = bf16[32,3,128,128]{3,2,1,0:T(8,128)(2,1)S(1)} async-done(((bf16[32,3,128,128]{3,2,1,0:T(8,128)(2,1)}), bf16[32,3,128,128]{3,2,1,0:T(8,128)(2,1)S(1)}, u32[]{:S(2)}, u32[]{:S(2)}) %all-to-all-start.3) | async-done | bytes 3145760 | tf_op jit(solution)/shard_map/all_to_all | solution.py:408
  197.8 2.6 %sum_tiles.1 = f32[32,128,128]{2,1,0:T(8,128)} custom-call(s32[3,1,32]{2,1,0:T(1,128)S(1)} %bitcast.18, bf16[96,128,128]{2,1,0:T(8,128)(2,1)S(1)} %bitcast.15), custom_call_target="tpu_custom_call" | custom-call | tf_op jit(solution)/shard_map/sum_tiles/pallas_call | solution.py:111
  (43 shorter events, 1.1 us)
Async XLA Ops:
  3.6 7.4 %copy-start.8 = (s32[2]{0:T(128)S(1)}, s32[2]{0:T(128)}, u32[]{:S(2)}) copy-start(s32[2]{0:T(128)} %param.18) | copy-start | bytes 28
  3.6 11.0 %copy-start.9 = (s32[2]{0:T(128)S(1)}, s32[2]{0:T(128)}, u32[]{:S(2)}) copy-start(s32[2]{0:T(128)} %param.13) | copy-start | bytes 28
  3.6 11.1 %copy-start.7 = (s32[2,6,6]{2,0,1:T(2,128)S(1)}, s32[2,6,6]{2,0,1:T(2,128)}, u32[]{:S(2)}) copy-start(s32[2,6,6]{2,0,1:T(2,128)} %param.14) | copy-start | bytes 868
  3.7 78.7 %all-to-all-start = ((bf16[32,3,128,128]{3,2,1,0:T(8,128)(2,1)}), bf16[32,3,128,128]{3,2,1,0:T(8,128)(2,1)S(1)}, u32[]{:S(2)}, u32[]{:S(2)}) async-start(bf16[32,3,128,128]{3,2,1,0:T(8,128)(2,1)} %bitcast.22), calls=%async_computation | async-start | bytes 6291456 | tf_op jit(solution)/shard_map/all_to_all | solution.py:408
  11.0 17.5 %collective-permute-start = (s32[2]{0:T(128)S(1)}, s32[2]{0:T(128)S(1)}, u32[]{:S(2)}, u32[]{:S(2)}) collective-permute-start(s32[2]{0:T(128)S(1)} %copy-done.8), channel_id=1, source_target_pairs={{0,1},{1,0},{2,3},{3,2},{4,5},{5,4},{6,7},{7,6},{8,9},{9,8},{10,11... | collective-permute-start | bytes 32 | tf_op jit(solution)/shard_map/ppermute | solution.py:399
  14.8 11.3 %copy-start.5 = (f32[2,2048]{1,0:T(2,128)S(1)}, f32[2,2048]{1,0:T(2,128)}, u32[]{:S(2)}) copy-start(f32[2,2048]{1,0:T(2,128)} %param.15) | copy-start | bytes 49156
  14.8 11.3 %copy-start.6 = (s32[2,2048]{1,0:T(2,128)S(1)}, s32[2,2048]{1,0:T(2,128)}, u32[]{:S(2)}) copy-start(s32[2,2048]{1,0:T(2,128)} %param.17) | copy-start | bytes 49156
  26.2 64.6 %copy-start = (f32[2,1,2048]{2,1,0:T(1,128)}, f32[2,1,2048]{2,1,0:T(1,128)S(1)}, u32[]{:S(2)}) copy-start(f32[2,1,2048]{2,1,0:T(1,128)S(1)} %broadcast_in_dim.18.wts_hbm) | copy-start | bytes 49156
  26.2 64.6 %copy-start.1 = (s32[2,1,2048]{2,1,0:T(1,128)}, s32[2,1,2048]{2,1,0:T(1,128)S(1)}, u32[]{:S(2)}) copy-start(s32[2,1,2048]{2,1,0:T(1,128)S(1)} %broadcast_in_dim.19.shell_hbm) | copy-start | bytes 49156
  27.6 63.2 %copy-start.2 = (s32[2,37]{1,0:T(2,128)}, s32[2,37]{1,0:T(2,128)S(1)}, u32[]{:S(2)}) copy-start(s32[2,37]{1,0:T(2,128)S(1)} %pad_add_fusion.plan_hbm) | copy-start | bytes 892
  28.6 3.6 %collective-permute-start.1 = (s32[4]{0:T(128)S(1)}, s32[4]{0:T(128)S(1)}, u32[]{:S(2)}, u32[]{:S(2)}) collective-permute-start(s32[4]{0:T(128)S(1)} %pad_add_fusion.1), channel_id=1, source_target_pairs={{0,2},{1,3},{2,0},{3,1},{4,6},{5,7},{6,4},{7,5},{8,10},{9,11},{10,... | collective-permute-start | bytes 56 | tf_op jit(solution)/shard_map/ppermute | solution.py:399
  32.3 3.6 %collective-permute-start.2 = (s32[8]{0:T(128)S(1)}, s32[8]{0:T(128)S(1)}, u32[]{:S(2)}, u32[]{:S(2)}) collective-permute-start(s32[8]{0:T(128)S(1)} %pad_add_fusion.2), channel_id=1, source_target_pairs={{0,4},{1,5},{2,6},{3,7},{4,0},{5,1},{6,2},{7,3},{8,12},{9,13},{10,... | collective-permute-start | bytes 104 | tf_op jit(solution)/shard_map/ppermute | solution.py:399
  36.0 27.0 %collective-permute-start.3 = (s32[16]{0:T(128)S(1)}, s32[16]{0:T(128)S(1)}, u32[]{:S(2)}, u32[]{:S(2)}) collective-permute-start(s32[16]{0:T(128)S(1)} %pad_add_fusion.3), channel_id=1, source_target_pairs={{0,8},{1,9},{2,10},{3,11},{4,12},{5,13},{6,14},{7,15},{8,0},{9,1},... | collective-permute-start | bytes 200 | tf_op jit(solution)/shard_map/ppermute | solution.py:399
  63.2 31.7 %collective-permute-start.4 = (s32[32]{0:T(128)S(1)}, s32[32]{0:T(128)S(1)}, u32[]{:S(2)}, u32[]{:S(2)}) collective-permute-start(s32[32]{0:T(128)S(1)} %pad_add_fusion.4), channel_id=1, source_target_pairs={{0,16},{1,17},{2,18},{3,19},{4,20},{5,21},{6,22},{7,23},{8,24},{9,... | collective-permute-start | bytes 392 | tf_op jit(solution)/shard_map/ppermute | solution.py:399
  90.8 11.4 %all-to-all-start.1 = ((f32[32,4,128]{2,1,0:T(4,128)}), f32[32,4,128]{2,1,0:T(4,128)S(1)}, u32[]{:S(2)}, u32[]{:S(2)}) async-start(f32[32,4,128]{2,1,0:T(4,128)} %get-tuple-element.7), calls=%async_computation.1 | async-start | bytes 131072 | tf_op jit(solution)/shard_map/all_to_all | solution.py:408
  123.4 3.0 %copy-start.4 = (f32[32,8,128]{2,1,0:T(8,128)S(1)}, f32[32,8,128]{2,1,0:T(8,128)}, u32[]{:S(2)}) copy-start(f32[32,8,128]{2,1,0:T(8,128)} %all_to_all.20.got) | copy-start | bytes 393220
  123.4 74.4 %copy-start.3 = (s32[1,32,3]{1,0,2:T(1,128)S(1)}, s32[1,32,3]{1,0,2:T(1,128)}, u32[]{:S(2)}) copy-start(s32[1,32,3]{1,0,2:T(1,128)} %param.11) | copy-start | bytes 1156
  123.4 74.4 %all-to-all-start.3 = ((bf16[32,3,128,128]{3,2,1,0:T(8,128)(2,1)}), bf16[32,3,128,128]{3,2,1,0:T(8,128)(2,1)S(1)}, u32[]{:S(2)}, u32[]{:S(2)}) async-start(bf16[32,3,128,128]{3,2,1,0:T(8,128)(2,1)} %bitcast.21), calls=%async_computation.3 | async-start | bytes 6291456 | tf_op jit(solution)/shard_map/all_to_all | solution.py:408

commit v9 on v8

--- a/solution.py
+++ b/solution.py
@@ -340,11 +340,9 @@
                         )
 
         bulk = pltpu.make_async_copy(out, out_hbm, sems.at[3])
-        for load in phi_loads:
-            load.wait()
-        for b in range(batches):
+        for b in range(batches):
+            phi_loads[b].wait()
             scaled[b] = (phi[b].astype(F32) * factors[b]).astype(BF16)
-        for b in range(batches):
             if b == batches - 1:
                 bulk.start()
             for first in range(0, span, wide):

time: 201 us -> 201 us (level)
  no operation moved by 1% of the time
where the time goes in v9:
time: 201 us; the launch traced here: 200 us
  waiting for transfers between devices  119 us (59%)
  Pallas kernels  23.7 us (12%)
  starting transfers between devices  23.7 us (12%)
  local copies, waits for them, and re-layouts  17.4 us (9%)
  blocking collectives  10.6 us (5%)
  between operations  4.85 us (2%)
    all_to_all x3, waiting for transfers between devices, exchange(): return lax.all_to_all(parts, AXES, split_axis=0, concat_axis=0, tiled=True)  92.7 us
    ppermute x5, waiting for transfers between devices, gathered(): other = lax.ppermute(values, AXES, [(d, d ^ reach) for d in range(devices)])  25.8 us
    all_to_all x3, starting transfers between devices, exchange(): return lax.all_to_all(parts, AXES, split_axis=0, concat_axis=0, tiled=True)  14.3 us
    unnamed x23, local copies, waits for them, and re-layouts  11.4 us
    all_to_all x1, blocking collectives, exchange(): return lax.all_to_all(parts, AXES, split_axis=0, concat_axis=0, tiled=True)  10.6 us
    ppermute x5, starting transfers between devices, gathered(): other = lax.ppermute(values, AXES, [(d, d ^ reach) for d in range(devices)])  9.39 us
    pallas_call x1, Pallas kernels, potential_pass(): pl.pallas_call(body, out_shape=jax.ShapeDtypeStruct((slot_count, blk, blk...  8.6 us
    pallas_call x1, Pallas kernels, density_pass(): pl.pallas_call(body, out_shape=(jax.ShapeDtypeStruct((SPARE * batches, 1,...  8.43 us
  transfers between devices with their start and end apart: 8, of which 6 were waited for; matrix products, arithmetic and copies ran while one was open for 9% of the time, Pallas kernels for 4%

profile of v9, /device:TPU:0, one launch (start us, length us, event | category | flops | bytes accessed | tf_op | source)
XLA Modules:
  0.0 199.8 jit_solution(15045105990278321139)
XLA Ops:
  0.6 3.0 %gather_tiles.1 = bf16[96,128,128]{2,1,0:T(8,128)(2,1)} custom-call(s32[3,1,32]{2,1,0:T(1,128)} %bitcast.17, bf16[32,128,128]{2,1,0:T(8,128)(2,1)} %tiles_ref.1), custom_call_target="tpu_custom_call" | custom-call | tf_op jit(solution)/shard_map/gather_tiles/pallas_call | solution.py:78
  3.7 7.3 %all-to-all-start = ((bf16[32,3,128,128]{3,2,1,0:T(8,128)(2,1)}), bf16[32,3,128,128]{3,2,1,0:T(8,128)(2,1)S(1)}, u32[]{:S(2)}, u32[]{:S(2)}) async-start(bf16[32,3,128,128]{3,2,1,0:T(8,128)(2,1)} %bitcast.22), calls=%async_computation | async-start | bytes 6291456 | tf_op jit(solution)/shard_map/all_to_all | solution.py:406
  11.0 0.3 collective-permute-start
  11.3 0.2 fusion
  11.5 0.6 fusion.1
  14.7 0.1 copy.32
  14.8 0.1 reshape.39
  14.8 8.8 %copy.33 = bf16[2,2048,768]{1,2,0:T(8,128)(2,1)} copy(bf16[2,2048,768]{2,1,0:T(8,128)(2,1)} %param.12) | data formatting | bytes 12582912 | tf_op args[2]
  23.6 2.5 %copy.34 = f32[2,49,2048]{2,1,0:T(8,128)} copy(f32[2,49,2048]{2,0,1:T(2,128)} %param.16) | data formatting | bytes 1605632 | tf_op args[6]
  27.6 0.9 constant_dynamic-slice_fusion.1
  28.6 1.7 collective-permute-start.1
  30.3 1.9 collective-permute-done.1
  32.3 1.6 collective-permute-start.2
  34.0 1.9 collective-permute-done.2
  36.0 1.7 collective-permute-start.3
  37.7 3.3 %pad.4.harm_hbm = f32[6,64,2048]{2,1,0:T(8,128)} pad(f32[2,49,2048]{2,1,0:T(8,128)} %copy.34, f32[]{:T(128)} %constant.11.clone.1), padding=0_4x0_15x0_0 | pad | bytes 3948548 | tf_op jit(solution)/shard_map/jit(_pad)/pad | solution.py:442
  41.0 22.0 %collective-permute-done.3 = s32[16]{0:T(128)S(1)} collective-permute-done((s32[16]{0:T(128)S(1)}, s32[16]{0:T(128)S(1)}, u32[]{:S(2)}, u32[]{:S(2)}) %collective-permute-start.3) | collective-permute-done | bytes 96 | tf_op jit(solution)/shard_map/ppermute | solution.py:397
  63.2 4.1 %collective-permute-start.4 = (s32[32]{0:T(128)S(1)}, s32[32]{0:T(128)S(1)}, u32[]{:S(2)}, u32[]{:S(2)}) collective-permute-start(s32[32]{0:T(128)S(1)} %pad_add_fusion.4), channel_id=1, source_target_pairs={{0,16},{1,17},{2,18},{3,19},{4,20},{5,21},{6,22},{7,23},{8,24},{9,... | collective-permute-start | bytes 392 | tf_op jit(solution)/shard_map/ppermute | solution.py:397
  67.3 15.1 %all-to-all-done = bf16[32,3,128,128]{3,2,1,0:T(8,128)(2,1)S(1)} async-done(((bf16[32,3,128,128]{3,2,1,0:T(8,128)(2,1)}), bf16[32,3,128,128]{3,2,1,0:T(8,128)(2,1)S(1)}, u32[]{:S(2)}, u32[]{:S(2)}) %all-to-all-start) | async-done | bytes 3145760 | tf_op jit(solution)/shard_map/all_to_all | solution.py:406
  82.3 8.4 %density_pass.1 = (f32[512,1,2048]{2,1,0:T(1,128)}, f32[32,4,128]{2,1,0:T(4,128)}) custom-call(s32[2,37]{1,0:T(2,128)S(1)} %pad_add_fusion.plan_hbm, bf16[96,128,128]{2,1,0:T(8,128)(2,1)S(1)} %bitcast.16, bf16[2,768,2048]{2,1,0:T(8,128)(2,1)} %bitcast.19, f32[6,64,2048]{2,1,0:T(8,128)} %pad.4.harm_hbm, f32[2,1,2048]{2,1,0:T(1,128)S(1)} %broadcast_in_dim.18.wts_hbm, ...), custom_call_target="tpu_custom_call" | custom-call | tf_op jit(solution)/shard_map/density_pass/pallas_call | solution.py:190
  90.8 4.0 %all-to-all-start.1 = ((f32[32,4,128]{2,1,0:T(4,128)}), f32[32,4,128]{2,1,0:T(4,128)S(1)}, u32[]{:S(2)}, u32[]{:S(2)}) async-start(f32[32,4,128]{2,1,0:T(4,128)} %get-tuple-element.7), calls=%async_computation.1 | async-start | bytes 131072 | tf_op jit(solution)/shard_map/all_to_all | solution.py:406
  94.9 0.1 concatenate.33
  95.0 0.1 copy.36
  95.2 0.1 copy.35
  95.4 6.9 %all-to-all-done.1.got = f32[32,4,128]{2,1,0:T(4,128)S(1)} async-done(((f32[32,4,128]{2,1,0:T(4,128)}), f32[32,4,128]{2,1,0:T(4,128)S(1)}, u32[]{:S(2)}, u32[]{:S(2)}) %all-to-all-start.1) | async-done | bytes 65568 | tf_op jit(solution)/shard_map/all_to_all | solution.py:406
  102.3 1.1 radial_solve.1
  103.4 10.6 %all_to_all.20.got = f32[32,8,128]{2,1,0:T(8,128)} all-to-all(f32[32,8,128]{2,1,0:T(8,128)S(1)} %radial_solve.1), channel_id=1, replica_groups=mesh['row'=4,'col'=8] {'row','col'}, dimensions={0} | all-to-all | bytes 262144 | tf_op jit(solution)/shard_map/all_to_all | solution.py:406
  114.0 8.6 %potential_pass.1 = bf16[96,128,128]{2,1,0:T(8,128)(2,1)} custom-call(s32[2,37]{1,0:T(2,128)} %copy-done.2, f32[32,8,128]{2,1,0:T(8,128)} %all_to_all.20.got, f32[512,1,2048]{2,1,0:T(1,128)} %get-tuple-element.9.rho_hbm, bf16[2,768,2048]{2,1,0:T(8,128)(2,1)} %bitcast.20, f32[6,64,2048]{2,1,0:T(8,128)} %pad.4.harm_hbm, f32[2,1,2048]{2,1,0:T(1,128)} %copy-done, ...), custom_call_target="tpu_custom_call" | custom-call | tf_op jit(solution)/shard_map/potential_pass/pallas_call | solution.py:366
  122.6 2.9 %all-to-all-start.3 = ((bf16[32,3,128,128]{3,2,1,0:T(8,128)(2,1)}), bf16[32,3,128,128]{3,2,1,0:T(8,128)(2,1)S(1)}, u32[]{:S(2)}, u32[]{:S(2)}) async-start(bf16[32,3,128,128]{3,2,1,0:T(8,128)(2,1)} %bitcast.21), calls=%async_computation.3 | async-start | bytes 6291456 | tf_op jit(solution)/shard_map/all_to_all | solution.py:406
  125.6 0.6 slice.17
  126.3 70.7 %all-to-all-done.3 = bf16[32,3,128,128]{3,2,1,0:T(8,128)(2,1)S(1)} async-done(((bf16[32,3,128,128]{3,2,1,0:T(8,128)(2,1)}), bf16[32,3,128,128]{3,2,1,0:T(8,128)(2,1)S(1)}, u32[]{:S(2)}, u32[]{:S(2)}) %all-to-all-start.3) | async-done | bytes 3145760 | tf_op jit(solution)/shard_map/all_to_all | solution.py:406
  197.0 2.6 %sum_tiles.1 = f32[32,128,128]{2,1,0:T(8,128)} custom-call(s32[3,1,32]{2,1,0:T(1,128)S(1)} %bitcast.18, bf16[96,128,128]{2,1,0:T(8,128)(2,1)S(1)} %bitcast.15), custom_call_target="tpu_custom_call" | custom-call | tf_op jit(solution)/shard_map/sum_tiles/pallas_call | solution.py:111
  (43 shorter events, 1.1 us)
Async XLA Ops:
  3.6 7.4 %copy-start.8 = (s32[2]{0:T(128)S(1)}, s32[2]{0:T(128)}, u32[]{:S(2)}) copy-start(s32[2]{0:T(128)} %param.18) | copy-start | bytes 28
  3.6 11.0 %copy-start.9 = (s32[2]{0:T(128)S(1)}, s32[2]{0:T(128)}, u32[]{:S(2)}) copy-start(s32[2]{0:T(128)} %param.13) | copy-start | bytes 28
  3.6 11.1 %copy-start.7 = (s32[2,6,6]{2,0,1:T(2,128)S(1)}, s32[2,6,6]{2,0,1:T(2,128)}, u32[]{:S(2)}) copy-start(s32[2,6,6]{2,0,1:T(2,128)} %param.14) | copy-start | bytes 868
  3.7 78.7 %all-to-all-start = ((bf16[32,3,128,128]{3,2,1,0:T(8,128)(2,1)}), bf16[32,3,128,128]{3,2,1,0:T(8,128)(2,1)S(1)}, u32[]{:S(2)}, u32[]{:S(2)}) async-start(bf16[32,3,128,128]{3,2,1,0:T(8,128)(2,1)} %bitcast.22), calls=%async_computation | async-start | bytes 6291456 | tf_op jit(solution)/shard_map/all_to_all | solution.py:406
  11.0 17.5 %collective-permute-start = (s32[2]{0:T(128)S(1)}, s32[2]{0:T(128)S(1)}, u32[]{:S(2)}, u32[]{:S(2)}) collective-permute-start(s32[2]{0:T(128)S(1)} %copy-done.8), channel_id=1, source_target_pairs={{0,1},{1,0},{2,3},{3,2},{4,5},{5,4},{6,7},{7,6},{8,9},{9,8},{10,11... | collective-permute-start | bytes 32 | tf_op jit(solution)/shard_map/ppermute | solution.py:397
  14.8 11.3 %copy-start.5 = (f32[2,2048]{1,0:T(2,128)S(1)}, f32[2,2048]{1,0:T(2,128)}, u32[]{:S(2)}) copy-start(f32[2,2048]{1,0:T(2,128)} %param.15) | copy-start | bytes 49156
  14.8 11.3 %copy-start.6 = (s32[2,2048]{1,0:T(2,128)S(1)}, s32[2,2048]{1,0:T(2,128)}, u32[]{:S(2)}) copy-start(s32[2,2048]{1,0:T(2,128)} %param.17) | copy-start | bytes 49156
  26.2 64.6 %copy-start = (f32[2,1,2048]{2,1,0:T(1,128)}, f32[2,1,2048]{2,1,0:T(1,128)S(1)}, u32[]{:S(2)}) copy-start(f32[2,1,2048]{2,1,0:T(1,128)S(1)} %broadcast_in_dim.18.wts_hbm) | copy-start | bytes 49156
  26.2 64.6 %copy-start.1 = (s32[2,1,2048]{2,1,0:T(1,128)}, s32[2,1,2048]{2,1,0:T(1,128)S(1)}, u32[]{:S(2)}) copy-start(s32[2,1,2048]{2,1,0:T(1,128)S(1)} %broadcast_in_dim.19.shell_hbm) | copy-start | bytes 49156
  27.6 63.2 %copy-start.2 = (s32[2,37]{1,0:T(2,128)}, s32[2,37]{1,0:T(2,128)S(1)}, u32[]{:S(2)}) copy-start(s32[2,37]{1,0:T(2,128)S(1)} %pad_add_fusion.plan_hbm) | copy-start | bytes 892
  28.6 3.6 %collective-permute-start.1 = (s32[4]{0:T(128)S(1)}, s32[4]{0:T(128)S(1)}, u32[]{:S(2)}, u32[]{:S(2)}) collective-permute-start(s32[4]{0:T(128)S(1)} %pad_add_fusion.1), channel_id=1, source_target_pairs={{0,2},{1,3},{2,0},{3,1},{4,6},{5,7},{6,4},{7,5},{8,10},{9,11},{10,... | collective-permute-start | bytes 56 | tf_op jit(solution)/shard_map/ppermute | solution.py:397
  32.3 3.6 %collective-permute-start.2 = (s32[8]{0:T(128)S(1)}, s32[8]{0:T(128)S(1)}, u32[]{:S(2)}, u32[]{:S(2)}) collective-permute-start(s32[8]{0:T(128)S(1)} %pad_add_fusion.2), channel_id=1, source_target_pairs={{0,4},{1,5},{2,6},{3,7},{4,0},{5,1},{6,2},{7,3},{8,12},{9,13},{10,... | collective-permute-start | bytes 104 | tf_op jit(solution)/shard_map/ppermute | solution.py:397
  36.0 27.0 %collective-permute-start.3 = (s32[16]{0:T(128)S(1)}, s32[16]{0:T(128)S(1)}, u32[]{:S(2)}, u32[]{:S(2)}) collective-permute-start(s32[16]{0:T(128)S(1)} %pad_add_fusion.3), channel_id=1, source_target_pairs={{0,8},{1,9},{2,10},{3,11},{4,12},{5,13},{6,14},{7,15},{8,0},{9,1},... | collective-permute-start | bytes 200 | tf_op jit(solution)/shard_map/ppermute | solution.py:397
  63.2 31.7 %collective-permute-start.4 = (s32[32]{0:T(128)S(1)}, s32[32]{0:T(128)S(1)}, u32[]{:S(2)}, u32[]{:S(2)}) collective-permute-start(s32[32]{0:T(128)S(1)} %pad_add_fusion.4), channel_id=1, source_target_pairs={{0,16},{1,17},{2,18},{3,19},{4,20},{5,21},{6,22},{7,23},{8,24},{9,... | collective-permute-start | bytes 392 | tf_op jit(solution)/shard_map/ppermute | solution.py:397
  90.8 11.4 %all-to-all-start.1 = ((f32[32,4,128]{2,1,0:T(4,128)}), f32[32,4,128]{2,1,0:T(4,128)S(1)}, u32[]{:S(2)}, u32[]{:S(2)}) async-start(f32[32,4,128]{2,1,0:T(4,128)} %get-tuple-element.7), calls=%async_computation.1 | async-start | bytes 131072 | tf_op jit(solution)/shard_map/all_to_all | solution.py:406
  122.6 3.0 %copy-start.4 = (f32[32,8,128]{2,1,0:T(8,128)S(1)}, f32[32,8,128]{2,1,0:T(8,128)}, u32[]{:S(2)}) copy-start(f32[32,8,128]{2,1,0:T(8,128)} %all_to_all.20.got) | copy-start | bytes 393220
  122.6 74.4 %copy-start.3 = (s32[1,32,3]{1,0,2:T(1,128)S(1)}, s32[1,32,3]{1,0,2:T(1,128)}, u32[]{:S(2)}) copy-start(s32[1,32,3]{1,0,2:T(1,128)} %param.11) | copy-start | bytes 1156
  122.6 74.4 %all-to-all-start.3 = ((bf16[32,3,128,128]{3,2,1,0:T(8,128)(2,1)}), bf16[32,3,128,128]{3,2,1,0:T(8,128)(2,1)S(1)}, u32[]{:S(2)}, u32[]{:S(2)}) async-start(bf16[32,3,128,128]{3,2,1,0:T(8,128)(2,1)} %bitcast.21), calls=%async_computation.3 | async-start | bytes 6291456 | tf_op jit(solution)/shard_map/all_to_all | solution.py:406
